TPU v7x, 128 devices: a whole 4x4x4 slice. The times are simulated.
128 devices in a mesh: dp: 32 (over y, x, core), head: 4 (over z).
Axes of the slice: x: 4, y: 4, z: 4, core: 2. Of those that a mesh axis runs over, the one named last changes fastest.
Arguments:
- feats: bfloat16 [4, 65536, 384], P('head', 'dp'), may hold values from -6 to 6
- valid: int32 [256], P('dp'), may hold values from 1 to 256
- owner_map: int32 [256], P('dp'), may hold values from 0 to 31, as said below
- w_conv: bfloat16 [4, 3, 384, 384], P('head', None, 'dp'), may hold values from -0.11785113 to 0.11785113
- w_mid: bfloat16 [4, 384, 384], P('head', 'dp'), may hold values from -0.20412415 to 0.20412415
- w_out: bfloat16 [4, 384], P('head', 'dp'), may hold values from -0.20412415 to 0.20412415
Outputs:
- grad_feats: bfloat16 [4, 131072, 384], P('head', 'dp')
- grad_conv: float32 [4, 3, 384, 384], P('head', None, 'dp')
- grad_mid: float32 [4, 384, 384], P('head', 'dp')
- grad_out: float32 [4, 384], P('head', 'dp')
Inputs may be any that keep to these rules, and one draw needn't show every extreme that they name: `owner_map`: image o is held by index o of dp. Every image owns 1 to 16 blocks; a quarter of the images own exactly 16. The 8 blocks of one index of dp belong to 8 different images.
All inputs are finite; a program needn't handle non-finite values.
Results may differ from a plain program's by a relative error of at most 0.019.
Values may be sent and summed in bfloat16 or wider, within the bound.
No kernel may reach another device: no remote copies, remote signals or barrier semaphores. Data moves between devices by JAX's collectives and lax.ppermute only.
A program may use at most 128 MiB of HBM per device.

v0:
```python
import functools

import jax
import jax.numpy as jnp
from jax import lax
from jax.sharding import Mesh
from jax.sharding import PartitionSpec as P

D = 384
TAPS = 4
BT = 256
DP = ("dp_0", "dp_1", "dp_2")
DP_HEAD = ("dp_0", "dp_1", "dp_2", "head")


def gather_turned(arrays, axis, dims):
    turned = [jnp.moveaxis(a, dim, 0) for a, dim in zip(arrays, dims)]
    widths = [t[0].size for t in turned]
    both = jnp.concatenate([t.reshape(-1, w) for t, w in zip(turned, widths)], axis=1)
    out = lax.all_gather(both, axis, axis=0, tiled=True)
    tiles = jnp.split(out, [sum(widths[:k]) for k in range(1, len(widths))], axis=1)
    return tuple(
        (
            jnp.moveaxis(b.reshape(-1, *t.shape[1:]), 0, dim)
            for b, t, dim in zip(tiles, turned, dims)
        )
    )


def copy_for_each(shard, axis):
    copies = jnp.broadcast_to(shard, (lax.axis_size(axis), *shard.shape))
    return lax.all_to_all(copies, axis, split_axis=0, concat_axis=0, tiled=True)


def combined_pairwise(pieces, combine):
    while len(jax.tree.leaves(pieces)[0]) > 1:
        pieces = jax.vmap(combine)(*(pieces[side::2] for side in (0, 1)))
    return pieces[0]


def entering(shard, axis, combine, identity):
    count, index = (lax.axis_size(axis), lax.axis_index(axis))
    passed = jnp.arange(count) < index

    def kept(part, zero, own):
        part = jnp.where(
            passed.reshape(-1, *(1 for _ in own.shape)), part, jnp.asarray(zero, own.dtype)
        )
        return part

    pieces = copy_for_each(shard, axis)
    return combined_pairwise(kept(pieces, identity, shard), combine)


def over_copies(shard, axis):
    return copy_for_each(shard, axis).sum(axis=0)


def by_axis(shard, axes):
    return functools.reduce(lax.psum, axes, shard)


def side_by_side(arrays, axis, split_dim, concat_dim, along):
    columns = [a.reshape(*a.shape[:along], -1) for a in arrays]
    both = jnp.concatenate(columns, axis=along)
    out, at, outs = (
        lax.all_to_all(both, axis, split_axis=split_dim, concat_axis=concat_dim, tiled=True),
        0,
        [],
    )
    for a, column in zip(arrays, columns):
        slab = out[..., at : at + column.shape[along]]
        outs.append(slab.reshape(*slab.shape[:along], *a.shape[along:]))
        at += column.shape[along]
    return tuple(outs)


def in_blocks(shard, dim, count):
    lengths = shard.shape
    tiles = shard.reshape(*lengths[:dim], count, lengths[dim] // count, *lengths[dim + 1 :])
    return jnp.moveaxis(tiles, dim, 0)


def sum_packed(arrays, axis, dims):
    count = lax.axis_size(axis)
    tiles = [in_blocks(a, dim, count) for a, dim in zip(arrays, dims)]
    lines = jnp.concatenate([b.reshape(count, -1) for b in tiles], axis=1)
    rows = max(16, -(-lines.shape[1] // 1024) * 8)
    lines = jnp.pad(lines, ((0, 0), (0, rows * 128 - lines.shape[1]))).reshape(-1, 128)
    ravelled, at, outs = (lax.psum_scatter(lines, axis, tiled=True).reshape(-1), 0, [])
    for b in tiles:
        part = b[0]
        outs.append(ravelled[at : at + part.size].reshape(part.shape))
        at += part.size
    return tuple(outs)


def activate(value):
    return 0.2 * value + 0.8 * jax.nn.softplus(value)


def derivative(value):
    return 0.2 + 0.8 * jax.nn.sigmoid(value)


def flatten(array):
    return array.reshape(-1, array.shape[-1])


def add_counts(earlier, later):
    return earlier + later


def forward_pass(blocks, mask, conv_w, mid_w, out_w):
    count = blocks.shape[0]
    width = blocks.shape[2]
    masked = (blocks * mask[:, :, None]).astype(jnp.bfloat16)
    zero_row = jnp.zeros((count, 1, width), jnp.bfloat16)
    previous = jnp.concatenate([zero_row, masked[:, :-1]], 1)
    following = jnp.concatenate([masked[:, 1:], zero_row], 1)
    first_pre = jnp.dot(flatten(previous), conv_w[0], preferred_element_type=jnp.float32)
    first_pre = first_pre + jnp.dot(flatten(masked), conv_w[1], preferred_element_type=jnp.float32)
    first_pre = first_pre + jnp.dot(
        flatten(following), conv_w[2], preferred_element_type=jnp.float32
    )
    first_act = activate(first_pre)
    first_low = first_act.astype(jnp.bfloat16)
    second_pre = jnp.dot(first_low, mid_w, preferred_element_type=jnp.float32)
    second_act = activate(second_pre) + first_act
    logits = jnp.dot(second_act, out_w.astype(jnp.float32), precision=lax.Precision.HIGHEST)
    return ((previous, masked, following, first_pre, first_low, second_pre, second_act), logits)


def backward_pass(saved, upstream, mask, conv_w, mid_w, out_w):
    previous, masked, following, first_pre, first_low, second_pre, second_act = saved
    count, length, width = masked.shape
    grad_second = upstream[:, None] * out_w.astype(jnp.float32)[None, :]
    grad_mid_pre = (grad_second * derivative(second_pre)).astype(jnp.bfloat16)
    grad_first = jnp.dot(grad_mid_pre, mid_w.T, preferred_element_type=jnp.float32) + grad_second
    grad_first_pre = (grad_first * derivative(first_pre)).astype(jnp.bfloat16)

    def through(index):
        return jnp.dot(grad_first_pre, conv_w[index].T, preferred_element_type=jnp.float32).reshape(
            count, length, width
        )

    zero_row = jnp.zeros((count, 1, width), jnp.float32)
    from_next = through(0)
    from_prev = through(2)
    total = (
        through(1)
        + jnp.concatenate([from_next[:, 1:], zero_row], 1)
        + jnp.concatenate([zero_row, from_prev[:, :-1]], 1)
    )
    grad_input = (total * mask[:, :, None]).astype(jnp.bfloat16)
    grad_conv = jnp.stack(
        [
            jnp.dot(flatten(previous).T, grad_first_pre, preferred_element_type=jnp.float32),
            jnp.dot(flatten(masked).T, grad_first_pre, preferred_element_type=jnp.float32),
            jnp.dot(flatten(following).T, grad_first_pre, preferred_element_type=jnp.float32),
        ]
    )
    grad_mid = jnp.dot(first_low.T, grad_mid_pre, preferred_element_type=jnp.float32)
    grad_out = jnp.dot(upstream, second_act, precision=lax.Precision.HIGHEST)
    return (grad_input, grad_conv, grad_mid, grad_out)


def pack_blocks(picks, blocks):
    packed = jnp.dot(
        picks.astype(jnp.bfloat16),
        flatten(blocks.reshape(blocks.shape[0], -1)),
        preferred_element_type=jnp.float32,
    )
    return packed.astype(jnp.bfloat16).reshape(-1, 1, blocks.shape[1], blocks.shape[2])


def place_blocks(received, codes, capacity):
    entries = codes[..., 0].astype(jnp.float32).reshape(-1)
    table = (entries[None, :] - 1.0 == jnp.arange(capacity, dtype=jnp.float32)[:, None]).astype(
        jnp.float32
    )
    rows_flat = received.reshape(entries.shape[0], -1)
    placed = jnp.dot(
        table.astype(jnp.bfloat16), rows_flat, preferred_element_type=jnp.float32
    ).astype(jnp.bfloat16)
    return (placed.reshape(capacity, received.shape[2], received.shape[3]), table)


def per_device(feats, valid, owner_map, w_conv, w_mid, w_out):
    conv_all, mid_all, out_all = gather_turned((w_conv, w_mid, w_out), DP, (2, 1, 1))
    conv_w = conv_all[0]
    mid_w = mid_all[0]
    out_w = out_all[0]
    devices = lax.axis_size(DP)
    capacity = devices // 2
    local = owner_map.shape[0]
    owners = jnp.arange(devices, dtype=jnp.int32)
    member_int = (owner_map[:, None] == owners[None, :]).astype(jnp.int32)
    earlier = jnp.cumsum(member_int, 0) - member_int
    within = jnp.sum(earlier * member_int, 1)
    lower = entering(jnp.sum(member_int, 0), DP, add_counts, jnp.zeros((devices,), jnp.int32))
    slots = jnp.sum(member_int * lower[None, :], 1) + within
    tokens = over_copies(jnp.sum(member_int * valid[:, None], 0).astype(jnp.float32), DP)
    scale_norm = jnp.sqrt(TAPS * tokens)
    picks = (owner_map[None, :] == owners[:, None]).astype(jnp.float32)
    labels = jnp.stack([slots + 1, valid], 1).astype(jnp.float32)
    meta = (
        jnp.dot(picks, labels, precision=lax.Precision.HIGHEST)
        .astype(jnp.bfloat16)
        .reshape(devices, 1, 2)
    )
    blocks_here = feats[0].reshape(local, BT, D)
    slot_valid = valid.astype(jnp.float32)
    members = member_int.astype(jnp.float32)
    count = blocks_here.shape[0]
    mask = (jnp.arange(BT, dtype=jnp.float32)[None, :] < slot_valid[:, None]).astype(jnp.float32)
    saved, logits = forward_pass(blocks_here, mask, conv_w, mid_w, out_w)
    block_sums = jnp.sum(logits.reshape(count, BT) * mask, 1)
    totals = by_axis(jnp.dot(block_sums, members, precision=lax.Precision.HIGHEST), DP_HEAD)
    strength = totals / scale_norm
    factor = -BT * jax.nn.sigmoid(-strength) / scale_norm
    upstream = (jnp.dot(members, factor, precision=lax.Precision.HIGHEST)[:, None] * mask).reshape(
        -1
    )
    grad_input, grad_conv, grad_mid, grad_out = backward_pass(
        saved, upstream, mask, conv_w, mid_w, out_w
    )
    outgoing_grads = pack_blocks(picks, grad_input)
    back, back_meta = side_by_side((outgoing_grads, meta), DP, 0, 0, 2)
    placed, ignored = place_blocks(back, back_meta, capacity)
    returned = placed.reshape(1, capacity * BT, D)
    conv_part, mid_part, out_part = tuple(
        (
            part.astype(jnp.float32)
            for part in sum_packed(
                (
                    grad_conv.astype(jnp.bfloat16),
                    grad_mid.astype(jnp.bfloat16),
                    grad_out.astype(jnp.bfloat16),
                ),
                DP,
                (1, 0, 0),
            )
        )
    )
    total_blocks = devices * local
    return (
        returned,
        (conv_part / total_blocks)[None],
        (mid_part / total_blocks)[None],
        (out_part / total_blocks)[None],
    )


def solution(mesh):
    split = Mesh(
        mesh.devices.reshape(4, 4, 2, mesh.shape["head"]), ("dp_0", "dp_1", "dp_2", "head")
    )
    in_specs = (
        P("head", DP, None),
        P(DP),
        P(DP),
        P("head", None, DP, None),
        P("head", DP, None),
        P("head", DP),
    )
    out_specs = (P("head", DP, None), P("head", None, DP, None), P("head", DP, None), P("head", DP))
    return jax.shard_map(
        per_device, mesh=split, in_specs=in_specs, out_specs=out_specs, check_vma=False
    )
```

profile of v0, /device:TPU:1, one launch (start us, length us, event | category | flops | bytes accessed | tf_op | source)
XLA Modules:
  0.0 367.6 jit_solution(13652263459947661605)
XLA Ops:
  8.8 1.3 maximum_bitcast_fusion.1
  12.4 8.6 %all-to-all-start.1 = ((s32[32,1,32]{2,1,0:T(1,128)}), s32[32,1,32]{2,1,0:T(1,128)S(1)}, u32[]{:S(2)}, u32[]{:S(2)}) async-start(s32[32,1,32]{2,1,0:T(1,128)} %broadcast_in_dim.22), calls=%async_computation.1 | async-start | bytes 32768 | tf_op jit(solution)/shard_map/all_to_all | solution.py:32
  21.7 1.7 multiply_convert_fusion.2
  24.2 1.4 concatenate.25
  26.0 1.9 all-to-all-done.1
  28.5 5.8 %all-to-all-start = ((f32[32,1,32]{2,1,0:T(1,128)}), f32[32,1,32]{2,1,0:T(1,128)S(1)}, u32[]{:S(2)}, u32[]{:S(2)}) async-start(f32[32,1,32]{2,1,0:T(1,128)} %broadcast_in_dim.20), calls=%async_computation | async-start | bytes 32768 | tf_op jit(solution)/shard_map/all_to_all | solution.py:32
  35.0 6.2 %all-to-all-done = f32[32,1,32]{2,1,0:T(1,128)S(1)} async-done(((f32[32,1,32]{2,1,0:T(1,128)}), f32[32,1,32]{2,1,0:T(1,128)S(1)}, u32[]{:S(2)}, u32[]{:S(2)}) %all-to-all-start) | async-done | bytes 4128 | tf_op jit(solution)/shard_map/all_to_all | solution.py:32
  41.2 16.7 %all-gather.3.cloned.1.call-done = bf16[32,12,1537]{2,1,0:T(8,128)(2,1)} async-done(((bf16[1,12,1537]{2,1,0:T(8,128)(2,1)}), bf16[32,12,1537]{2,1,0:T(8,128)(2,1)}) %all-gather.3.cloned.1.call-update) | async-done | bytes 1180432 | tf_op jit(solution)/shard_map/all_gather | solution.py:20
  57.9 2.5 reshape.260
  60.6 1.2 split.12
  61.7 2.2 copy.74
  63.9 2.3 copy.75
  66.2 2.2 fusion.72
  68.5 1.2 fusion.14
  69.9 1.2 add_add_fusion
  71.0 8.4 %fusion.8 = (f32[2048,384]{1,0:T(8,128)S(1)}, f32[2048,384]{1,0:T(8,128)}) fusion(f32[2048,384]{1,0:T(8,128)S(1)} %add_add_fusion, bf16[384,1537]{1,0:T(8,128)(2,1)} %copy-done.8), kind=kOutput, calls=%fused_computation.16 | convolution fusion | flops 626786304 | bytes 12877824 | tf_op jit(solution)/shard_map/dot_general | solution.py:128
  79.4 1.7 copy-done.4
  81.1 1.5 fusion.116
  83.0 8.0 %psum.28 = f32[32]{0:T(128)S(1)} all-reduce(f32[32]{0:T(128)S(1)} %convolution_bitcast_fusion.1), channel_id=1, replica_groups=mesh['dp_0'=4,'dp_1'=4,'dp_2'=2,'head'=4] {'dp_0'}, use_global_device_ids=true, to_apply=%region_1.2 | all-reduce | flops 32 | bytes 256 | tf_op jit(solution)/shard_map/psum | solution.py:60
  91.0 6.6 %psum.29 = f32[32]{0:T(128)S(1)} all-reduce(f32[32]{0:T(128)S(1)} %psum.28), channel_id=1, replica_groups=mesh['dp_0'=4,'dp_1'=4,'dp_2'=2,'head'=4] {'dp_1'}, use_global_device_ids=true, to_apply=%region_2.3 | all-reduce | flops 32 | bytes 256 | tf_op jit(solution)/shard_map/psum | solution.py:60
  97.6 6.4 %psum.30 = f32[32]{0:T(128)S(1)} all-reduce(f32[32]{0:T(128)S(1)} %psum.29), channel_id=1, replica_groups=mesh['dp_0'=4,'dp_1'=4,'dp_2'=2,'head'=4] {'dp_2'}, use_global_device_ids=true, to_apply=%region_3.4 | all-reduce | flops 32 | bytes 256 | tf_op jit(solution)/shard_map/psum | solution.py:60
  104.0 8.8 %psum.31 = f32[32]{0:T(128)S(1)} all-reduce(f32[32]{0:T(128)S(1)} %psum.30), channel_id=1, replica_groups=mesh['dp_0'=4,'dp_1'=4,'dp_2'=2,'head'=4] {'head'}, use_global_device_ids=true, to_apply=%region_4.5 | all-reduce | flops 32 | bytes 256 | tf_op jit(solution)/shard_map/psum | solution.py:60
  113.1 3.0 fusion.1
  116.2 3.2 fusion.3
  119.4 1.1 fusion.17
  120.5 1.1 fusion.19
  121.6 1.5 fusion.32
  124.1 1.8 fusion
  125.8 3.1 pad_maximum_fusion
  129.4 9.2 %reduce.8 = bf16[32,98306]{1,0:T(8,128)(2,1)} reduce(bf16[32,1,98306]{2,0,1:T(8,128)(2,1)} %pad_maximum_fusion, bf16[]{:T(256)} %broadcast.190), dimensions={1}, to_apply=%copy.78.reduce_sub_computation | reduce | bytes 12583170 | tf_op jit(solution)/shard_map/concatenate | solution.py:65
  138.6 7.7 %reshape.280 = bf16[32,2,49153]{2,1,0:T(2,128)(2,1)} reshape(bf16[32,98306]{1,0:T(8,128)(2,1)} %reduce.8) | data formatting | bytes 12583168
  146.4 6.8 %all-to-all-start.2 = ((bf16[32,2,49153]{2,1,0:T(2,128)(2,1)}), bf16[32,2,49153]{2,1,0:T(2,128)(2,1)}, u32[]{:S(2)}, u32[]{:S(2)}) async-start(bf16[32,2,49153]{2,1,0:T(2,128)(2,1)} %reshape.280), calls=%async_computation.2 | async-start | bytes 12615680 | tf_op jit(solution)/shard_map/all_to_all | solution.py:67
  153.3 2.1 copy.80
  155.3 2.6 copy.84
  159.1 1.6 reshape.250
  160.6 3.8 %reshape.249 = bf16[32,12,2048]{2,1,0:T(8,128)(2,1)} reshape(bf16[384,2048]{1,0:T(8,128)(2,1)} %bitcast.153) | data formatting | bytes 3145728 | tf_op jit(solution)/shard_map/reshape.156
  164.4 3.6 reshape.251
  168.1 1.6 convolution_reduce_fusion
  169.8 5.0 %convolution_convert_fusion.2 = bf16[384,384]{1,0:T(8,128)(2,1)S(1)} fusion(bf16[2048,384]{1,0:T(8,128)(2,1)} %copy-done.13, f32[2048,384]{1,0:T(8,128)} %copy-done.9), kind=kOutput, calls=%fused_computation.51 | convolution fusion | flops 611991552 | bytes 5013504 | tf_op jit(solution)/shard_map/dot_general | solution.py:163
  175.2 2.8 fusion.55
  178.0 1.1 fusion.50
  179.6 1.1 fusion.60
  181.9 1.4 reshape.254
  184.6 127.5 %all-reduce.8.cloned.1.call-done = bf16[4864,128]{1,0:T(8,128)(2,1)} async-done(((bf16[4864,128]{1,0:T(8,128)(2,1)}), bf16[4864,128]{1,0:T(8,128)(2,1)}) %all-reduce.8.cloned.1.call-update) | async-done | bytes 1245200
  316.2 29.3 %reshape.281 = bf16[32,1,98306]{2,1,0:T(2,128)(2,1)} reshape(bf16[32,2,49153]{2,1,0:T(2,128)(2,1)} %all-to-all-done.2) | data formatting | bytes 12583168
  346.5 4.6 %slice-done = bf16[32,1,98304]{2,1,0:T(2,128)(2,1)S(1)} async-done(((bf16[32,1,98306]{2,1,0:T(2,128)(2,1)}), bf16[32,1,98304]{2,1,0:T(2,128)(2,1)S(1)}, s32[]{:S(2)}) %slice-start) | async-done | bytes 6291480 | tf_op jit(solution)/shard_map/slice | solution.py:72
  351.1 6.9 %convolution_convert_fusion.1 = bf16[16,98304]{1,0:T(8,128)(2,1)S(1)} fusion(bf16[32,1,98304]{2,1,0:T(2,128)(2,1)S(1)} %slice-done, f32[32]{0:T(128)S(1)} %fusion.84), kind=kOutput, calls=%fused_computation.2 | convolution fusion | flops 102237696 | bytes 9437312 | tf_op jit(solution)/shard_map/dot_general | solution.py:183
  358.0 2.6 reshape_reshape.14
  (101 shorter events, 18.4 us)
Async XLA Ops:
  7.2 50.7 %all-gather.3.cloned.1.call-start = ((), (), s32[]{:S(2)}) async-start(), calls=%async_computation.3 | async-start | bytes 1757184 | tf_op jit(solution)/shard_map/all_gather | solution.py:20
  12.4 15.5 %all-to-all-start.1 = ((s32[32,1,32]{2,1,0:T(1,128)}), s32[32,1,32]{2,1,0:T(1,128)S(1)}, u32[]{:S(2)}, u32[]{:S(2)}) async-start(s32[32,1,32]{2,1,0:T(1,128)} %broadcast_in_dim.22), calls=%async_computation.1 | async-start | bytes 32768 | tf_op jit(solution)/shard_map/all_to_all | solution.py:32
  24.1 10.4 %copy-start.14 = (s32[8]{0:T(128)S(1)}, s32[8]{0:T(128)}, u32[]{:S(2)}) copy-start(s32[8]{0:T(128)} %param.8) | copy-start | bytes 100
  24.2 10.6 %copy-start.15 = (s32[8]{0:T(128)S(1)}, s32[8]{0:T(128)}, u32[]{:S(2)}) copy-start(s32[8]{0:T(128)} %param.7) | copy-start | bytes 100
  28.5 12.7 %all-to-all-start = ((f32[32,1,32]{2,1,0:T(1,128)}), f32[32,1,32]{2,1,0:T(1,128)S(1)}, u32[]{:S(2)}, u32[]{:S(2)}) async-start(f32[32,1,32]{2,1,0:T(1,128)} %broadcast_in_dim.20), calls=%async_computation | async-start | bytes 32768 | tf_op jit(solution)/shard_map/all_to_all | solution.py:32
  60.4 5.8 %copy-start.8 = (bf16[384,1537]{1,0:T(8,128)(2,1)}, bf16[384,1537]{1,0:T(8,128)(2,1)S(1)}, u32[]{:S(2)}) copy-start(bf16[384,1537]{1,0:T(8,128)(2,1)S(1)} %reshape.260) | copy-start | bytes 3541252
  66.2 2.3 copy-start
  66.2 2.3 copy-start.6
  68.5 1.4 copy-start.3
  71.0 8.4 %copy-start.9 = (f32[2048,384]{1,0:T(8,128)}, f32[2048,384]{1,0:T(8,128)S(1)}, u32[]{:S(2)}) copy-start(f32[2048,384]{1,0:T(8,128)S(1)} %add_add_fusion) | copy-start | bytes 9437188
  79.4 1.7 copy-start.4
  112.9 3.3 copy-start.10
  116.1 3.2 copy-start.13
  116.1 3.2 copy-start.7
  119.3 2.3 copy-start.1
  146.4 169.8 %all-to-all-start.2 = ((bf16[32,2,49153]{2,1,0:T(2,128)(2,1)}), bf16[32,2,49153]{2,1,0:T(2,128)(2,1)}, u32[]{:S(2)}, u32[]{:S(2)}) async-start(bf16[32,2,49153]{2,1,0:T(2,128)(2,1)} %reshape.280), calls=%async_computation.2 | async-start | bytes 12615680 | tf_op jit(solution)/shard_map/all_to_all | solution.py:67
  153.2 158.9 %all-reduce.8.cloned.1.call-start = ((), (), s32[]{:S(2)}) async-start(), calls=%async_computation.4 | async-start | bytes 2490368
  160.6 7.4 %copy-start.5 = (f32[2048,384]{1,0:T(8,128)S(1)}, f32[2048,384]{1,0:T(8,128)}, u32[]{:S(2)}) copy-start(f32[2048,384]{1,0:T(8,128)} %copy-done.4) | copy-start | bytes 9437188
  169.8 5.4 %copy-start.2 = (bf16[2048,384]{1,0:T(8,128)(2,1)S(1)}, bf16[2048,384]{1,0:T(8,128)(2,1)}, u32[]{:S(2)}) copy-start(bf16[2048,384]{1,0:T(8,128)(2,1)} %copy-done.1) | copy-start | bytes 4718596
  175.2 2.8 copy-start.12
  178.0 1.6 copy-start.11
  181.8 1.6 copy-start.16
  346.5 4.6 %slice-start = ((bf16[32,1,98306]{2,1,0:T(2,128)(2,1)}), bf16[32,1,98304]{2,1,0:T(2,128)(2,1)S(1)}, s32[]{:S(2)}) async-start(bf16[32,1,98306]{2,1,0:T(2,128)(2,1)} %reshape.281), calls=%async_computation.5 | async-start | bytes 25165824 | tf_op jit(solution)/shard_map/slice | solution.py:72
Sparse Core Ops, SparseCore 0:
  10.9 46.9 all-gather.2
  183.4 128.6 all-reduce.7
where the time goes:
time: 372 us; the launch traced here: 368 us
  waiting for transfers between devices  152 us (41%)
  local copies, waits for them, and re-layouts  81.8 us (22%)
  matrix products  42 us (11%)
  blocking collectives  29.9 us (8%)
  other arithmetic  24.9 us (7%)
  starting transfers between devices  21.3 us (6%)
  between operations  15.4 us (4%)
    unnamed x3, waiting for transfers between devices  128 us
    unnamed x44, local copies, waits for them, and re-layouts  43.5 us
    psum x4, blocking collectives, by_axis(): return functools.reduce(lax.psum, axes, shard)  29.9 us
    all_gather x1, waiting for transfers between devices, gather_turned(): out = lax.all_gather(both, axis, axis=0, tiled=True)  16.7 us
    all_to_all x2, starting transfers between devices, copy_for_each(): return lax.all_to_all(copies, axis, split_axis=0, concat_axis=0, tiled=True)  14.4 us
    concatenate x2, other arithmetic, side_by_side(): both = jnp.concatenate(columns, axis=along)  12.3 us
    another operation x3, local copies, waits for them, and re-layouts  9 us
    dot_general x1, matrix products, forward_pass(): second_pre = jnp.dot(first_low, mid_w, preferred_element_type=jnp.float32)  8.4 us
  transfers between devices with their start and end apart: 5, of which 4 were waited for; matrix products, arithmetic and copies ran while one was open for 12% of the time, Pallas kernels for 0%

commit v1 on v0

v1 whole, which is shorter than its diff:
```python
import functools

import jax
import jax.numpy as jnp
from jax import lax
from jax.experimental import pallas as pl
from jax.experimental.pallas import tpu as pltpu
from jax.sharding import Mesh
from jax.sharding import PartitionSpec as P

DP = ("dp_0", "dp_1", "dp_2")
CHIPS = ("dp_0", "dp_1")
WHOLE = ("head", "dp_1", "dp_0", "dp_2")
BF16 = jnp.bfloat16
F32 = jnp.float32
TAPS = 4
BT = 256
D = 384
ROWS = 56
GROUP = 2
VMEM_LIMIT = 56 * 1024 * 1024


def swapped(x):
    return lax.ppermute(x, "dp_2", [(0, 1), (1, 0)])


def turned(x, axis, shift):
    count = lax.axis_size(axis)
    return lax.ppermute(x, axis, [(i, (i + shift) % count) for i in range(count)])


def total_over(x, axes):
    for axis in axes:
        x = sum((turned(x, axis, r) for r in range(1, lax.axis_size(axis))), x)
    return x


def scattered_sum(parts, axis, dim):
    count, index = lax.axis_size(axis), lax.axis_index(axis)

    def piece(shift):
        return lax.dynamic_index_in_dim(parts, (index + shift) % count, dim, keepdims=False)

    total = piece(0).astype(F32)
    for r in range(1, count):
        total = total + turned(piece(r).astype(BF16), axis, r).astype(F32)
    return total


def gate(value):
    half = jnp.tanh(0.5 * value)
    act = jnp.maximum(value, 0.2 * value) - 0.8 * jnp.log(0.5 + 0.5 * jnp.abs(half))
    return act, 0.6 + 0.4 * half


def row_mask(valid_ref, step, blocks):
    rows = lax.broadcasted_iota(jnp.int32, (blocks * BT, 1), 0)
    limit = jnp.full_like(rows, valid_ref[step * blocks])
    for j in range(1, blocks):
        limit = jnp.where(rows < j * BT, limit, j * BT + valid_ref[step * blocks + j])
    return rows < limit


def neighbours(x):
    count = x.shape[0]
    place = lax.broadcasted_iota(jnp.int32, (count, 1), 0) % BT
    before = jnp.where(place == 0, 0.0, pltpu.roll(x, 1, 0))
    after = jnp.where(place == BT - 1, 0.0, pltpu.roll(x, count - 1, 0))
    return before, after


def forward_kernel(
    valid_ref, core_ref, feats_ref, own_ref, other_ref, out_w_ref,
    low_ref, mid_grad_ref, slope_ref, sums_ref, weights_ref, wide_ref,
):
    step = pl.program_id(0)

    def unpack(parity, source):
        for chip in range(source.shape[0]):
            tile = source[chip].astype(F32)
            at = 12 * (2 * chip + parity)
            for k in range(4):
                wide_ref[k, at : at + 12, :] = tile[12 * k : 12 * k + 12]

    @pl.when(step == 0)
    def _():
        @pl.when(core_ref[0] == 0)
        def _():
            unpack(0, own_ref)
            unpack(1, other_ref)

        @pl.when(core_ref[0] == 1)
        def _():
            unpack(1, own_ref)
            unpack(0, other_ref)

        weights_ref[...] = wide_ref[...].astype(BF16)

    keep = row_mask(valid_ref, step, GROUP)
    masked = jnp.where(keep, feats_ref[...].astype(F32), 0.0)
    before, after = neighbours(masked)
    first = jnp.dot(before.astype(BF16), weights_ref[0], preferred_element_type=F32)
    first += jnp.dot(masked.astype(BF16), weights_ref[1], preferred_element_type=F32)
    first += jnp.dot(after.astype(BF16), weights_ref[2], preferred_element_type=F32)
    first_act, slope = gate(first)
    low = first_act.astype(BF16)
    low_ref[...] = low
    slope_ref[...] = slope.astype(BF16)
    second = jnp.dot(low, weights_ref[3], preferred_element_type=F32)
    second_act, second_slope = gate(second)
    mid_grad_ref[...] = jnp.where(keep, out_w_ref[...] * second_slope, 0.0).astype(BF16)
    total = jnp.where(keep, second_act + first_act, 0.0)
    for j in range(GROUP):
        sums_ref[j] = jnp.sum(total[j * BT : (j + 1) * BT], 0, keepdims=True)


def backward_kernel(
    valid_ref, owner_ref, mid_grad_ref, slope_ref, weights_ref, out_w_ref, first_grad_ref, slots_ref
):
    step = pl.program_id(0)
    keep = row_mask(valid_ref, step, 1)
    turn = (((1,), (1,)), ((), ()))
    grad = lax.dot_general(mid_grad_ref[...], weights_ref[3], turn, preferred_element_type=F32)
    grad = (grad + jnp.where(keep, out_w_ref[...], 0.0)) * slope_ref[...].astype(F32)
    low = grad.astype(BF16)
    first_grad_ref[...] = low
    before, after = neighbours(low.astype(F32))
    total = lax.dot_general(low, weights_ref[1], turn, preferred_element_type=F32)
    total += lax.dot_general(after.astype(BF16), weights_ref[0], turn, preferred_element_type=F32)
    total += lax.dot_general(before.astype(BF16), weights_ref[2], turn, preferred_element_type=F32)
    slots_ref[0] = jnp.where(keep, total, 0.0).astype(BF16)


def weight_kernel(
    valid_ref, factor_ref, feats_ref, low_ref, mid_grad_ref, first_grad_ref, out_part_ref,
    parts_ref, conv_ref, mid_ref, stage_ref,
):
    step = pl.program_id(0)
    keep = row_mask(valid_ref, step, 1)
    factor = factor_ref[step]
    over_rows = (((0,), (0,)), ((), ()))
    masked = jnp.where(keep, feats_ref[...].astype(F32), 0.0).astype(BF16)
    grad = first_grad_ref[...].astype(F32) * factor
    before, after = neighbours(grad)
    wide = jnp.concatenate([after, grad, before], axis=1).astype(BF16)
    conv = lax.dot_general(masked, wide, over_rows, preferred_element_type=F32)
    mid_grad = (mid_grad_ref[...].astype(F32) * factor).astype(BF16)
    mid = lax.dot_general(low_ref[...], mid_grad, over_rows, preferred_element_type=F32)

    @pl.when(step == 0)
    def _():
        conv_ref[...] = conv
        mid_ref[...] = mid

    @pl.when(step > 0)
    def _():
        conv_ref[...] += conv
        mid_ref[...] += mid

    @pl.when(step == pl.num_programs(0) - 1)
    def _():
        stage_ref[48:56, :] = jnp.zeros((8, D), F32)
        for d in range(parts_ref.shape[0]):
            at = 12 * d
            for k in range(3):
                stage_ref[12 * k : 12 * k + 12, :] = conv_ref[at : at + 12, k * D : (k + 1) * D]
            stage_ref[36:48, :] = mid_ref[at : at + 12, :]
            stage_ref[48:49, :] = out_part_ref[d : d + 1, :]
            parts_ref[d] = stage_ref[...].astype(BF16)


def place_kernel(source_ref, count_ref, factor_ref, received_ref, placed_ref):
    slot = pl.program_id(0)

    @pl.when(slot < count_ref[0])
    def _():
        placed_ref[...] = (received_ref[0].astype(F32) * factor_ref[0]).astype(BF16)

    @pl.when(slot >= count_ref[0])
    def _():
        placed_ref[...] = jnp.zeros_like(placed_ref)


def params():
    return pltpu.CompilerParams(
        dimension_semantics=("arbitrary",), vmem_limit_bytes=VMEM_LIMIT
    )


def fixed(shape):
    return pl.BlockSpec(shape, lambda *_: (0,) * len(shape))


def rows(count):
    return pl.BlockSpec((count, D), lambda i, *_: (i, 0))


def per_device(feats, valid, owner_map, w_conv, w_mid, w_out):
    local = owner_map.shape[0]
    devices = lax.axis_size(DP)
    chips = devices // 2
    capacity = devices // 2
    tokens_here = local * BT
    me = lax.axis_index(DP)
    core = lax.axis_index("dp_2").astype(jnp.int32).reshape(1)

    extras = jnp.concatenate([w_out[0], owner_map.astype(BF16), valid.astype(BF16)])
    extras = jnp.pad(extras, (0, D - extras.shape[0]))[None]
    shard = jnp.concatenate([w_conv[0].reshape(-1, D), w_mid[0], extras], axis=0)
    shard = jnp.pad(shard, ((0, ROWS - shard.shape[0]), (0, 0)))
    copies = jnp.broadcast_to(shard[None], (chips, ROWS, D))
    own = lax.all_to_all(copies, CHIPS, split_axis=0, concat_axis=0, tiled=True)
    other = swapped(own)

    gathered = jnp.stack([own[:, 48, :32], other[:, 48, :32]])
    gathered = jnp.where(core[0] == 0, gathered, gathered[::-1])
    gathered = gathered.transpose(1, 0, 2).reshape(devices, 32).astype(F32)
    out_w = gathered[:, :12].reshape(1, D)
    owners = gathered[:, 12 : 12 + local].astype(jnp.int32)
    valids = gathered[:, 20 : 20 + local]

    low, mid_grad, slope, sums, weights = pl.pallas_call(
        forward_kernel,
        grid_spec=pltpu.PrefetchScalarGridSpec(
            num_scalar_prefetch=2,
            grid=(local // GROUP,),
            in_specs=[
                rows(GROUP * BT),
                fixed((chips, ROWS, D)),
                fixed((chips, ROWS, D)),
                fixed((1, D)),
            ],
            out_specs=[
                rows(GROUP * BT),
                rows(GROUP * BT),
                rows(GROUP * BT),
                pl.BlockSpec((GROUP, 1, D), lambda i, *_: (i, 0, 0)),
                fixed((4, D, D)),
            ],
            scratch_shapes=[pltpu.VMEM((4, D, D), F32)],
        ),
        out_shape=[
            jax.ShapeDtypeStruct((tokens_here, D), BF16),
            jax.ShapeDtypeStruct((tokens_here, D), BF16),
            jax.ShapeDtypeStruct((tokens_here, D), BF16),
            jax.ShapeDtypeStruct((local, 1, D), F32),
            jax.ShapeDtypeStruct((4, D, D), BF16),
        ],
        compiler_params=params(),
        name="forward",
    )(valid, core, feats[0], own, other, out_w)

    first_grad, slots = pl.pallas_call(
        backward_kernel,
        grid_spec=pltpu.PrefetchScalarGridSpec(
            num_scalar_prefetch=2,
            grid=(local,),
            in_specs=[rows(BT), rows(BT), fixed((4, D, D)), fixed((1, D))],
            out_specs=[
                rows(BT),
                pl.BlockSpec((1, BT, D), lambda i, valid_ref, owner_ref: (owner_ref[i], 0, 0)),
            ],
        ),
        out_shape=[
            jax.ShapeDtypeStruct((tokens_here, D), BF16),
            jax.ShapeDtypeStruct((devices, BT, D), BF16),
        ],
        compiler_params=params(),
        name="backward",
    )(valid, owner_map, mid_grad, slope, weights, out_w)

    received = lax.all_to_all(slots, DP, split_axis=0, concat_axis=0, tiled=True)

    images = jnp.arange(devices, dtype=jnp.int32)
    sums = sums[:, 0, :]
    block_sums = jnp.sum(sums * out_w, 1)
    members = (owner_map[:, None] == images[None, :]).astype(F32)
    totals = total_over(jnp.sum(block_sums[:, None] * members, 0)[None], WHOLE)[0]
    tokens = jnp.sum(
        jnp.where(owners.reshape(-1, 1) == images[None, :], valids.reshape(-1, 1), 0.0), 0
    )
    norm = jnp.sqrt(TAPS * tokens)
    factor = -BT * jax.nn.sigmoid(-totals / norm) / norm
    block_factor = jnp.sum(members * factor[None, :], 1)
    own_factor = jnp.sum(jnp.where(images == me, factor, 0.0)).reshape(1)

    out_part = jnp.sum(sums * block_factor[:, None], 0).reshape(devices, 12)
    out_part = jnp.pad(out_part, ((0, 0), (0, D - 12)))
    parts = pl.pallas_call(
        weight_kernel,
        grid_spec=pltpu.PrefetchScalarGridSpec(
            num_scalar_prefetch=2,
            grid=(local,),
            in_specs=[rows(BT)] * 4 + [fixed((devices, D))],
            out_specs=fixed((devices, ROWS, D)),
            scratch_shapes=[
                pltpu.VMEM((D, 3 * D), F32),
                pltpu.VMEM((D, D), F32),
                pltpu.VMEM((ROWS, D), F32),
            ],
        ),
        out_shape=jax.ShapeDtypeStruct((devices, ROWS, D), BF16),
        compiler_params=params(),
        name="weight_grads",
    )(valid, block_factor, feats[0], low, mid_grad, first_grad, out_part)
    parts = parts.reshape(4, 4, 2, ROWS, D)
    parts = scattered_sum(parts, "dp_2", 2)
    parts = scattered_sum(parts, "dp_0", 0)
    parts = scattered_sum(parts, "dp_1", 0) / (devices * local)

    present = jnp.sum((owners == me).astype(jnp.int32), 1)
    rank = jnp.cumsum(present) - present
    count = jnp.sum(present)
    wanted = jnp.minimum(jnp.arange(capacity, dtype=jnp.int32), count - 1)
    hit = (rank[None, :] == wanted[:, None]) & (present[None, :] > 0)
    source = jnp.sum(jnp.where(hit, images[None, :], 0), 1).astype(jnp.int32)
    placed = pl.pallas_call(
        place_kernel,
        grid_spec=pltpu.PrefetchScalarGridSpec(
            num_scalar_prefetch=3,
            grid=(capacity,),
            in_specs=[pl.BlockSpec((1, BT, D), lambda i, source_ref, *_: (source_ref[i], 0, 0))],
            out_specs=rows(BT),
        ),
        out_shape=jax.ShapeDtypeStruct((capacity * BT, D), BF16),
        compiler_params=params(),
        name="place",
    )(source, count.reshape(1), own_factor, received)

    return (
        placed[None],
        parts[:36].reshape(1, 3, 12, D),
        parts[36:48][None],
        parts[48, :12][None],
    )


def solution(mesh):
    split = Mesh(
        mesh.devices.reshape(4, 4, 2, mesh.shape["head"]), ("dp_0", "dp_1", "dp_2", "head")
    )
    in_specs = (
        P("head", DP, None),
        P(DP),
        P(DP),
        P("head", None, DP, None),
        P("head", DP, None),
        P("head", DP),
    )
    out_specs = (P("head", DP, None), P("head", None, DP, None), P("head", DP, None), P("head", DP))
    return jax.shard_map(
        per_device, mesh=split, in_specs=in_specs, out_specs=out_specs, check_vma=False
    )
```

time: 372 us -> 188 us (0.51)
  the two profiles are of different devices: /device:TPU:1 before, /device:TPU:0 now
where the time goes in v1:
time: 188 us; the launch traced here: 186 us
  waiting for transfers between devices  78.4 us (42%)
  Pallas kernels  42.4 us (23%)
  starting transfers between devices  30.9 us (16%)
  blocking collectives  20.2 us (11%)
  other arithmetic  6.11 us (3%)
  local copies, waits for them, and re-layouts  5.98 us (3%)
    ppermute x17, waiting for transfers between devices, turned(): lax.ppermute(x, axis, [(i, (i + shift) % count) for i in range(count)])  76.2 us
    ppermute x17, starting transfers between devices, turned(): lax.ppermute(x, axis, [(i, (i + shift) % count) for i in range(count)])  25.9 us
    all_to_all x1, blocking collectives, per_device(): own = lax.all_to_all(copies, CHIPS, split_axis=0, concat_axis=0, tiled=True)  20.2 us
    pallas_call x1, Pallas kernels, per_device(): pl.pallas_call(weight_kernel, grid_spec=pltpu.PrefetchScalarGridSpec(num_...  11 us
    pallas_call x1, Pallas kernels, per_device(): pl.pallas_call(forward_kernel, grid_spec=pltpu.PrefetchScalarGridSpec(num...  10.7 us
    pallas_call x1, Pallas kernels, per_device(): pl.pallas_call(backward_kernel, grid_spec=pltpu.PrefetchScalarGridSpec(nu...  10.5 us
    pallas_call x1, Pallas kernels, per_device(): pl.pallas_call(place_kernel, grid_spec=pltpu.PrefetchScalarGridSpec(num_s...  10.2 us
    all_to_all x1, starting transfers between devices, per_device(): lax.all_to_all(slots, DP, split_axis=0, concat_axis=0, tiled=True)  5.04 us
  transfers between devices with their start and end apart: 19, of which 15 were waited for; matrix products, arithmetic and copies ran while one was open for 4% of the time, Pallas kernels for 6%

profile of v1, /device:TPU:0, one launch (start us, length us, event | category | flops | bytes accessed | tf_op | source)
XLA Modules:
  0.0 185.5 jit_solution(11070931271531940331)
XLA Ops:
  0.6 0.8 reshape_squeeze.3
  1.4 0.7 convert_element_type.91
  2.1 0.7 convert_element_type.92
  2.7 0.7 fusion.22
  3.5 0.7 fusion.15
  4.3 20.2 %all_to_all.10.own_ref = bf16[16,56,384]{2,1,0:T(8,128)(2,1)S(1)} all-to-all(bf16[16,56,384]{2,1,0:T(8,128)(2,1)S(1)} %broadcast_in_dim.59), channel_id=1, replica_groups=mesh['dp_0'=4,'dp_1'=4,'dp_2'=2,'head'=4] {'dp_0','dp_1'}, dimensions={0} | all-to-all | bytes 1376256 | tf_op jit(solution)/shard_map/all_to_all | solution.py:213
  24.5 2.1 %collective-permute-done.other_ref = bf16[16,56,384]{2,1,0:T(8,128)(2,1)S(1)} collective-permute-done((bf16[16,56,384]{2,1,0:T(8,128)(2,1)S(1)}, bf16[16,56,384]{2,1,0:T(8,128)(2,1)S(1)}, u32[]{:S(2)}, u32[]{:S(2)}) %collective-permute-start) | collective-permute-done | bytes 688160 | tf_op jit(solution)/shard_map/ppermute | solution.py:25
  26.7 0.7 reshape.104.out_w_ref
  27.5 10.7 %forward.1 = (bf16[2048,384]{1,0:T(8,128)(2,1)}, bf16[2048,384]{1,0:T(8,128)(2,1)}, bf16[2048,384]{1,0:T(8,128)(2,1)}, f32[8,1,384]{2,1,0:T(1,128)}, bf16[4,384,384]{2,1,0:T(8,128)(2,1)}) custom-call(s32[8]{0:T(128)} %valid_ref.5, s32[1]{0:T(128)} %bitcast.6.core_ref, bf16[2048,384]{1,0:T(8,128)(2,1)} %bitcast.74, bf16[16,56,384]{2,1,0:T(8,128)(2,1)} %copy-done.1, ...), custom_call_target="tpu_custom_call" | custom-call | tf_op jit(solution)/shard_map/forward/pallas_call | solution.py:223
  38.1 10.5 %backward.1 = (bf16[2048,384]{1,0:T(8,128)(2,1)}, bf16[32,256,384]{2,1,0:T(8,128)(2,1)}) custom-call(s32[8]{0:T(128)} %valid_ref.5, s32[8]{0:T(128)} %owner_ref.1, bf16[2048,384]{1,0:T(8,128)(2,1)} %get-tuple-element.12.mid_grad_ref, bf16[2048,384]{1,0:T(8,128)(2,1)} %get-tuple-element.13.slope_ref, bf16[4,384,384]{2,1,0:T(8,128)(2,1)} %get-tuple-element.14.weights_ref, ...), custom_call_target="tpu_custom_call" | custom-call | tf_op jit(solution)/shard_map/backward/pallas_call | solution.py:254
  48.7 5.0 %all-to-all-start.1 = ((bf16[32,256,384]{2,1,0:T(8,128)(2,1)}), bf16[32,256,384]{2,1,0:T(8,128)(2,1)}, u32[]{:S(2)}, u32[]{:S(2)}) async-start(bf16[32,256,384]{2,1,0:T(8,128)(2,1)} %get-tuple-element.15), calls=%async_computation.1 | async-start | bytes 12582912 | tf_op jit(solution)/shard_map/all_to_all | solution.py:273
  54.1 1.9 %collective-permute-start.1 = (f32[1,32]{1,0:T(1,128)S(1)}, f32[1,32]{1,0:T(1,128)S(1)}, u32[]{:S(2)}, u32[]{:S(2)}) collective-permute-start(f32[1,32]{1,0:T(1,128)S(1)} %bitcast.88), channel_id=1, source_target_pairs={{0,1},{1,2},{2,3},{3,0},{4,5},{5,6},{6,7},{7,4},{8,9},{9,10},{10,1... | collective-permute-start | bytes 392 | tf_op jit(solution)/shard_map/ppermute | solution.py:30
  56.0 3.6 %collective-permute-start.2 = (f32[1,32]{1,0:T(1,128)S(1)}, f32[1,32]{1,0:T(1,128)S(1)}, u32[]{:S(2)}, u32[]{:S(2)}) collective-permute-start(f32[1,32]{1,0:T(1,128)S(1)} %bitcast.89), channel_id=1, source_target_pairs={{0,2},{1,3},{2,0},{3,1},{4,6},{5,7},{6,4},{7,5},{8,10},{9,11},{10,... | collective-permute-start | bytes 392 | tf_op jit(solution)/shard_map/ppermute | solution.py:30
  59.6 1.0 collective-permute-start.3
  61.1 2.0 %collective-permute-done.3 = f32[1,32]{1,0:T(1,128)S(1)} collective-permute-done((f32[1,32]{1,0:T(1,128)S(1)}, f32[1,32]{1,0:T(1,128)S(1)}, u32[]{:S(2)}, u32[]{:S(2)}) %collective-permute-start.3) | collective-permute-done | bytes 160 | tf_op jit(solution)/shard_map/ppermute | solution.py:30
  63.1 1.6 collective-permute-start.4
  64.8 2.7 %collective-permute-start.5 = (f32[1,32]{1,0:T(1,128)S(1)}, f32[1,32]{1,0:T(1,128)S(1)}, u32[]{:S(2)}, u32[]{:S(2)}) collective-permute-start(f32[1,32]{1,0:T(1,128)S(1)} %add_add_fusion.2), channel_id=1, source_target_pairs={{0,16},{8,24},{16,0},{24,8},{1,17},{9,25},{17,1},{25,9},{2,18},{10... | collective-permute-start | bytes 392 | tf_op jit(solution)/shard_map/ppermute | solution.py:30
  67.5 1.4 collective-permute-start.6
  68.9 55.8 %collective-permute-done.4 = f32[1,32]{1,0:T(1,128)S(1)} collective-permute-done((f32[1,32]{1,0:T(1,128)S(1)}, f32[1,32]{1,0:T(1,128)S(1)}, u32[]{:S(2)}, u32[]{:S(2)}) %collective-permute-start.4) | collective-permute-done | bytes 160 | tf_op jit(solution)/shard_map/ppermute | solution.py:30
  124.7 5.0 %collective-permute-done.5 = f32[1,32]{1,0:T(1,128)S(1)} collective-permute-done((f32[1,32]{1,0:T(1,128)S(1)}, f32[1,32]{1,0:T(1,128)S(1)}, u32[]{:S(2)}, u32[]{:S(2)}) %collective-permute-start.5) | collective-permute-done | bytes 160 | tf_op jit(solution)/shard_map/ppermute | solution.py:30
  129.7 1.7 collective-permute-start.7
  131.3 2.8 %collective-permute-start.8 = (f32[1,32]{1,0:T(1,128)S(1)}, f32[1,32]{1,0:T(1,128)S(1)}, u32[]{:S(2)}, u32[]{:S(2)}) collective-permute-start(f32[1,32]{1,0:T(1,128)S(1)} %add_add_fusion.1), channel_id=1, source_target_pairs={{0,64},{32,96},{64,0},{96,32},{1,65},{33,97},{65,1},{97,33},{2,66}... | collective-permute-start | bytes 392 | tf_op jit(solution)/shard_map/ppermute | solution.py:30
  134.1 0.9 collective-permute-start.9
  135.0 1.3 collective-permute-done.8
  136.4 1.3 collective-permute-done.9
  137.8 1.0 collective-permute-done.10
  139.2 0.6 pad.14.out_part_ref
  139.8 11.0 %weight_grads.1 = bf16[32,56,384]{2,1,0:T(8,128)(2,1)} custom-call(s32[8]{0:T(128)} %valid_ref.5, f32[8]{0:T(128)} %copy-done.4, bf16[2048,384]{1,0:T(8,128)(2,1)} %bitcast.75, bf16[2048,384]{1,0:T(8,128)(2,1)} %get-tuple-element.16.low_ref, bf16[2048,384]{1,0:T(8,128)(2,1)} %get-tuple-element.12.mid_grad_ref, ...), custom_call_target="tpu_custom_call" | custom-call | tf_op jit(solution)/shard_map/weight_grads/pallas_call | solution.py:290
  150.9 1.3 dynamic-slice_bitcast_fusion
  152.1 0.3 collective-permute-start.11
  152.4 0.7 convert_reduce_fusion
  154.1 0.3 collective-permute-done.11
  154.7 3.6 %collective-permute-start.13 = (bf16[4,56,384]{2,1,0:T(8,128)(2,1)S(1)}, bf16[4,56,384]{2,1,0:T(8,128)(2,1)S(1)}, u32[]{:S(2)}, u32[]{:S(2)}) collective-permute-start(bf16[4,56,384]{2,1,0:T(8,128)(2,1)S(1)} %get-tuple-element.22), channel_id=1, source_target_pairs={{0,64},{32,96},{64,0},{96,32},{1,65},{33,97},{65,1},{97,33},{2,66}... | collective-permute-start | bytes 516104 | tf_op jit(solution)/shard_map/ppermute | solution.py:30
  158.2 0.6 collective-permute-start.14
  158.9 0.8 select_reduce_fusion.1.source_ref
  159.6 3.1 %collective-permute-done.12 = bf16[4,56,384]{2,1,0:T(8,128)(2,1)S(1)} collective-permute-done((bf16[4,56,384]{2,1,0:T(8,128)(2,1)S(1)}, bf16[4,56,384]{2,1,0:T(8,128)(2,1)S(1)}, u32[]{:S(2)}, u32[]{:S(2)}) %collective-permute-start.12) | collective-permute-done | bytes 172064 | tf_op jit(solution)/shard_map/ppermute | solution.py:30
  162.7 3.7 %collective-permute-done.13 = bf16[4,56,384]{2,1,0:T(8,128)(2,1)S(1)} collective-permute-done((bf16[4,56,384]{2,1,0:T(8,128)(2,1)S(1)}, bf16[4,56,384]{2,1,0:T(8,128)(2,1)S(1)}, u32[]{:S(2)}, u32[]{:S(2)}) %collective-permute-start.13) | collective-permute-done | bytes 172064 | tf_op jit(solution)/shard_map/ppermute | solution.py:30
  166.4 0.3 collective-permute-done.14
  166.8 0.9 collective-permute-start.15
  167.7 1.6 collective-permute-start.16
  169.3 1.2 collective-permute-start.17
  170.5 0.7 fusion.23
  171.2 1.0 collective-permute-done.15
  172.2 1.0 collective-permute-done.16
  173.5 0.5 slice.39
  174.0 0.7 reshape.108
  174.7 0.6 broadcast_in_dim.68
  175.3 10.2 %place.1 = bf16[4096,384]{1,0:T(8,128)(2,1)} custom-call(s32[16]{0:T(128)} %select_reduce_fusion.1.source_ref, s32[1]{0:T(128)} %bitcast.5.count_ref, f32[1]{0:T(128)} %bitcast.10.factor_ref, bf16[32,256,384]{2,1,0:T(8,128)(2,1)} %all-to-all-done.1.received_ref), custom_call_target="tpu_custom_call" | custom-call | tf_op jit(solution)/shard_map/place/pallas_call | solution.py:318
  (57 shorter events, 2.4 us)
Async XLA Ops:
  24.5 2.9 %copy-start.1 = (bf16[16,56,384]{2,1,0:T(8,128)(2,1)}, bf16[16,56,384]{2,1,0:T(8,128)(2,1)S(1)}, u32[]{:S(2)}) copy-start(bf16[16,56,384]{2,1,0:T(8,128)(2,1)S(1)} %all_to_all.10.own_ref) | copy-start | bytes 2064388
  24.5 2.1 %collective-permute-start = (bf16[16,56,384]{2,1,0:T(8,128)(2,1)S(1)}, bf16[16,56,384]{2,1,0:T(8,128)(2,1)S(1)}, u32[]{:S(2)}, u32[]{:S(2)}) collective-permute-start(bf16[16,56,384]{2,1,0:T(8,128)(2,1)S(1)} %all_to_all.10.own_ref), channel_id=1, source_target_pairs={{0,4},{4,0},{1,5},{5,1},{2,6},{6,2},{3,7},{7,3},{8,12},{12,8},{9,1... | collective-permute-start | bytes 2064392 | tf_op jit(solution)/shard_map/ppermute | solution.py:25
  26.6 0.9 copy-start.2
  48.7 5.2 %copy-start.3 = (f32[8,1,384]{2,1,0:T(1,128)S(1)}, f32[8,1,384]{2,1,0:T(1,128)}, u32[]{:S(2)}) copy-start(f32[8,1,384]{2,1,0:T(1,128)} %get-tuple-element.11) | copy-start | bytes 36868
  48.7 5.3 %copy-start.5 = (s32[8]{0:T(128)S(1)}, s32[8]{0:T(128)}, u32[]{:S(2)}) copy-start(s32[8]{0:T(128)} %owner_ref.1) | copy-start | bytes 100
  48.7 126.6 %all-to-all-start.1 = ((bf16[32,256,384]{2,1,0:T(8,128)(2,1)}), bf16[32,256,384]{2,1,0:T(8,128)(2,1)}, u32[]{:S(2)}, u32[]{:S(2)}) async-start(bf16[32,256,384]{2,1,0:T(8,128)(2,1)} %get-tuple-element.15), calls=%async_computation.1 | async-start | bytes 12582912 | tf_op jit(solution)/shard_map/all_to_all | solution.py:273
  54.1 6.8 %collective-permute-start.1 = (f32[1,32]{1,0:T(1,128)S(1)}, f32[1,32]{1,0:T(1,128)S(1)}, u32[]{:S(2)}, u32[]{:S(2)}) collective-permute-start(f32[1,32]{1,0:T(1,128)S(1)} %bitcast.88), channel_id=1, source_target_pairs={{0,1},{1,2},{2,3},{3,0},{4,5},{5,6},{6,7},{7,4},{8,9},{9,10},{10,1... | collective-permute-start | bytes 392 | tf_op jit(solution)/shard_map/ppermute | solution.py:30
  56.0 5.1 %collective-permute-start.2 = (f32[1,32]{1,0:T(1,128)S(1)}, f32[1,32]{1,0:T(1,128)S(1)}, u32[]{:S(2)}, u32[]{:S(2)}) collective-permute-start(f32[1,32]{1,0:T(1,128)S(1)} %bitcast.89), channel_id=1, source_target_pairs={{0,2},{1,3},{2,0},{3,1},{4,6},{5,7},{6,4},{7,5},{8,10},{9,11},{10,... | collective-permute-start | bytes 392 | tf_op jit(solution)/shard_map/ppermute | solution.py:30
  59.6 3.5 %collective-permute-start.3 = (f32[1,32]{1,0:T(1,128)S(1)}, f32[1,32]{1,0:T(1,128)S(1)}, u32[]{:S(2)}, u32[]{:S(2)}) collective-permute-start(f32[1,32]{1,0:T(1,128)S(1)} %bitcast.90), channel_id=1, source_target_pairs={{0,3},{1,0},{2,1},{3,2},{4,7},{5,4},{6,5},{7,6},{8,11},{9,8},{10,9... | collective-permute-start | bytes 392 | tf_op jit(solution)/shard_map/ppermute | solution.py:30
  63.1 61.5 %collective-permute-start.4 = (f32[1,32]{1,0:T(1,128)S(1)}, f32[1,32]{1,0:T(1,128)S(1)}, u32[]{:S(2)}, u32[]{:S(2)}) collective-permute-start(f32[1,32]{1,0:T(1,128)S(1)} %add_add_fusion.2), channel_id=1, source_target_pairs={{0,8},{8,16},{16,24},{24,0},{1,9},{9,17},{17,25},{25,1},{2,10},{10... | collective-permute-start | bytes 392 | tf_op jit(solution)/shard_map/ppermute | solution.py:30
  64.8 64.9 %collective-permute-start.5 = (f32[1,32]{1,0:T(1,128)S(1)}, f32[1,32]{1,0:T(1,128)S(1)}, u32[]{:S(2)}, u32[]{:S(2)}) collective-permute-start(f32[1,32]{1,0:T(1,128)S(1)} %add_add_fusion.2), channel_id=1, source_target_pairs={{0,16},{8,24},{16,0},{24,8},{1,17},{9,25},{17,1},{25,9},{2,18},{10... | collective-permute-start | bytes 392 | tf_op jit(solution)/shard_map/ppermute | solution.py:30
  67.5 62.2 %collective-permute-start.6 = (f32[1,32]{1,0:T(1,128)S(1)}, f32[1,32]{1,0:T(1,128)S(1)}, u32[]{:S(2)}, u32[]{:S(2)}) collective-permute-start(f32[1,32]{1,0:T(1,128)S(1)} %add_add_fusion.2), channel_id=1, source_target_pairs={{0,24},{8,0},{16,8},{24,16},{1,25},{9,1},{17,9},{25,17},{2,26},{10... | collective-permute-start | bytes 392 | tf_op jit(solution)/shard_map/ppermute | solution.py:30
  129.7 5.4 %collective-permute-start.7 = (f32[1,32]{1,0:T(1,128)S(1)}, f32[1,32]{1,0:T(1,128)S(1)}, u32[]{:S(2)}, u32[]{:S(2)}) collective-permute-start(f32[1,32]{1,0:T(1,128)S(1)} %add_add_fusion.1), channel_id=1, source_target_pairs={{0,32},{32,64},{64,96},{96,0},{1,33},{33,65},{65,97},{97,1},{2,34}... | collective-permute-start | bytes 392 | tf_op jit(solution)/shard_map/ppermute | solution.py:30
  131.3 5.0 %collective-permute-start.8 = (f32[1,32]{1,0:T(1,128)S(1)}, f32[1,32]{1,0:T(1,128)S(1)}, u32[]{:S(2)}, u32[]{:S(2)}) collective-permute-start(f32[1,32]{1,0:T(1,128)S(1)} %add_add_fusion.1), channel_id=1, source_target_pairs={{0,64},{32,96},{64,0},{96,32},{1,65},{33,97},{65,1},{97,33},{2,66}... | collective-permute-start | bytes 392 | tf_op jit(solution)/shard_map/ppermute | solution.py:30
  134.1 3.5 %collective-permute-start.9 = (f32[1,32]{1,0:T(1,128)S(1)}, f32[1,32]{1,0:T(1,128)S(1)}, u32[]{:S(2)}, u32[]{:S(2)}) collective-permute-start(f32[1,32]{1,0:T(1,128)S(1)} %add_add_fusion.1), channel_id=1, source_target_pairs={{0,96},{32,0},{64,32},{96,64},{1,97},{33,1},{65,33},{97,65},{2,98}... | collective-permute-start | bytes 392 | tf_op jit(solution)/shard_map/ppermute | solution.py:30
  137.7 1.1 collective-permute-start.10
  139.0 0.8 copy-start.4
  150.9 3.5 %copy-start = (bf16[32,56,384]{2,1,0:T(8,128)(2,1)S(1)}, bf16[32,56,384]{2,1,0:T(8,128)(2,1)}, u32[]{:S(2)}) copy-start(bf16[32,56,384]{2,1,0:T(8,128)(2,1)} %weight_grads.1) | copy-start | bytes 4128772
  152.1 2.2 %collective-permute-start.11 = (bf16[4,4,56,384]{3,2,1,0:T(8,128)(2,1)S(1)}, bf16[4,4,56,384]{3,2,1,0:T(8,128)(2,1)S(1)}, u32[]{:S(2)}, u32[]{:S(2)}) collective-permute-start(bf16[4,4,56,384]{3,2,1,0:T(8,128)(2,1)S(1)} %dynamic-slice_bitcast_fusion), channel_id=1, source_target_pairs={{0,4},{4,0},{1,5},{5,1},{2,6},{6,2},{3,7},{7,3},{8,12},{12,8},{9,1... | collective-permute-start | bytes 2064392 | tf_op jit(solution)/shard_map/ppermute | solution.py:30
  154.6 8.1 %collective-permute-start.12 = (bf16[4,56,384]{2,1,0:T(8,128)(2,1)S(1)}, bf16[4,56,384]{2,1,0:T(8,128)(2,1)S(1)}, u32[]{:S(2)}, u32[]{:S(2)}) collective-permute-start(bf16[4,56,384]{2,1,0:T(8,128)(2,1)S(1)} %get-tuple-element.20), channel_id=1, source_target_pairs={{0,32},{32,64},{64,96},{96,0},{1,33},{33,65},{65,97},{97,1},{2,34}... | collective-permute-start | bytes 516104 | tf_op jit(solution)/shard_map/ppermute | solution.py:30
  154.7 11.7 %collective-permute-start.13 = (bf16[4,56,384]{2,1,0:T(8,128)(2,1)S(1)}, bf16[4,56,384]{2,1,0:T(8,128)(2,1)S(1)}, u32[]{:S(2)}, u32[]{:S(2)}) collective-permute-start(bf16[4,56,384]{2,1,0:T(8,128)(2,1)S(1)} %get-tuple-element.22), channel_id=1, source_target_pairs={{0,64},{32,96},{64,0},{96,32},{1,65},{33,97},{65,1},{97,33},{2,66}... | collective-permute-start | bytes 516104 | tf_op jit(solution)/shard_map/ppermute | solution.py:30
  158.2 8.5 %collective-permute-start.14 = (bf16[4,56,384]{2,1,0:T(8,128)(2,1)S(1)}, bf16[4,56,384]{2,1,0:T(8,128)(2,1)S(1)}, u32[]{:S(2)}, u32[]{:S(2)}) collective-permute-start(bf16[4,56,384]{2,1,0:T(8,128)(2,1)S(1)} %get-tuple-element.21), channel_id=1, source_target_pairs={{0,96},{32,0},{64,32},{96,64},{1,97},{33,1},{65,33},{97,65},{2,98}... | collective-permute-start | bytes 516104 | tf_op jit(solution)/shard_map/ppermute | solution.py:30
  166.8 5.4 %collective-permute-start.15 = (bf16[56,384]{1,0:T(8,128)(2,1)S(1)}, bf16[56,384]{1,0:T(8,128)(2,1)S(1)}, u32[]{:S(2)}, u32[]{:S(2)}) collective-permute-start(bf16[56,384]{1,0:T(8,128)(2,1)S(1)} %get-tuple-element.23), channel_id=1, source_target_pairs={{0,8},{8,16},{16,24},{24,0},{1,9},{9,17},{17,25},{25,1},{2,10},{10... | collective-permute-start | bytes 129032 | tf_op jit(solution)/shard_map/ppermute | solution.py:30
  167.7 5.5 %collective-permute-start.16 = (bf16[56,384]{1,0:T(8,128)(2,1)S(1)}, bf16[56,384]{1,0:T(8,128)(2,1)S(1)}, u32[]{:S(2)}, u32[]{:S(2)}) collective-permute-start(bf16[56,384]{1,0:T(8,128)(2,1)S(1)} %get-tuple-element.25), channel_id=1, source_target_pairs={{0,16},{8,24},{16,0},{24,8},{1,17},{9,25},{17,1},{25,9},{2,18},{10... | collective-permute-start | bytes 129032 | tf_op jit(solution)/shard_map/ppermute | solution.py:30
  169.3 4.1 %collective-permute-start.17 = (bf16[56,384]{1,0:T(8,128)(2,1)S(1)}, bf16[56,384]{1,0:T(8,128)(2,1)S(1)}, u32[]{:S(2)}, u32[]{:S(2)}) collective-permute-start(bf16[56,384]{1,0:T(8,128)(2,1)S(1)} %get-tuple-element.24), channel_id=1, source_target_pairs={{0,24},{8,0},{16,8},{24,16},{1,25},{9,1},{17,9},{25,17},{2,26},{10... | collective-permute-start | bytes 129032 | tf_op jit(solution)/shard_map/ppermute | solution.py:30

commit v2 on v1

v2 whole, which is shorter than its diff:
```python
import jax
import jax.numpy as jnp
from jax import lax
from jax.experimental import pallas as pl
from jax.experimental.pallas import tpu as pltpu
from jax.sharding import Mesh
from jax.sharding import PartitionSpec as P

DP = ("dp_0", "dp_1", "dp_2")
CHIPS = ("dp_0", "dp_1")
BF16 = jnp.bfloat16
F32 = jnp.float32
TAPS = 4
BT = 256
D = 384
SHARD = 12
EXTRA = 4 * SHARD
ROWS = 56
GROUP = 2
VMEM_LIMIT = 20 * 1024 * 1024

IN_VMEM = pl.BlockSpec(memory_space=pltpu.VMEM)
IN_SMEM = pl.BlockSpec(memory_space=pltpu.SMEM)
IN_HBM = pl.BlockSpec(memory_space=pltpu.HBM)
OVER_LAST = (((1,), (1,)), ((), ()))
OVER_ROWS = (((0,), (0,)), ((), ()))


def swapped(x):
    return lax.ppermute(x, "dp_2", [(0, 1), (1, 0)])


def turned(x, axis, shift):
    count = lax.axis_size(axis)
    return lax.ppermute(x, axis, [(i, (i + shift) % count) for i in range(count)])


def total_over(x, axis):
    return sum((turned(x, axis, r) for r in range(1, lax.axis_size(axis))), x)


def scattered_sum(parts, axis, dim):
    count, index = lax.axis_size(axis), lax.axis_index(axis)

    def piece(shift):
        return lax.dynamic_index_in_dim(parts, (index + shift) % count, dim, keepdims=False)

    total = piece(0).astype(F32)
    for r in range(1, count):
        total = total + turned(piece(r).astype(BF16), axis, r).astype(F32)
    return total


def gate(value):
    half = jnp.tanh(0.5 * value)
    act = jnp.maximum(value, 0.2 * value) - 0.8 * jnp.log(0.5 + 0.5 * jnp.abs(half))
    return act, 0.6 + 0.4 * half


def row_mask(valid_ref, first, blocks):
    rows = lax.broadcasted_iota(jnp.int32, (blocks * BT, 1), 0)
    limit = jnp.full_like(rows, valid_ref[first])
    for j in range(1, blocks):
        limit = jnp.where(rows < j * BT, limit, j * BT + valid_ref[first + j])
    return rows < limit


def neighbours(x):
    count = x.shape[0]
    place = lax.broadcasted_iota(jnp.int32, (count, 1), 0) % BT
    before = jnp.where(place == 0, 0.0, pltpu.roll(x, 1, 0))
    after = jnp.where(place == BT - 1, 0.0, pltpu.roll(x, count - 1, 0))
    return before.astype(BF16), after.astype(BF16)


def pack_kernel(valid_ref, owner_ref, conv_ref, mid_ref, out_ref, copies_ref, stage_ref):
    local = valid_ref.shape[0]
    lane = lax.broadcasted_iota(jnp.int32, (1, D), 1)
    extras = jnp.zeros((1, D), F32)
    for j in range(local):
        extras = jnp.where(lane == SHARD + j, owner_ref[j].astype(F32), extras)
        extras = jnp.where(lane == SHARD + local + j, valid_ref[j].astype(F32), extras)
    stage_ref[EXTRA:ROWS, :] = jnp.zeros((ROWS - EXTRA, D), F32)
    for k in range(3):
        stage_ref[SHARD * k : SHARD * (k + 1), :] = conv_ref[k].astype(F32)
    stage_ref[3 * SHARD : EXTRA, :] = mid_ref[...].astype(F32)
    stage_ref[EXTRA : EXTRA + 1, :] = extras
    stage_ref[EXTRA : EXTRA + 1, 0:SHARD] = out_ref[...].astype(F32)
    packed = stage_ref[...].astype(BF16)
    for j in range(copies_ref.shape[0]):
        copies_ref[j] = packed


def forward_kernel(
    valid_ref, core_ref, feats_ref, own_ref, other_ref,
    masked_out, low_out, mid_grad_out, mid_grad_ref, slope_ref, sums_ref, weights_ref, out_w_ref,
    extras_ref, raw_ref, masked_ref, low_ref, wide_ref, sems, out_sems,
):
    local = valid_ref.shape[0]
    copies, departures = [], []

    def send(source, target, rows, sem):
        copy = pltpu.make_async_copy(source.at[rows], target.at[rows], sem)
        copy.start()
        departures.append(copy)

    for j in range(0, local, GROUP):
        rows = pl.ds(j * BT, GROUP * BT)
        copy = pltpu.make_async_copy(feats_ref.at[rows], raw_ref.at[rows], sems.at[j // GROUP])
        copy.start()
        copies.append(copy)

    def unpack(parity, source):
        for chip in range(source.shape[0]):
            tile = source[chip].astype(F32)
            device = 2 * chip + parity
            at = SHARD * device
            for k in range(4):
                wide_ref[k, at : at + SHARD, :] = tile[SHARD * k : SHARD * (k + 1)]
            extras_ref[device : device + 1, :] = tile[EXTRA : EXTRA + 1, :128]

    @pl.when(core_ref[0] == 0)
    def _():
        unpack(0, own_ref)
        unpack(1, other_ref)

    @pl.when(core_ref[0] == 1)
    def _():
        unpack(1, own_ref)
        unpack(0, other_ref)

    weights_ref[...] = wide_ref[...].astype(BF16)
    devices = extras_ref.shape[0]
    column = lax.broadcasted_iota(jnp.int32, (128, D), 1).astype(F32)
    place = lax.broadcasted_iota(jnp.int32, (128, D), 0).astype(F32)
    home = jnp.floor((column + 0.5) * (1.0 / SHARD))
    pick = jnp.where(column - SHARD * home == place, 1.0, 0.0).astype(BF16)
    spread = jnp.dot(extras_ref[...].astype(BF16), pick, preferred_element_type=F32)
    device = lax.broadcasted_iota(jnp.int32, (devices, D), 0).astype(F32)
    out_w = jnp.sum(jnp.where(home[:devices] == device, spread, 0.0), 0, keepdims=True)
    out_w_ref[...] = out_w

    for j in range(0, local, GROUP):
        rows = pl.ds(j * BT, GROUP * BT)
        copies[j // GROUP].wait()
        keep = row_mask(valid_ref, j, GROUP)
        masked = jnp.where(keep, raw_ref[rows, :].astype(F32), 0.0)
        before, after = neighbours(masked)
        masked = masked.astype(BF16)
        masked_ref[rows, :] = masked
        first = jnp.dot(before, weights_ref[0], preferred_element_type=F32)
        first += jnp.dot(masked, weights_ref[1], preferred_element_type=F32)
        first += jnp.dot(after, weights_ref[2], preferred_element_type=F32)
        first_act, slope = gate(first)
        low = first_act.astype(BF16)
        low_ref[rows, :] = low
        slope_ref[rows, :] = slope.astype(BF16)
        second = jnp.dot(low, weights_ref[3], preferred_element_type=F32)
        second_act, second_slope = gate(second)
        mid_grad_ref[rows, :] = jnp.where(keep, out_w * second_slope, 0.0).astype(BF16)
        total = jnp.where(keep, second_act + first_act, 0.0)
        for i in range(GROUP):
            block = jnp.sum(total[i * BT : (i + 1) * BT], 0, keepdims=True)
            sums_ref[j + i : j + i + 1, :] = block
        send(masked_ref, masked_out, rows, out_sems.at[0, j // GROUP])
        send(low_ref, low_out, rows, out_sems.at[1, j // GROUP])
        send(mid_grad_ref, mid_grad_out, rows, out_sems.at[2, j // GROUP])
    for copy in departures:
        copy.wait()


def backward_kernel(
    valid_ref, owner_ref, mid_grad_ref, slope_ref, weights_ref, out_w_ref,
    first_grad_out, slots_ref, first_grad_ref, ready_ref, sems, out_sems,
):
    local = valid_ref.shape[0]
    copies = []
    for j in range(local):
        rows = pl.ds(j * BT, BT)
        keep = row_mask(valid_ref, j, 1)
        grad = lax.dot_general(
            mid_grad_ref[rows, :], weights_ref[3], OVER_LAST, preferred_element_type=F32
        )
        grad = (grad + jnp.where(keep, out_w_ref[...], 0.0)) * slope_ref[rows, :].astype(F32)
        before, after = neighbours(grad)
        low = grad.astype(BF16)
        first_grad_ref[rows, :] = low
        copy = pltpu.make_async_copy(
            first_grad_ref.at[rows], first_grad_out.at[rows], out_sems.at[j]
        )
        copy.start()
        copies.append(copy)
        total = lax.dot_general(low, weights_ref[1], OVER_LAST, preferred_element_type=F32)
        total += lax.dot_general(after, weights_ref[0], OVER_LAST, preferred_element_type=F32)
        total += lax.dot_general(before, weights_ref[2], OVER_LAST, preferred_element_type=F32)
        ready_ref[j] = jnp.where(keep, total, 0.0).astype(BF16)
        copy = pltpu.make_async_copy(ready_ref.at[j], slots_ref.at[owner_ref[j]], sems.at[j])
        copy.start()
        copies.append(copy)
    for copy in copies:
        copy.wait()


def weight_kernel(
    factor_ref, masked_ref, low_ref, mid_grad_ref, first_grad_ref, sums_ref,
    parts_ref, conv_ref, mid_ref, stage_ref,
):
    local = factor_ref.shape[0]
    out = jnp.zeros((1, D), F32)
    for j in range(local):
        rows = pl.ds(j * BT, BT)
        factor = factor_ref[j]
        out += sums_ref[j : j + 1, :] * factor
        grad = first_grad_ref[rows, :].astype(F32) * factor
        before, after = neighbours(grad)
        mid_grad = (mid_grad_ref[rows, :].astype(F32) * factor).astype(BF16)
        masked = masked_ref[rows, :]
        terms = [
            lax.dot_general(masked, x, OVER_ROWS, preferred_element_type=F32)
            for x in (after, grad.astype(BF16), before)
        ]
        mid = lax.dot_general(low_ref[rows, :], mid_grad, OVER_ROWS, preferred_element_type=F32)
        for k in range(3):
            conv_ref[k] = terms[k] if j == 0 else conv_ref[k] + terms[k]
        mid_ref[...] = mid if j == 0 else mid_ref[...] + mid

    devices = parts_ref.shape[0]
    column = lax.broadcasted_iota(jnp.int32, (D, D), 0).astype(F32)
    place = lax.broadcasted_iota(jnp.int32, (D, D), 1).astype(F32)
    home = jnp.floor((column + 0.5) * (1.0 / SHARD))
    pick = jnp.where(column - SHARD * home == place, 1.0, 0.0).astype(BF16)
    device = lax.broadcasted_iota(jnp.int32, (devices, D), 0).astype(F32)
    lane = lax.broadcasted_iota(jnp.int32, (devices, D), 1).astype(F32)
    mine = jnp.floor((lane + 0.5) * (1.0 / SHARD)) == device
    out_rows = jnp.where(mine, out, 0.0).astype(BF16)
    out_rows = jnp.dot(out_rows, pick, preferred_element_type=F32)
    stage_ref[EXTRA:ROWS, :] = jnp.zeros((ROWS - EXTRA, D), F32)
    for d in range(devices):
        at = SHARD * d
        for k in range(3):
            stage_ref[SHARD * k : SHARD * (k + 1), :] = conv_ref[k, at : at + SHARD, :]
        stage_ref[3 * SHARD : EXTRA, :] = mid_ref[at : at + SHARD, :]
        stage_ref[EXTRA : EXTRA + 1, :] = out_rows[d : d + 1, :]
        parts_ref[d] = stage_ref[...].astype(BF16)


def place_kernel(
    source_ref, count_ref, factor_ref, received_ref, placed_ref, raw_ref, ready_ref, in_sems, out_sems
):
    capacity = source_ref.shape[0]
    arrivals, departures = [], []
    for slot in range(capacity):
        copy = pltpu.make_async_copy(
            received_ref.at[source_ref[slot]], raw_ref.at[slot], in_sems.at[slot]
        )
        copy.start()
        arrivals.append(copy)
    for slot in range(capacity):
        arrivals[slot].wait()
        factor = jnp.where(slot < count_ref[0], factor_ref[0], 0.0)
        ready_ref[slot] = (raw_ref[slot].astype(F32) * factor).astype(BF16)
        copy = pltpu.make_async_copy(
            ready_ref.at[slot], placed_ref.at[pl.ds(slot * BT, BT)], out_sems.at[slot]
        )
        copy.start()
        departures.append(copy)
    for copy in departures:
        copy.wait()


def in_hbm(x):
    return pltpu.with_memory_space_constraint(x, pltpu.HBM)


def in_vmem(x):
    return pltpu.with_memory_space_constraint(x, pltpu.VMEM)


def call(kernel, name, in_specs, outs, scratch=()):
    return pl.pallas_call(
        kernel,
        in_specs=in_specs,
        out_specs=[spec for spec, _, _ in outs],
        out_shape=[
            (pltpu.HBM if spec is IN_HBM else pltpu.VMEM)(shape, dtype) for spec, shape, dtype in outs
        ],
        scratch_shapes=list(scratch),
        compiler_params=pltpu.CompilerParams(vmem_limit_bytes=VMEM_LIMIT),
        name=name,
    )


def per_device(feats, valid, owner_map, w_conv, w_mid, w_out):
    local = owner_map.shape[0]
    devices = lax.axis_size(DP)
    chips = devices // 2
    capacity = devices // 2
    tokens_here = local * BT
    me = lax.axis_index(DP)
    core = lax.axis_index("dp_2").astype(jnp.int32).reshape(1)
    images = jnp.arange(devices, dtype=jnp.int32)

    (copies,) = call(
        pack_kernel,
        "pack",
        [IN_SMEM, IN_SMEM, IN_VMEM, IN_VMEM, IN_VMEM],
        [(IN_VMEM, (chips, ROWS, D), BF16)],
        [pltpu.VMEM((ROWS, D), F32)],
    )(valid, owner_map, w_conv[0], w_mid[0], w_out)
    own = lax.all_to_all(copies, CHIPS, split_axis=0, concat_axis=0, tiled=True)
    other = swapped(own)

    here = (IN_VMEM, (tokens_here, D), BF16)
    later = (IN_HBM, (tokens_here, D), BF16)
    masked, low, mid_grad, mid_grad_here, slope, sums, weights, out_w, extras = call(
        forward_kernel,
        "forward",
        [IN_SMEM, IN_SMEM, IN_HBM, IN_VMEM, IN_VMEM],
        [
            later,
            later,
            later,
            here,
            here,
            (IN_VMEM, (local, D), F32),
            (IN_VMEM, (4, D, D), BF16),
            (IN_VMEM, (1, D), F32),
            (IN_VMEM, (devices, 128), F32),
        ],
        [
            pltpu.VMEM((tokens_here, D), BF16),
            pltpu.VMEM((tokens_here, D), BF16),
            pltpu.VMEM((tokens_here, D), BF16),
            pltpu.VMEM((4, D, D), F32),
            pltpu.SemaphoreType.DMA((local // GROUP,)),
            pltpu.SemaphoreType.DMA((3, local // GROUP)),
        ],
    )(valid, core, in_hbm(feats[0]), in_vmem(own), in_vmem(other))

    members = (owner_map[:, None] == images[None, :]).astype(F32)
    block_sums = jnp.sum(sums * out_w, 1)
    totals = jnp.sum(block_sums[:, None] * members, 0)
    totals = jnp.broadcast_to(totals[None, None, :], (devices, 1, devices))
    totals = lax.all_to_all(totals, DP, split_axis=0, concat_axis=0, tiled=True)

    first_grad, slots = call(
        backward_kernel,
        "backward",
        [IN_SMEM, IN_SMEM, IN_VMEM, IN_VMEM, IN_VMEM, IN_VMEM],
        [later, (IN_HBM, (devices, BT, D), BF16)],
        [
            pltpu.VMEM((tokens_here, D), BF16),
            pltpu.VMEM((local, BT, D), BF16),
            pltpu.SemaphoreType.DMA((local,)),
            pltpu.SemaphoreType.DMA((local,)),
        ],
    )(valid, owner_map, in_vmem(mid_grad_here), in_vmem(slope), in_vmem(weights), out_w)

    slots, totals = lax.optimization_barrier((slots, totals))
    received = lax.all_to_all(slots, DP, split_axis=0, concat_axis=0, tiled=True)

    totals = total_over(jnp.sum(totals[:, 0, :], 0)[None], "head")[0]
    owners = extras[:, SHARD : SHARD + local].astype(jnp.int32)
    valids = extras[:, SHARD + local : SHARD + 2 * local]
    tokens = jnp.sum(jnp.where(owners[:, :, None] == images, valids[:, :, None], 0.0), (0, 1))
    norm = jnp.sqrt(TAPS * tokens)
    factor = -BT * jax.nn.sigmoid(-totals / norm) / norm
    block_factor = jnp.sum(members * factor[None, :], 1)
    own_factor = jnp.sum(jnp.where(images == me, factor, 0.0)).reshape(1)

    (parts,) = call(
        weight_kernel,
        "weight_grads",
        [IN_SMEM, IN_VMEM, IN_VMEM, IN_VMEM, IN_VMEM, IN_VMEM],
        [(IN_VMEM, (devices, ROWS, D), BF16)],
        [pltpu.VMEM((3, D, D), F32), pltpu.VMEM((D, D), F32), pltpu.VMEM((ROWS, D), F32)],
    )(block_factor, masked, low, mid_grad, first_grad, sums)
    parts = parts.reshape(4, 4, 2, ROWS, D)
    parts = scattered_sum(parts, "dp_2", 2)
    parts = scattered_sum(parts, "dp_0", 0)
    parts = scattered_sum(parts, "dp_1", 0) / (devices * local)

    present = jnp.sum((owners == me).astype(jnp.int32), 1)
    rank = jnp.sum(jnp.where(images[None, :] < images[:, None], present[None, :], 0), 1)
    count = jnp.sum(present)
    wanted = jnp.minimum(jnp.arange(capacity, dtype=jnp.int32), count - 1)
    hit = (rank[None, :] == wanted[:, None]) & (present[None, :] > 0)
    source = jnp.sum(jnp.where(hit, images[None, :], 0), 1).astype(jnp.int32)
    (placed,) = call(
        place_kernel,
        "place",
        [IN_SMEM, IN_SMEM, IN_SMEM, IN_HBM],
        [(IN_HBM, (capacity * BT, D), BF16)],
        [
            pltpu.VMEM((capacity, BT, D), BF16),
            pltpu.VMEM((capacity, BT, D), BF16),
            pltpu.SemaphoreType.DMA((capacity,)),
            pltpu.SemaphoreType.DMA((capacity,)),
        ],
    )(source, count.reshape(1), own_factor, received)

    return (
        placed[None],
        parts[: 3 * SHARD].reshape(1, 3, SHARD, D),
        parts[3 * SHARD : EXTRA][None],
        parts[EXTRA, :SHARD][None],
    )


def solution(mesh):
    split = Mesh(
        mesh.devices.reshape(4, 4, 2, mesh.shape["head"]), ("dp_0", "dp_1", "dp_2", "head")
    )
    in_specs = (
        P("head", DP, None),
        P(DP),
        P(DP),
        P("head", None, DP, None),
        P("head", DP, None),
        P("head", DP),
    )
    out_specs = (P("head", DP, None), P("head", None, DP, None), P("head", DP, None), P("head", DP))
    return jax.shard_map(
        per_device, mesh=split, in_specs=in_specs, out_specs=out_specs, check_vma=False
    )
```

time: 188 us -> 158 us (0.84)
  the two profiles are of different devices: /device:TPU:0 before, /device:TPU:1 now
where the time goes in v2:
time: 158 us; the launch traced here: 156 us
  waiting for transfers between devices  60.6 us (38%)
  starting transfers between devices  30 us (19%)
  Pallas kernels  27 us (17%)
  blocking collectives  19.6 us (12%)
  local copies, waits for them, and re-layouts  14.8 us (9%)
  other arithmetic  2.62 us (2%)
  between operations  1.63 us (1%)
    ppermute x10, waiting for transfers between devices, turned(): lax.ppermute(x, axis, [(i, (i + shift) % count) for i in range(count)])  58.8 us
    all_to_all x1, blocking collectives, per_device(): own = lax.all_to_all(copies, CHIPS, split_axis=0, concat_axis=0, tiled=True)  19.6 us
    ppermute x10, starting transfers between devices, turned(): lax.ppermute(x, axis, [(i, (i + shift) % count) for i in range(count)])  16.4 us
    unnamed x30, local copies, waits for them, and re-layouts  12.2 us
    pallas_call x1, Pallas kernels, per_device(): call(forward_kernel, 'forward', [IN_SMEM, IN_SMEM, IN_HBM, IN_VMEM, IN_VM...  9.66 us
    all_to_all x1, starting transfers between devices, per_device(): lax.all_to_all(slots, DP, split_axis=0, concat_axis=0, tiled=True)  7.7 us
    pallas_call x1, Pallas kernels, per_device(): call(backward_kernel, 'backward', [IN_SMEM, IN_SMEM, IN_VMEM, IN_VMEM, IN...  6.43 us
    pallas_call x1, Pallas kernels, per_device(): call(place_kernel, 'place', [IN_SMEM, IN_SMEM, IN_SMEM, IN_HBM], [(IN_HBM...  5.83 us
  transfers between devices with their start and end apart: 13, of which 7 were waited for; matrix products, arithmetic and copies ran while one was open for 3% of the time, Pallas kernels for 7%

profile of v2, /device:TPU:1, one launch (start us, length us, event | category | flops | bytes accessed | tf_op | source)
XLA Modules:
  0.0 156.3 jit_solution(5627108488569447034)
XLA Ops:
  0.7 0.8 copy-done.8
  1.4 0.7 copy-done.9
  2.1 0.7 copy-done.10
  2.8 0.7 copy-done.12
  3.4 0.7 copy-done.14
  4.1 0.6 pack.1
  4.7 19.6 %all_to_all.15.own_ref = bf16[16,56,384]{2,1,0:T(8,128)(2,1)S(1)} all-to-all(bf16[16,56,384]{2,1,0:T(8,128)(2,1)S(1)} %pack.1), channel_id=1, replica_groups=mesh['dp_0'=4,'dp_1'=4,'dp_2'=2,'head'=4] {'dp_0','dp_1'}, dimensions={0} | all-to-all | bytes 1376256 | tf_op jit(solution)/shard_map/all_to_all | solution.py:310
  24.3 2.0 %collective-permute-start = (bf16[16,56,384]{2,1,0:T(8,128)(2,1)S(1)}, bf16[16,56,384]{2,1,0:T(8,128)(2,1)S(1)}, u32[]{:S(2)}, u32[]{:S(2)}) collective-permute-start(bf16[16,56,384]{2,1,0:T(8,128)(2,1)S(1)} %all_to_all.15.own_ref), channel_id=1, source_target_pairs={{0,4},{4,0},{1,5},{5,1},{2,6},{6,2},{3,7},{7,3},{8,12},{12,8},{9,1... | collective-permute-start | bytes 2064392 | tf_op jit(solution)/shard_map/ppermute | solution.py:30
  26.3 1.8 %collective-permute-done.other_ref = bf16[16,56,384]{2,1,0:T(8,128)(2,1)S(1)} collective-permute-done((bf16[16,56,384]{2,1,0:T(8,128)(2,1)S(1)}, bf16[16,56,384]{2,1,0:T(8,128)(2,1)S(1)}, u32[]{:S(2)}, u32[]{:S(2)}) %collective-permute-start) | collective-permute-done | bytes 688160 | tf_op jit(solution)/shard_map/ppermute | solution.py:30
  28.1 0.8 copy-done.6
  29.0 1.1 copy-done.7
  30.1 9.7 %forward.1 = (bf16[2048,384]{1,0:T(8,128)(2,1)}, bf16[2048,384]{1,0:T(8,128)(2,1)}, bf16[2048,384]{1,0:T(8,128)(2,1)}, bf16[2048,384]{1,0:T(8,128)(2,1)S(1)}, bf...) custom-call(s32[8]{0:T(128)S(1)} %copy-done.11, ...), custom_call_target="tpu_custom_call" | custom-call | tf_op jit(solution)/shard_map/forward/pallas_call | solution.py:315
  39.7 1.2 copy-done
  40.9 0.1 multiply_reduce_fusion
  41.1 0.6 broadcast_in_dim.73
  41.8 3.9 %all-to-all-start.1 = ((f32[32,1,32]{2,1,0:T(1,128)}), f32[32,1,32]{2,1,0:T(1,128)S(1)}, u32[]{:S(2)}, u32[]{:S(2)}) async-start(f32[32,1,32]{2,1,0:T(1,128)} %broadcast_in_dim.73), calls=%async_computation.1 | async-start | bytes 32768 | tf_op jit(solution)/shard_map/all_to_all | solution.py:344
  45.6 1.4 copy-done.1
  47.0 6.4 %backward.1 = (bf16[2048,384]{1,0:T(8,128)(2,1)}, bf16[32,256,384]{2,1,0:T(8,128)(2,1)}) custom-call(s32[8]{0:T(128)S(1)} %copy-done.11, s32[8]{0:T(128)S(1)} %copy-done.13, bf16[2048,384]{1,0:T(8,128)(2,1)S(1)} %get-tuple-element.18.mid_grad_ref, bf16[2048,384]{1,0:T(8,128)(2,1)S(1)} %copy-done.1, bf16[4,384,384]{2,1,0:T(8,128)(2,1)S(1)} %get-tuple-element.20.weights_ref, ...), custom_call_target="tpu_custom_call" | custom-call | tf_op jit(solution)/shard_map/backward/pallas_call | solution.py:346
  53.5 7.7 %all-to-all-start.2 = ((bf16[32,256,384]{2,1,0:T(8,128)(2,1)}), bf16[32,256,384]{2,1,0:T(8,128)(2,1)}, u32[]{:S(2)}, u32[]{:S(2)}) async-start(bf16[32,256,384]{2,1,0:T(8,128)(2,1)} %get-tuple-element.25), calls=%async_computation.2 | async-start | bytes 12582912 | tf_op jit(solution)/shard_map/all_to_all | solution.py:360
  61.3 0.2 select_reduce_fusion
  61.5 1.7 %collective-permute-start.1 = (f32[1,32]{1,0:T(1,128)S(1)}, f32[1,32]{1,0:T(1,128)S(1)}, u32[]{:S(2)}, u32[]{:S(2)}) collective-permute-start(f32[1,32]{1,0:T(1,128)S(1)} %bitcast.63), channel_id=1, source_target_pairs={{0,1},{1,2},{2,3},{3,0},{4,5},{5,6},{6,7},{7,4},{8,9},{9,10},{10,1... | collective-permute-start | bytes 392 | tf_op jit(solution)/shard_map/ppermute | solution.py:35
  63.2 3.3 %collective-permute-start.2 = (f32[1,32]{1,0:T(1,128)S(1)}, f32[1,32]{1,0:T(1,128)S(1)}, u32[]{:S(2)}, u32[]{:S(2)}) collective-permute-start(f32[1,32]{1,0:T(1,128)S(1)} %bitcast.64), channel_id=1, source_target_pairs={{0,2},{1,3},{2,0},{3,1},{4,6},{5,7},{6,4},{7,5},{8,10},{9,11},{10,... | collective-permute-start | bytes 392 | tf_op jit(solution)/shard_map/ppermute | solution.py:35
  66.5 0.7 collective-permute-start.3
  67.2 0.6 collective-permute-done.2
  67.8 1.5 collective-permute-done.3
  69.3 0.2 select_reduce_fusion.3.factor_ref
  69.5 1.4 copy-done.3
  70.9 1.4 copy-done.4
  72.3 1.4 copy-done.5
  73.7 4.5 %weight_grads.1 = bf16[32,56,384]{2,1,0:T(8,128)(2,1)S(1)} custom-call(f32[8]{0:T(128)S(1)} %select_reduce_fusion.3.factor_ref, bf16[2048,384]{1,0:T(8,128)(2,1)S(1)} %copy-done.2, bf16[2048,384]{1,0:T(8,128)(2,1)S(1)} %copy-done.3, bf16[2048,384]{1,0:T(8,128)(2,1)S(1)} %copy-done.4, bf16[2048,384]{1,0:T(8,128)(2,1)S(1)} %copy-done.5, ...), custom_call_target="tpu_custom_call" | custom-call | tf_op jit(solution)/shard_map/weight_grads/pallas_call | solution.py:371
  78.3 1.7 %collective-permute-start.4 = (bf16[4,4,56,384]{3,2,1,0:T(8,128)(2,1)S(1)}, bf16[4,4,56,384]{3,2,1,0:T(8,128)(2,1)S(1)}, u32[]{:S(2)}, u32[]{:S(2)}) collective-permute-start(bf16[4,4,56,384]{3,2,1,0:T(8,128)(2,1)S(1)} %dynamic-slice_bitcast_fusion), channel_id=1, source_target_pairs={{0,4},{4,0},{1,5},{5,1},{2,6},{6,2},{3,7},{7,3},{8,12},{12,8},{9,1... | collective-permute-start | bytes 2064392 | tf_op jit(solution)/shard_map/ppermute | solution.py:35
  80.0 0.7 convert_reduce_fusion
  81.5 0.3 collective-permute-done.4
  81.8 0.2 convert_add_fusion
  82.0 1.5 collective-permute-start.5
  83.5 2.4 %collective-permute-start.6 = (bf16[4,56,384]{2,1,0:T(8,128)(2,1)S(1)}, bf16[4,56,384]{2,1,0:T(8,128)(2,1)S(1)}, u32[]{:S(2)}, u32[]{:S(2)}) collective-permute-start(bf16[4,56,384]{2,1,0:T(8,128)(2,1)S(1)} %get-tuple-element.36), channel_id=1, source_target_pairs={{0,64},{32,96},{64,0},{96,32},{1,65},{33,97},{65,1},{97,33},{2,66}... | collective-permute-start | bytes 516104 | tf_op jit(solution)/shard_map/ppermute | solution.py:35
  86.0 1.1 collective-permute-start.7
  87.1 0.2 select_reduce_fusion.2.source_ref
  87.3 46.4 %collective-permute-done.5 = bf16[4,56,384]{2,1,0:T(8,128)(2,1)S(1)} collective-permute-done((bf16[4,56,384]{2,1,0:T(8,128)(2,1)S(1)}, bf16[4,56,384]{2,1,0:T(8,128)(2,1)S(1)}, u32[]{:S(2)}, u32[]{:S(2)}) %collective-permute-start.5) | collective-permute-done | bytes 172064 | tf_op jit(solution)/shard_map/ppermute | solution.py:35
  133.7 7.4 %collective-permute-done.6 = bf16[4,56,384]{2,1,0:T(8,128)(2,1)S(1)} collective-permute-done((bf16[4,56,384]{2,1,0:T(8,128)(2,1)S(1)}, bf16[4,56,384]{2,1,0:T(8,128)(2,1)S(1)}, u32[]{:S(2)}, u32[]{:S(2)}) %collective-permute-start.6) | collective-permute-done | bytes 172064 | tf_op jit(solution)/shard_map/ppermute | solution.py:35
  141.2 2.6 %collective-permute-start.10 = (bf16[56,384]{1,0:T(8,128)(2,1)S(1)}, bf16[56,384]{1,0:T(8,128)(2,1)S(1)}, u32[]{:S(2)}, u32[]{:S(2)}) collective-permute-start(bf16[56,384]{1,0:T(8,128)(2,1)S(1)} %get-tuple-element.38), channel_id=1, source_target_pairs={{0,24},{8,0},{16,8},{24,16},{1,25},{9,1},{17,9},{25,17},{2,26},{10... | collective-permute-start | bytes 129032 | tf_op jit(solution)/shard_map/ppermute | solution.py:35
  143.9 1.3 collective-permute-start.9
  145.1 0.6 fusion.11
  145.7 2.7 %collective-permute-done.8 = bf16[56,384]{1,0:T(8,128)(2,1)S(1)} collective-permute-done((bf16[56,384]{1,0:T(8,128)(2,1)S(1)}, bf16[56,384]{1,0:T(8,128)(2,1)S(1)}, u32[]{:S(2)}, u32[]{:S(2)}) %collective-permute-start.8) | collective-permute-done | bytes 43040 | tf_op jit(solution)/shard_map/ppermute | solution.py:35
  148.5 0.5 slice.22
  149.0 0.7 reshape.66
  149.6 0.6 broadcast_in_dim.79
  150.3 5.8 %place.1 = bf16[4096,384]{1,0:T(8,128)(2,1)} custom-call(s32[16]{0:T(128)S(1)} %select_reduce_fusion.2.source_ref, s32[1]{0:T(128)} %bitcast.4.count_ref, f32[1]{0:T(128)} %bitcast.7.factor_ref, bf16[32,256,384]{2,1,0:T(8,128)(2,1)} %all-to-all-done.2.received_ref), custom_call_target="tpu_custom_call" | custom-call | tf_op jit(solution)/shard_map/place/pallas_call | solution.py:389
  (40 shorter events, 0.7 us)
Async XLA Ops:
  0.6 28.3 %copy-start.11 = (s32[8]{0:T(128)S(1)}, s32[8]{0:T(128)}, u32[]{:S(2)}) copy-start(s32[8]{0:T(128)} %valid_ref.5) | copy-start | bytes 100
  0.6 0.8 copy-start.8
  1.4 0.7 copy-start.9
  2.1 0.7 copy-start.10
  2.8 0.7 copy-start.12
  3.4 0.7 copy-start.14
  24.3 16.7 %copy-start.13 = (s32[8]{0:T(128)S(1)}, s32[8]{0:T(128)}, u32[]{:S(2)}) copy-start(s32[8]{0:T(128)} %owner_ref.3) | copy-start | bytes 100
  24.3 3.8 %collective-permute-start = (bf16[16,56,384]{2,1,0:T(8,128)(2,1)S(1)}, bf16[16,56,384]{2,1,0:T(8,128)(2,1)S(1)}, u32[]{:S(2)}, u32[]{:S(2)}) collective-permute-start(bf16[16,56,384]{2,1,0:T(8,128)(2,1)S(1)} %all_to_all.15.own_ref), channel_id=1, source_target_pairs={{0,4},{4,0},{1,5},{5,1},{2,6},{6,2},{3,7},{7,3},{8,12},{12,8},{9,1... | collective-permute-start | bytes 2064392 | tf_op jit(solution)/shard_map/ppermute | solution.py:30
  28.1 0.8 copy-start.6
  29.0 1.1 copy-start.7
  39.7 1.2 copy-start
  41.8 11.7 %all-to-all-start.1 = ((f32[32,1,32]{2,1,0:T(1,128)}), f32[32,1,32]{2,1,0:T(1,128)S(1)}, u32[]{:S(2)}, u32[]{:S(2)}) async-start(f32[32,1,32]{2,1,0:T(1,128)} %broadcast_in_dim.73), calls=%async_computation.1 | async-start | bytes 32768 | tf_op jit(solution)/shard_map/all_to_all | solution.py:344
  45.6 1.4 copy-start.1
  53.5 16.0 %copy-start.2 = (bf16[2048,384]{1,0:T(8,128)(2,1)S(1)}, bf16[2048,384]{1,0:T(8,128)(2,1)}, u32[]{:S(2)}) copy-start(bf16[2048,384]{1,0:T(8,128)(2,1)} %get-tuple-element.26.masked_ref) | copy-start | bytes 4718596
  53.5 96.8 %all-to-all-start.2 = ((bf16[32,256,384]{2,1,0:T(8,128)(2,1)}), bf16[32,256,384]{2,1,0:T(8,128)(2,1)}, u32[]{:S(2)}, u32[]{:S(2)}) async-start(bf16[32,256,384]{2,1,0:T(8,128)(2,1)} %get-tuple-element.25), calls=%async_computation.2 | async-start | bytes 12582912 | tf_op jit(solution)/shard_map/all_to_all | solution.py:360
  61.5 5.7 %collective-permute-start.1 = (f32[1,32]{1,0:T(1,128)S(1)}, f32[1,32]{1,0:T(1,128)S(1)}, u32[]{:S(2)}, u32[]{:S(2)}) collective-permute-start(f32[1,32]{1,0:T(1,128)S(1)} %bitcast.63), channel_id=1, source_target_pairs={{0,1},{1,2},{2,3},{3,0},{4,5},{5,6},{6,7},{7,4},{8,9},{9,10},{10,1... | collective-permute-start | bytes 392 | tf_op jit(solution)/shard_map/ppermute | solution.py:35
  63.2 4.6 %collective-permute-start.2 = (f32[1,32]{1,0:T(1,128)S(1)}, f32[1,32]{1,0:T(1,128)S(1)}, u32[]{:S(2)}, u32[]{:S(2)}) collective-permute-start(f32[1,32]{1,0:T(1,128)S(1)} %bitcast.64), channel_id=1, source_target_pairs={{0,2},{1,3},{2,0},{3,1},{4,6},{5,7},{6,4},{7,5},{8,10},{9,11},{10,... | collective-permute-start | bytes 392 | tf_op jit(solution)/shard_map/ppermute | solution.py:35
  66.5 2.8 %collective-permute-start.3 = (f32[1,32]{1,0:T(1,128)S(1)}, f32[1,32]{1,0:T(1,128)S(1)}, u32[]{:S(2)}, u32[]{:S(2)}) collective-permute-start(f32[1,32]{1,0:T(1,128)S(1)} %bitcast.65), channel_id=1, source_target_pairs={{0,3},{1,0},{2,1},{3,2},{4,7},{5,4},{6,5},{7,6},{8,11},{9,8},{10,9... | collective-permute-start | bytes 392 | tf_op jit(solution)/shard_map/ppermute | solution.py:35
  69.5 1.4 copy-start.3
  70.9 1.4 copy-start.4
  72.3 1.4 copy-start.5
  78.3 3.5 %collective-permute-start.4 = (bf16[4,4,56,384]{3,2,1,0:T(8,128)(2,1)S(1)}, bf16[4,4,56,384]{3,2,1,0:T(8,128)(2,1)S(1)}, u32[]{:S(2)}, u32[]{:S(2)}) collective-permute-start(bf16[4,4,56,384]{3,2,1,0:T(8,128)(2,1)S(1)} %dynamic-slice_bitcast_fusion), channel_id=1, source_target_pairs={{0,4},{4,0},{1,5},{5,1},{2,6},{6,2},{3,7},{7,3},{8,12},{12,8},{9,1... | collective-permute-start | bytes 2064392 | tf_op jit(solution)/shard_map/ppermute | solution.py:35
  82.0 51.6 %collective-permute-start.5 = (bf16[4,56,384]{2,1,0:T(8,128)(2,1)S(1)}, bf16[4,56,384]{2,1,0:T(8,128)(2,1)S(1)}, u32[]{:S(2)}, u32[]{:S(2)}) collective-permute-start(bf16[4,56,384]{2,1,0:T(8,128)(2,1)S(1)} %get-tuple-element.34), channel_id=1, source_target_pairs={{0,32},{32,64},{64,96},{96,0},{1,33},{33,65},{65,97},{97,1},{2,34}... | collective-permute-start | bytes 516104 | tf_op jit(solution)/shard_map/ppermute | solution.py:35
  83.5 57.5 %collective-permute-start.6 = (bf16[4,56,384]{2,1,0:T(8,128)(2,1)S(1)}, bf16[4,56,384]{2,1,0:T(8,128)(2,1)S(1)}, u32[]{:S(2)}, u32[]{:S(2)}) collective-permute-start(bf16[4,56,384]{2,1,0:T(8,128)(2,1)S(1)} %get-tuple-element.36), channel_id=1, source_target_pairs={{0,64},{32,96},{64,0},{96,32},{1,65},{33,97},{65,1},{97,33},{2,66}... | collective-permute-start | bytes 516104 | tf_op jit(solution)/shard_map/ppermute | solution.py:35
  86.0 55.1 %collective-permute-start.7 = (bf16[4,56,384]{2,1,0:T(8,128)(2,1)S(1)}, bf16[4,56,384]{2,1,0:T(8,128)(2,1)S(1)}, u32[]{:S(2)}, u32[]{:S(2)}) collective-permute-start(bf16[4,56,384]{2,1,0:T(8,128)(2,1)S(1)} %get-tuple-element.35), channel_id=1, source_target_pairs={{0,96},{32,0},{64,32},{96,64},{1,97},{33,1},{65,33},{97,65},{2,98}... | collective-permute-start | bytes 516104 | tf_op jit(solution)/shard_map/ppermute | solution.py:35
  141.2 4.5 %collective-permute-start.10 = (bf16[56,384]{1,0:T(8,128)(2,1)S(1)}, bf16[56,384]{1,0:T(8,128)(2,1)S(1)}, u32[]{:S(2)}, u32[]{:S(2)}) collective-permute-start(bf16[56,384]{1,0:T(8,128)(2,1)S(1)} %get-tuple-element.38), channel_id=1, source_target_pairs={{0,24},{8,0},{16,8},{24,16},{1,25},{9,1},{17,9},{25,17},{2,26},{10... | collective-permute-start | bytes 129032 | tf_op jit(solution)/shard_map/ppermute | solution.py:35
  143.9 4.5 %collective-permute-start.8 = (bf16[56,384]{1,0:T(8,128)(2,1)S(1)}, bf16[56,384]{1,0:T(8,128)(2,1)S(1)}, u32[]{:S(2)}, u32[]{:S(2)}) collective-permute-start(bf16[56,384]{1,0:T(8,128)(2,1)S(1)} %get-tuple-element.37), channel_id=1, source_target_pairs={{0,8},{8,16},{16,24},{24,0},{1,9},{9,17},{17,25},{25,1},{2,10},{10... | collective-permute-start | bytes 129032 | tf_op jit(solution)/shard_map/ppermute | solution.py:35
  143.9 4.5 %collective-permute-start.9 = (bf16[56,384]{1,0:T(8,128)(2,1)S(1)}, bf16[56,384]{1,0:T(8,128)(2,1)S(1)}, u32[]{:S(2)}, u32[]{:S(2)}) collective-permute-start(bf16[56,384]{1,0:T(8,128)(2,1)S(1)} %get-tuple-element.39), channel_id=1, source_target_pairs={{0,16},{8,24},{16,0},{24,8},{1,17},{9,25},{17,1},{25,9},{2,18},{10... | collective-permute-start | bytes 129032 | tf_op jit(solution)/shard_map/ppermute | solution.py:35

commit v3 on v2

--- a/solution.py
+++ b/solution.py
@@ -39,16 +39,17 @@
     return sum((turned(x, axis, r) for r in range(1, lax.axis_size(axis))), x)
 
 
-def scattered_sum(parts, axis, dim):
+def scattered(parts, axis, dim):
     count, index = lax.axis_size(axis), lax.axis_index(axis)
 
     def piece(shift):
         return lax.dynamic_index_in_dim(parts, (index + shift) % count, dim, keepdims=False)
 
-    total = piece(0).astype(F32)
-    for r in range(1, count):
-        total = total + turned(piece(r).astype(BF16), axis, r).astype(F32)
-    return total
+    return [piece(0)] + [turned(piece(r).astype(BF16), axis, r) for r in range(1, count)]
+
+
+def scattered_sum(parts, axis, dim):
+    return sum(piece.astype(F32) for piece in scattered(parts, axis, dim))
 
 
 def gate(value):
@@ -73,7 +74,20 @@
     return before.astype(BF16), after.astype(BF16)
 
 
-def pack_kernel(valid_ref, owner_ref, conv_ref, mid_ref, out_ref, copies_ref, stage_ref):
+def pack_kernel(
+    valid_hbm, owner_hbm, conv_hbm, mid_hbm, out_hbm,
+    copies_ref, valid_ref, owner_ref, conv_ref, mid_ref, out_ref, stage_ref, sems,
+):
+    sources = (valid_hbm, owner_hbm, conv_hbm, mid_hbm, out_hbm)
+    targets = (valid_ref, owner_ref, conv_ref, mid_ref, out_ref)
+    arrivals = [
+        pltpu.make_async_copy(source, target, sems.at[i])
+        for i, (source, target) in enumerate(zip(sources, targets))
+    ]
+    for copy in arrivals:
+        copy.start()
+    for copy in arrivals:
+        copy.wait()
     local = valid_ref.shape[0]
     lane = lax.broadcasted_iota(jnp.int32, (1, D), 1)
     extras = jnp.zeros((1, D), F32)
@@ -92,12 +106,16 @@
 
 
 def forward_kernel(
-    valid_ref, core_ref, feats_ref, own_ref, other_ref,
-    masked_out, low_out, mid_grad_out, mid_grad_ref, slope_ref, sums_ref, weights_ref, out_w_ref,
-    extras_ref, raw_ref, masked_ref, low_ref, wide_ref, sems, out_sems,
+    valid_ref, owner_ref, core_ref, feats_ref, own_hbm, other_ref,
+    masked_out, low_out, mid_grad_out, weights_out, state_ref, sums_ref, out_w_ref,
+    extras_ref, totals_ref, raw_ref, weights_ref, own_ref, masked_ref, low_ref, wide_ref,
+    sems, out_sems, weight_sems,
 ):
     local = valid_ref.shape[0]
     copies, departures = [], []
+    mid_grad_ref, slope_ref = state_ref.at[0], state_ref.at[1]
+    arrival = pltpu.make_async_copy(own_hbm, own_ref, weight_sems.at[0])
+    arrival.start()
 
     def send(source, target, rows, sem):
         copy = pltpu.make_async_copy(source.at[rows], target.at[rows], sem)
@@ -119,6 +137,8 @@
                 wide_ref[k, at : at + SHARD, :] = tile[SHARD * k : SHARD * (k + 1)]
             extras_ref[device : device + 1, :] = tile[EXTRA : EXTRA + 1, :128]
 
+    arrival.wait()
+
     @pl.when(core_ref[0] == 0)
     def _():
         unpack(0, own_ref)
@@ -130,16 +150,21 @@
         unpack(0, other_ref)
 
     weights_ref[...] = wide_ref[...].astype(BF16)
+    copy = pltpu.make_async_copy(weights_ref, weights_out, weight_sems.at[1])
+    copy.start()
+    departures.append(copy)
     devices = extras_ref.shape[0]
     column = lax.broadcasted_iota(jnp.int32, (128, D), 1).astype(F32)
     place = lax.broadcasted_iota(jnp.int32, (128, D), 0).astype(F32)
     home = jnp.floor((column + 0.5) * (1.0 / SHARD))
     pick = jnp.where(column - SHARD * home == place, 1.0, 0.0).astype(BF16)
     spread = jnp.dot(extras_ref[...].astype(BF16), pick, preferred_element_type=F32)
-    device = lax.broadcasted_iota(jnp.int32, (devices, D), 0).astype(F32)
-    out_w = jnp.sum(jnp.where(home[:devices] == device, spread, 0.0), 0, keepdims=True)
+    row = lax.broadcasted_iota(jnp.int32, (devices, D), 0).astype(F32)
+    out_w = jnp.sum(jnp.where(home[:devices] == row, spread, 0.0), 0, keepdims=True)
     out_w_ref[...] = out_w
 
+    lane = lax.broadcasted_iota(jnp.int32, (1, 128), 1)
+    totals = jnp.zeros((1, 128), F32)
     for j in range(0, local, GROUP):
         rows = pl.ds(j * BT, GROUP * BT)
         copies[j // GROUP].wait()
@@ -162,22 +187,35 @@
         for i in range(GROUP):
             block = jnp.sum(total[i * BT : (i + 1) * BT], 0, keepdims=True)
             sums_ref[j + i : j + i + 1, :] = block
+            block_sum = jnp.sum(block * out_w, 1, keepdims=True)
+            totals += jnp.where(lane == owner_ref[j + i], block_sum, 0.0)
         send(masked_ref, masked_out, rows, out_sems.at[0, j // GROUP])
         send(low_ref, low_out, rows, out_sems.at[1, j // GROUP])
         send(mid_grad_ref, mid_grad_out, rows, out_sems.at[2, j // GROUP])
+    for device in range(devices):
+        totals_ref[device] = totals
     for copy in departures:
         copy.wait()
 
 
 def backward_kernel(
-    valid_ref, owner_ref, mid_grad_ref, slope_ref, weights_ref, out_w_ref,
-    first_grad_out, slots_ref, first_grad_ref, ready_ref, sems, out_sems,
+    valid_ref, owner_ref, state_ref, weights_hbm, out_w_ref,
+    first_grad_out, slots_ref, weights_ref, first_grad_ref, ready_ref, sems, out_sems, weight_sems,
 ):
     local = valid_ref.shape[0]
+    arrivals = {}
+    for k in (3, 1, 0, 2):
+        arrivals[k] = pltpu.make_async_copy(
+            weights_hbm.at[k], weights_ref.at[k], weight_sems.at[k]
+        )
+        arrivals[k].start()
+    mid_grad_ref, slope_ref = state_ref.at[0], state_ref.at[1]
     copies = []
     for j in range(local):
         rows = pl.ds(j * BT, BT)
         keep = row_mask(valid_ref, j, 1)
+        if j == 0:
+            arrivals[3].wait()
         grad = lax.dot_general(
             mid_grad_ref[rows, :], weights_ref[3], OVER_LAST, preferred_element_type=F32
         )
@@ -190,6 +228,9 @@
         )
         copy.start()
         copies.append(copy)
+        if j == 0:
+            for k in (1, 0, 2):
+                arrivals[k].wait()
         total = lax.dot_general(low, weights_ref[1], OVER_LAST, preferred_element_type=F32)
         total += lax.dot_general(after, weights_ref[0], OVER_LAST, preferred_element_type=F32)
         total += lax.dot_general(before, weights_ref[2], OVER_LAST, preferred_element_type=F32)
@@ -244,6 +285,18 @@
         parts_ref[d] = stage_ref[...].astype(BF16)
 
 
+def finish_kernel(own_ref, first_ref, second_ref, third_ref, conv_ref, mid_ref, out_ref, total_ref):
+    total = own_ref[...]
+    for piece in (first_ref, second_ref, third_ref):
+        total += piece[...].astype(F32)
+    total_ref[...] = total * (1.0 / BT)
+    for row in range(3 * SHARD):
+        conv_ref[row] = total_ref[row : row + 1, :]
+    for row in range(SHARD):
+        mid_ref[row] = total_ref[3 * SHARD + row : 3 * SHARD + row + 1, :]
+    out_ref[...] = total_ref[EXTRA : EXTRA + 1, 0:SHARD]
+
+
 def place_kernel(
     source_ref, count_ref, factor_ref, received_ref, placed_ref, raw_ref, ready_ref, in_sems, out_sems
 ):
@@ -276,7 +329,7 @@
     return pltpu.with_memory_space_constraint(x, pltpu.VMEM)
 
 
-def call(kernel, name, in_specs, outs, scratch=()):
+def call(kernel, name, in_specs, outs, scratch=(), megabytes=0):
     return pl.pallas_call(
         kernel,
         in_specs=in_specs,
@@ -286,6 +339,9 @@
         ],
         scratch_shapes=list(scratch),
         compiler_params=pltpu.CompilerParams(vmem_limit_bytes=VMEM_LIMIT),
+        cost_estimate=pl.CostEstimate(
+            flops=0, transcendentals=0, bytes_accessed=megabytes * 1024 * 1024
+        ),
         name=name,
     )
 
@@ -303,63 +359,73 @@
     (copies,) = call(
         pack_kernel,
         "pack",
-        [IN_SMEM, IN_SMEM, IN_VMEM, IN_VMEM, IN_VMEM],
+        [IN_HBM] * 5,
         [(IN_VMEM, (chips, ROWS, D), BF16)],
-        [pltpu.VMEM((ROWS, D), F32)],
-    )(valid, owner_map, w_conv[0], w_mid[0], w_out)
+        [
+            pltpu.SMEM((local,), jnp.int32),
+            pltpu.SMEM((local,), jnp.int32),
+            pltpu.VMEM((3, SHARD, D), BF16),
+            pltpu.VMEM((SHARD, D), BF16),
+            pltpu.VMEM((1, SHARD), BF16),
+            pltpu.VMEM((ROWS, D), F32),
+            pltpu.SemaphoreType.DMA((5,)),
+        ],
+    )(*(in_hbm(x) for x in (valid, owner_map, w_conv[0], w_mid[0], w_out)))
     own = lax.all_to_all(copies, CHIPS, split_axis=0, concat_axis=0, tiled=True)
     other = swapped(own)
 
-    here = (IN_VMEM, (tokens_here, D), BF16)
     later = (IN_HBM, (tokens_here, D), BF16)
-    masked, low, mid_grad, mid_grad_here, slope, sums, weights, out_w, extras = call(
+    masked, low, mid_grad, weights, state, sums, out_w, extras, totals = call(
         forward_kernel,
         "forward",
-        [IN_SMEM, IN_SMEM, IN_HBM, IN_VMEM, IN_VMEM],
+        [IN_SMEM, IN_SMEM, IN_SMEM, IN_HBM, IN_HBM, IN_VMEM],
         [
             later,
             later,
             later,
-            here,
-            here,
+            (IN_HBM, (4, D, D), BF16),
+            (IN_VMEM, (2, tokens_here, D), BF16),
             (IN_VMEM, (local, D), F32),
-            (IN_VMEM, (4, D, D), BF16),
             (IN_VMEM, (1, D), F32),
             (IN_VMEM, (devices, 128), F32),
+            (IN_VMEM, (devices, 1, 128), F32),
         ],
         [
             pltpu.VMEM((tokens_here, D), BF16),
+            pltpu.VMEM((4, D, D), BF16),
+            pltpu.VMEM((chips, ROWS, D), BF16),
             pltpu.VMEM((tokens_here, D), BF16),
             pltpu.VMEM((tokens_here, D), BF16),
             pltpu.VMEM((4, D, D), F32),
             pltpu.SemaphoreType.DMA((local // GROUP,)),
             pltpu.SemaphoreType.DMA((3, local // GROUP)),
-        ],
-    )(valid, core, in_hbm(feats[0]), in_vmem(own), in_vmem(other))
-
-    members = (owner_map[:, None] == images[None, :]).astype(F32)
-    block_sums = jnp.sum(sums * out_w, 1)
-    totals = jnp.sum(block_sums[:, None] * members, 0)
-    totals = jnp.broadcast_to(totals[None, None, :], (devices, 1, devices))
+            pltpu.SemaphoreType.DMA((2,)),
+        ],
+    )(valid, owner_map, core, in_hbm(feats[0]), in_hbm(own), in_vmem(other))
+
     totals = lax.all_to_all(totals, DP, split_axis=0, concat_axis=0, tiled=True)
 
     first_grad, slots = call(
         backward_kernel,
         "backward",
-        [IN_SMEM, IN_SMEM, IN_VMEM, IN_VMEM, IN_VMEM, IN_VMEM],
+        [IN_SMEM, IN_SMEM, IN_VMEM, IN_HBM, IN_VMEM],
         [later, (IN_HBM, (devices, BT, D), BF16)],
         [
+            pltpu.VMEM((4, D, D), BF16),
             pltpu.VMEM((tokens_here, D), BF16),
             pltpu.VMEM((local, BT, D), BF16),
             pltpu.SemaphoreType.DMA((local,)),
             pltpu.SemaphoreType.DMA((local,)),
-        ],
-    )(valid, owner_map, in_vmem(mid_grad_here), in_vmem(slope), in_vmem(weights), out_w)
+            pltpu.SemaphoreType.DMA((4,)),
+        ],
+        megabytes=24,
+    )(valid, owner_map, in_vmem(state), in_hbm(weights), in_vmem(out_w))
 
     slots, totals = lax.optimization_barrier((slots, totals))
     received = lax.all_to_all(slots, DP, split_axis=0, concat_axis=0, tiled=True)
 
-    totals = total_over(jnp.sum(totals[:, 0, :], 0)[None], "head")[0]
+    totals = total_over(jnp.sum(totals[:, 0, :devices], 0)[None], "head")[0]
+    members = (owner_map[:, None] == images[None, :]).astype(F32)
     owners = extras[:, SHARD : SHARD + local].astype(jnp.int32)
     valids = extras[:, SHARD + local : SHARD + 2 * local]
     tokens = jnp.sum(jnp.where(owners[:, :, None] == images, valids[:, :, None], 0.0), (0, 1))
@@ -374,11 +440,13 @@
         [IN_SMEM, IN_VMEM, IN_VMEM, IN_VMEM, IN_VMEM, IN_VMEM],
         [(IN_VMEM, (devices, ROWS, D), BF16)],
         [pltpu.VMEM((3, D, D), F32), pltpu.VMEM((D, D), F32), pltpu.VMEM((ROWS, D), F32)],
+        megabytes=16,
     )(block_factor, masked, low, mid_grad, first_grad, sums)
     parts = parts.reshape(4, 4, 2, ROWS, D)
     parts = scattered_sum(parts, "dp_2", 2)
     parts = scattered_sum(parts, "dp_0", 0)
-    parts = scattered_sum(parts, "dp_1", 0) / (devices * local)
+    parts, received = lax.optimization_barrier((parts, received))
+    pieces = scattered(parts, "dp_1", 0)
 
     present = jnp.sum((owners == me).astype(jnp.int32), 1)
     rank = jnp.sum(jnp.where(images[None, :] < images[:, None], present[None, :], 0), 1)
@@ -397,14 +465,22 @@
             pltpu.SemaphoreType.DMA((capacity,)),
             pltpu.SemaphoreType.DMA((capacity,)),
         ],
+        megabytes=24,
     )(source, count.reshape(1), own_factor, received)
 
-    return (
-        placed[None],
-        parts[: 3 * SHARD].reshape(1, 3, SHARD, D),
-        parts[3 * SHARD : EXTRA][None],
-        parts[EXTRA, :SHARD][None],
-    )
+    conv, mid, out = pl.pallas_call(
+        finish_kernel,
+        in_specs=[IN_VMEM] * 4,
+        out_specs=[IN_VMEM] * 3,
+        out_shape=[
+            jax.ShapeDtypeStruct((3 * SHARD, 1, D), F32),
+            jax.ShapeDtypeStruct((SHARD, 1, D), F32),
+            jax.ShapeDtypeStruct((1, SHARD), F32),
+        ],
+        scratch_shapes=[pltpu.VMEM((ROWS, D), F32)],
+        name="finish",
+    )(*(in_vmem(x) for x in pieces))
+    return placed[None], conv.reshape(1, 3, SHARD, D), mid.reshape(1, SHARD, D), out
 
 
 def solution(mesh):

time: 158 us -> 149 us (0.943)
  local copies, waits for them, and re-layouts: 14.8 us -> 6.36 us
  Pallas kernels: 27 us -> 31.2 us
  waiting for transfers between devices: 60.6 us -> 58.4 us
    unnamed x30 -> x18, local copies, waits for them, and re-layouts: 12.2 us -> 6.18 us
    pallas_call x3 -> x4, Pallas kernels: 16.7 us -> 20.5 us  [the longest x1 11.4 us: per_device(): call(forward_kernel, 'forward', [IN_SMEM, IN_SMEM, IN_SMEM, IN_HBM, IN_HB...]
    ppermute x10, waiting for transfers between devices: 58.8 us -> 56.6 us  [turned(): lax.ppermute(x, axis, [(i, (i + shift) % count) for i in range(count)])]
  transfers between devices with their start and end apart: 13 -> 13, of which waited for: 7 -> 5; matrix products, arithmetic and copies ran while one was open for 3% -> 2% of each run, Pallas kernels for 7% -> 12%
where the time goes in v3:
time: 149 us; the launch traced here: 148 us
  waiting for transfers between devices  58.4 us (39%)
  Pallas kernels  31.2 us (21%)
  starting transfers between devices  28.6 us (19%)
  blocking collectives  19.6 us (13%)
  local copies, waits for them, and re-layouts  6.36 us (4%)
  other arithmetic  2.38 us (2%)
  between operations  1.5 us (1%)
    ppermute x10, waiting for transfers between devices, turned(): lax.ppermute(x, axis, [(i, (i + shift) % count) for i in range(count)])  56.6 us
    all_to_all x1, blocking collectives, per_device(): own = lax.all_to_all(copies, CHIPS, split_axis=0, concat_axis=0, tiled=True)  19.6 us
    ppermute x10, starting transfers between devices, turned(): lax.ppermute(x, axis, [(i, (i + shift) % count) for i in range(count)])  15 us
    pallas_call x1, Pallas kernels, per_device(): call(forward_kernel, 'forward', [IN_SMEM, IN_SMEM, IN_SMEM, IN_HBM, IN_HB...  11.4 us
    all_to_all x1, starting transfers between devices, per_device(): lax.all_to_all(slots, DP, split_axis=0, concat_axis=0, tiled=True)  7.67 us
    pallas_call x1, Pallas kernels, per_device(): call(backward_kernel, 'backward', [IN_SMEM, IN_SMEM, IN_VMEM, IN_HBM, IN_...  7.5 us
    pallas_call x1, Pallas kernels, per_device(): call(place_kernel, 'place', [IN_SMEM, IN_SMEM, IN_SMEM, IN_HBM], [(IN_HBM...  6.24 us
    unnamed x18, local copies, waits for them, and re-layouts  6.18 us
  transfers between devices with their start and end apart: 13, of which 5 were waited for; matrix products, arithmetic and copies ran while one was open for 2% of the time, Pallas kernels for 12%

profile of v3, /device:TPU:1, one launch (start us, length us, event | category | flops | bytes accessed | tf_op | source)
XLA Modules:
  0.0 148.0 jit_solution(332898825123867266)
XLA Ops:
  0.7 0.9 pack.1
  1.6 19.6 %all_to_all.15.own_hbm = bf16[16,56,384]{2,1,0:T(8,128)(2,1)S(1)} all-to-all(bf16[16,56,384]{2,1,0:T(8,128)(2,1)S(1)} %pack.1), channel_id=1, replica_groups=mesh['dp_0'=4,'dp_1'=4,'dp_2'=2,'head'=4] {'dp_0','dp_1'}, dimensions={0} | all-to-all | bytes 1376256 | tf_op jit(solution)/shard_map/all_to_all | solution.py:374
  21.2 2.0 %collective-permute-start = (bf16[16,56,384]{2,1,0:T(8,128)(2,1)S(1)}, bf16[16,56,384]{2,1,0:T(8,128)(2,1)S(1)}, u32[]{:S(2)}, u32[]{:S(2)}) collective-permute-start(bf16[16,56,384]{2,1,0:T(8,128)(2,1)S(1)} %all_to_all.15.own_hbm), channel_id=1, source_target_pairs={{0,4},{4,0},{1,5},{5,1},{2,6},{6,2},{3,7},{7,3},{8,12},{12,8},{9,1... | collective-permute-start | bytes 2064392 | tf_op jit(solution)/shard_map/ppermute | solution.py:30
  23.2 1.8 %collective-permute-done.other_ref = bf16[16,56,384]{2,1,0:T(8,128)(2,1)S(1)} collective-permute-done((bf16[16,56,384]{2,1,0:T(8,128)(2,1)S(1)}, bf16[16,56,384]{2,1,0:T(8,128)(2,1)S(1)}, u32[]{:S(2)}, u32[]{:S(2)}) %collective-permute-start) | collective-permute-done | bytes 688160 | tf_op jit(solution)/shard_map/ppermute | solution.py:30
  25.0 0.8 copy-done.4
  25.8 1.1 copy-done.5
  26.9 11.4 %forward.1 = (bf16[2048,384]{1,0:T(8,128)(2,1)}, bf16[2048,384]{1,0:T(8,128)(2,1)}, bf16[2048,384]{1,0:T(8,128)(2,1)}, bf16[4,384,384]{2,1,0:T(8,128)(2,1)}, bf1...) custom-call(s32[8]{0:T(128)S(1)} %copy-done.6, ...), custom_call_target="tpu_custom_call" | custom-call | tf_op jit(solution)/shard_map/forward/pallas_call | solution.py:378
  38.3 3.9 %all-to-all-start.1 = ((f32[32,1,128]{2,1,0:T(1,128)}), f32[32,1,128]{2,1,0:T(1,128)S(1)}, u32[]{:S(2)}, u32[]{:S(2)}) async-start(f32[32,1,128]{2,1,0:T(1,128)} %get-tuple-element.27), calls=%async_computation.1 | async-start | bytes 32768 | tf_op jit(solution)/shard_map/all_to_all | solution.py:406
  42.2 7.5 %backward.1 = (bf16[2048,384]{1,0:T(8,128)(2,1)}, bf16[32,256,384]{2,1,0:T(8,128)(2,1)}) custom-call(s32[8]{0:T(128)S(1)} %copy-done.6, s32[8]{0:T(128)S(1)} %copy-done.7, bf16[2,2048,384]{2,1,0:T(8,128)(2,1)S(1)} %get-tuple-element.23.state_ref, bf16[4,384,384]{2,1,0:T(8,128)(2,1)} %get-tuple-element.24.weights_hbm, f32[1,384]{1,0:T(1,128)S(1)} %get-tuple-element.25.out_w_ref), custom_call_target="tpu_custom_call" | custom-call | bytes 25165824 | tf_op jit(solution)/shard_map/backward/pallas_call | solution.py:408
  49.7 0.0 copy-start
  49.7 7.7 %all-to-all-start.2 = ((bf16[32,256,384]{2,1,0:T(8,128)(2,1)}), bf16[32,256,384]{2,1,0:T(8,128)(2,1)}, u32[]{:S(2)}, u32[]{:S(2)}) async-start(bf16[32,256,384]{2,1,0:T(8,128)(2,1)} %get-tuple-element.34), calls=%async_computation.2 | async-start | bytes 12582912 | tf_op jit(solution)/shard_map/all_to_all | solution.py:425
  57.4 0.1 slice_convert_fusion
  57.5 0.2 select_reduce_fusion
  57.7 0.1 slice_reduce_fusion
  57.7 3.8 %collective-permute-start.3 = (f32[1,32]{1,0:T(1,128)S(1)}, f32[1,32]{1,0:T(1,128)S(1)}, u32[]{:S(2)}, u32[]{:S(2)}) collective-permute-start(f32[1,32]{1,0:T(1,128)S(1)} %bitcast.59), channel_id=1, source_target_pairs={{0,3},{1,0},{2,1},{3,2},{4,7},{5,4},{6,5},{7,6},{8,11},{9,8},{10,9... | collective-permute-start | bytes 392 | tf_op jit(solution)/shard_map/ppermute | solution.py:35
  61.5 0.7 collective-permute-start.1
  62.2 0.0 collective-permute-done.3
  62.3 3.6 %collective-permute-done.2 = f32[1,32]{1,0:T(1,128)S(1)} collective-permute-done((f32[1,32]{1,0:T(1,128)S(1)}, f32[1,32]{1,0:T(1,128)S(1)}, u32[]{:S(2)}, u32[]{:S(2)}) %collective-permute-start.2) | collective-permute-done | bytes 160 | tf_op jit(solution)/shard_map/ppermute | solution.py:35
  65.8 0.0 collective-permute-done.1
  65.9 0.2 select_reduce_fusion.3.factor_ref
  66.1 1.4 copy-done.1
  67.5 1.4 copy-done.2
  68.9 1.4 copy-done.3
  70.3 4.5 %weight_grads.1 = bf16[32,56,384]{2,1,0:T(8,128)(2,1)S(1)} custom-call(f32[8]{0:T(128)S(1)} %select_reduce_fusion.3.factor_ref, bf16[2048,384]{1,0:T(8,128)(2,1)S(1)} %copy-done, bf16[2048,384]{1,0:T(8,128)(2,1)S(1)} %copy-done.1, bf16[2048,384]{1,0:T(8,128)(2,1)S(1)} %copy-done.2, bf16[2048,384]{1,0:T(8,128)(2,1)S(1)} %copy-done.3, ...), custom_call_target="tpu_custom_call" | custom-call | bytes 16777216 | tf_op jit(solution)/shard_map/weight_grads/pallas_call | solution.py:437
  74.8 0.1 dynamic-slice_bitcast_fusion
  74.9 1.4 collective-permute-start.4
  76.3 0.7 convert_reduce_fusion
  77.6 0.1 select_reduce_fusion.1
  77.8 0.3 collective-permute-done.4
  78.0 0.2 convert_add_fusion
  78.2 0.1 fusion.2
  78.3 2.8 %collective-permute-start.7 = (bf16[4,56,384]{2,1,0:T(8,128)(2,1)S(1)}, bf16[4,56,384]{2,1,0:T(8,128)(2,1)S(1)}, u32[]{:S(2)}, u32[]{:S(2)}) collective-permute-start(bf16[4,56,384]{2,1,0:T(8,128)(2,1)S(1)} %get-tuple-element.45), channel_id=1, source_target_pairs={{0,96},{32,0},{64,32},{96,64},{1,97},{33,1},{65,33},{97,65},{2,98}... | collective-permute-start | bytes 516104 | tf_op jit(solution)/shard_map/ppermute | solution.py:35
  81.1 0.5 collective-permute-start.6
  81.6 0.6 collective-permute-start.5
  82.2 0.2 select_reduce_fusion.2.source_ref
  82.4 0.6 fusion.8
  83.0 49.8 %collective-permute-done.7 = bf16[4,56,384]{2,1,0:T(8,128)(2,1)S(1)} collective-permute-done((bf16[4,56,384]{2,1,0:T(8,128)(2,1)S(1)}, bf16[4,56,384]{2,1,0:T(8,128)(2,1)S(1)}, u32[]{:S(2)}, u32[]{:S(2)}) %collective-permute-start.7) | collective-permute-done | bytes 172064 | tf_op jit(solution)/shard_map/ppermute | solution.py:35
  132.8 0.0 collective-permute-done.6
  132.8 2.9 %collective-permute-done.5 = bf16[4,56,384]{2,1,0:T(8,128)(2,1)S(1)} collective-permute-done((bf16[4,56,384]{2,1,0:T(8,128)(2,1)S(1)}, bf16[4,56,384]{2,1,0:T(8,128)(2,1)S(1)}, u32[]{:S(2)}, u32[]{:S(2)}) %collective-permute-start.5) | collective-permute-done | bytes 172064 | tf_op jit(solution)/shard_map/ppermute | solution.py:35
  135.7 0.1 fusion.1
  135.8 0.0 all-to-all-done.2.received_ref
  135.8 1.3 collective-permute-start.8
  137.1 2.4 %collective-permute-start.9 = (bf16[56,384]{1,0:T(8,128)(2,1)S(1)}, bf16[56,384]{1,0:T(8,128)(2,1)S(1)}, u32[]{:S(2)}, u32[]{:S(2)}) collective-permute-start(bf16[56,384]{1,0:T(8,128)(2,1)S(1)} %get-tuple-element.48), channel_id=1, source_target_pairs={{0,16},{8,24},{16,0},{24,8},{1,17},{9,25},{17,1},{25,9},{2,18},{10... | collective-permute-start | bytes 129032 | tf_op jit(solution)/shard_map/ppermute | solution.py:35
  139.5 1.6 %collective-permute-start.10 = (bf16[56,384]{1,0:T(8,128)(2,1)S(1)}, bf16[56,384]{1,0:T(8,128)(2,1)S(1)}, u32[]{:S(2)}, u32[]{:S(2)}) collective-permute-start(bf16[56,384]{1,0:T(8,128)(2,1)S(1)} %get-tuple-element.47), channel_id=1, source_target_pairs={{0,24},{8,0},{16,8},{24,16},{1,25},{9,1},{17,9},{25,17},{2,26},{10... | collective-permute-start | bytes 129032 | tf_op jit(solution)/shard_map/ppermute | solution.py:35
  141.1 6.2 %place.1 = bf16[4096,384]{1,0:T(8,128)(2,1)} custom-call(s32[16]{0:T(128)S(1)} %select_reduce_fusion.2.source_ref, s32[1]{0:T(128)} %bitcast.4.count_ref, f32[1]{0:T(128)} %bitcast.7.factor_ref, bf16[32,256,384]{2,1,0:T(8,128)(2,1)} %all-to-all-done.2.received_ref), custom_call_target="tpu_custom_call" | custom-call | bytes 25165824 | tf_op jit(solution)/shard_map/place/pallas_call | solution.py:457
  147.3 0.0 collective-permute-done.9.second_ref
  147.3 0.0 collective-permute-done.10.third_ref
  147.3 0.7 finish.1
  (20 shorter events, 0.1 us)
Async XLA Ops:
  0.6 25.2 %copy-start.6 = (s32[8]{0:T(128)S(1)}, s32[8]{0:T(128)}, u32[]{:S(2)}) copy-start(s32[8]{0:T(128)} %valid_ref.3) | copy-start | bytes 100
  0.6 25.2 %copy-start.7 = (s32[8]{0:T(128)S(1)}, s32[8]{0:T(128)}, u32[]{:S(2)}) copy-start(s32[8]{0:T(128)} %owner_ref.3) | copy-start | bytes 100
  21.2 4.7 %copy-start.8 = (bf16[16,56,384]{2,1,0:T(8,128)(2,1)}, bf16[16,56,384]{2,1,0:T(8,128)(2,1)S(1)}, u32[]{:S(2)}) copy-start(bf16[16,56,384]{2,1,0:T(8,128)(2,1)S(1)} %all_to_all.15.own_hbm) | copy-start | bytes 2064388
  21.2 3.8 %collective-permute-start = (bf16[16,56,384]{2,1,0:T(8,128)(2,1)S(1)}, bf16[16,56,384]{2,1,0:T(8,128)(2,1)S(1)}, u32[]{:S(2)}, u32[]{:S(2)}) collective-permute-start(bf16[16,56,384]{2,1,0:T(8,128)(2,1)S(1)} %all_to_all.15.own_hbm), channel_id=1, source_target_pairs={{0,4},{4,0},{1,5},{5,1},{2,6},{6,2},{3,7},{7,3},{8,12},{12,8},{9,1... | collective-permute-start | bytes 2064392 | tf_op jit(solution)/shard_map/ppermute | solution.py:30
  25.0 0.8 copy-start.4
  25.8 1.1 copy-start.5
  38.3 11.4 %all-to-all-start.1 = ((f32[32,1,128]{2,1,0:T(1,128)}), f32[32,1,128]{2,1,0:T(1,128)S(1)}, u32[]{:S(2)}, u32[]{:S(2)}) async-start(f32[32,1,128]{2,1,0:T(1,128)} %get-tuple-element.27), calls=%async_computation.1 | async-start | bytes 32768 | tf_op jit(solution)/shard_map/all_to_all | solution.py:406
  49.7 16.3 %copy-start = (bf16[2048,384]{1,0:T(8,128)(2,1)S(1)}, bf16[2048,384]{1,0:T(8,128)(2,1)}, u32[]{:S(2)}) copy-start(bf16[2048,384]{1,0:T(8,128)(2,1)} %get-tuple-element.29.masked_ref) | copy-start | bytes 4718596
  49.7 86.0 %all-to-all-start.2 = ((bf16[32,256,384]{2,1,0:T(8,128)(2,1)}), bf16[32,256,384]{2,1,0:T(8,128)(2,1)}, u32[]{:S(2)}, u32[]{:S(2)}) async-start(bf16[32,256,384]{2,1,0:T(8,128)(2,1)} %get-tuple-element.34), calls=%async_computation.2 | async-start | bytes 12582912 | tf_op jit(solution)/shard_map/all_to_all | solution.py:425
  57.7 4.5 %collective-permute-start.3 = (f32[1,32]{1,0:T(1,128)S(1)}, f32[1,32]{1,0:T(1,128)S(1)}, u32[]{:S(2)}, u32[]{:S(2)}) collective-permute-start(f32[1,32]{1,0:T(1,128)S(1)} %bitcast.59), channel_id=1, source_target_pairs={{0,3},{1,0},{2,1},{3,2},{4,7},{5,4},{6,5},{7,6},{8,11},{9,8},{10,9... | collective-permute-start | bytes 392 | tf_op jit(solution)/shard_map/ppermute | solution.py:35
  61.5 4.3 %collective-permute-start.2 = (f32[1,32]{1,0:T(1,128)S(1)}, f32[1,32]{1,0:T(1,128)S(1)}, u32[]{:S(2)}, u32[]{:S(2)}) collective-permute-start(f32[1,32]{1,0:T(1,128)S(1)} %bitcast.60), channel_id=1, source_target_pairs={{0,2},{1,3},{2,0},{3,1},{4,6},{5,7},{6,4},{7,5},{8,10},{9,11},{10,... | collective-permute-start | bytes 392 | tf_op jit(solution)/shard_map/ppermute | solution.py:35
  61.5 4.3 %collective-permute-start.1 = (f32[1,32]{1,0:T(1,128)S(1)}, f32[1,32]{1,0:T(1,128)S(1)}, u32[]{:S(2)}, u32[]{:S(2)}) collective-permute-start(f32[1,32]{1,0:T(1,128)S(1)} %bitcast.61), channel_id=1, source_target_pairs={{0,1},{1,2},{2,3},{3,0},{4,5},{5,6},{6,7},{7,4},{8,9},{9,10},{10,1... | collective-permute-start | bytes 392 | tf_op jit(solution)/shard_map/ppermute | solution.py:35
  66.1 1.4 copy-start.1
  67.5 1.4 copy-start.2
  68.9 1.4 copy-start.3
  74.9 3.2 %collective-permute-start.4 = (bf16[4,4,56,384]{3,2,1,0:T(8,128)(2,1)S(1)}, bf16[4,4,56,384]{3,2,1,0:T(8,128)(2,1)S(1)}, u32[]{:S(2)}, u32[]{:S(2)}) collective-permute-start(bf16[4,4,56,384]{3,2,1,0:T(8,128)(2,1)S(1)} %dynamic-slice_bitcast_fusion), channel_id=1, source_target_pairs={{0,4},{4,0},{1,5},{5,1},{2,6},{6,2},{3,7},{7,3},{8,12},{12,8},{9,1... | collective-permute-start | bytes 2064392 | tf_op jit(solution)/shard_map/ppermute | solution.py:35
  78.3 54.5 %collective-permute-start.7 = (bf16[4,56,384]{2,1,0:T(8,128)(2,1)S(1)}, bf16[4,56,384]{2,1,0:T(8,128)(2,1)S(1)}, u32[]{:S(2)}, u32[]{:S(2)}) collective-permute-start(bf16[4,56,384]{2,1,0:T(8,128)(2,1)S(1)} %get-tuple-element.45), channel_id=1, source_target_pairs={{0,96},{32,0},{64,32},{96,64},{1,97},{33,1},{65,33},{97,65},{2,98}... | collective-permute-start | bytes 516104 | tf_op jit(solution)/shard_map/ppermute | solution.py:35
  81.1 51.7 %collective-permute-start.6 = (bf16[4,56,384]{2,1,0:T(8,128)(2,1)S(1)}, bf16[4,56,384]{2,1,0:T(8,128)(2,1)S(1)}, u32[]{:S(2)}, u32[]{:S(2)}) collective-permute-start(bf16[4,56,384]{2,1,0:T(8,128)(2,1)S(1)} %get-tuple-element.46), channel_id=1, source_target_pairs={{0,64},{32,96},{64,0},{96,32},{1,65},{33,97},{65,1},{97,33},{2,66}... | collective-permute-start | bytes 516104 | tf_op jit(solution)/shard_map/ppermute | solution.py:35
  81.6 54.1 %collective-permute-start.5 = (bf16[4,56,384]{2,1,0:T(8,128)(2,1)S(1)}, bf16[4,56,384]{2,1,0:T(8,128)(2,1)S(1)}, u32[]{:S(2)}, u32[]{:S(2)}) collective-permute-start(bf16[4,56,384]{2,1,0:T(8,128)(2,1)S(1)} %get-tuple-element.44), channel_id=1, source_target_pairs={{0,32},{32,64},{64,96},{96,0},{1,33},{33,65},{65,97},{97,1},{2,34}... | collective-permute-start | bytes 516104 | tf_op jit(solution)/shard_map/ppermute | solution.py:35
  135.8 11.5 %collective-permute-start.8 = (bf16[56,384]{1,0:T(8,128)(2,1)S(1)}, bf16[56,384]{1,0:T(8,128)(2,1)S(1)}, u32[]{:S(2)}, u32[]{:S(2)}) collective-permute-start(bf16[56,384]{1,0:T(8,128)(2,1)S(1)} %get-tuple-element.49), channel_id=1, source_target_pairs={{0,8},{8,16},{16,24},{24,0},{1,9},{9,17},{17,25},{25,1},{2,10},{10... | collective-permute-start | bytes 129032 | tf_op jit(solution)/shard_map/ppermute | solution.py:35
  137.1 10.2 %collective-permute-start.9 = (bf16[56,384]{1,0:T(8,128)(2,1)S(1)}, bf16[56,384]{1,0:T(8,128)(2,1)S(1)}, u32[]{:S(2)}, u32[]{:S(2)}) collective-permute-start(bf16[56,384]{1,0:T(8,128)(2,1)S(1)} %get-tuple-element.48), channel_id=1, source_target_pairs={{0,16},{8,24},{16,0},{24,8},{1,17},{9,25},{17,1},{25,9},{2,18},{10... | collective-permute-start | bytes 129032 | tf_op jit(solution)/shard_map/ppermute | solution.py:35
  139.5 7.8 %collective-permute-start.10 = (bf16[56,384]{1,0:T(8,128)(2,1)S(1)}, bf16[56,384]{1,0:T(8,128)(2,1)S(1)}, u32[]{:S(2)}, u32[]{:S(2)}) collective-permute-start(bf16[56,384]{1,0:T(8,128)(2,1)S(1)} %get-tuple-element.47), channel_id=1, source_target_pairs={{0,24},{8,0},{16,8},{24,16},{1,25},{9,1},{17,9},{25,17},{2,26},{10... | collective-permute-start | bytes 129032 | tf_op jit(solution)/shard_map/ppermute | solution.py:35

commit v4 on v3

--- a/solution.py
+++ b/solution.py
@@ -66,12 +66,15 @@
     return rows < limit
 
 
-def neighbours(x):
+def neighbours(x, place, last):
     count = x.shape[0]
-    place = lax.broadcasted_iota(jnp.int32, (count, 1), 0) % BT
     before = jnp.where(place == 0, 0.0, pltpu.roll(x, 1, 0))
-    after = jnp.where(place == BT - 1, 0.0, pltpu.roll(x, count - 1, 0))
+    after = jnp.where(place == last, 0.0, pltpu.roll(x, count - 1, 0))
     return before.astype(BF16), after.astype(BF16)
+
+
+def block_place(count):
+    return lax.broadcasted_iota(jnp.int32, (count, 1), 0) % BT
 
 
 def pack_kernel(
@@ -105,28 +108,33 @@
         copies_ref[j] = packed
 
 
+def state_rows(local):
+    tokens = local * BT
+    return pl.ds(0, tokens), pl.ds(tokens, 4 * D)
+
+
+def weight(ref, k):
+    return ref[k * D : (k + 1) * D, :]
+
+
 def forward_kernel(
-    valid_ref, owner_ref, core_ref, feats_ref, own_hbm, other_ref,
-    masked_out, low_out, mid_grad_out, weights_out, state_ref, sums_ref, out_w_ref,
-    extras_ref, totals_ref, raw_ref, weights_ref, own_ref, masked_ref, low_ref, wide_ref,
-    sems, out_sems, weight_sems,
+    valid_ref, owner_ref, core_ref, feats_ref, own_hbm, other_hbm,
+    low_out, mid_grad_out, state_ref, sums_ref, out_w_ref, extras_ref, totals_ref,
+    raw_ref, own_ref, other_ref, low_ref, mid_grad_ref, wide_ref, sems, out_sems, weight_sems,
 ):
     local = valid_ref.shape[0]
-    copies, departures = [], []
-    mid_grad_ref, slope_ref = state_ref.at[0], state_ref.at[1]
-    arrival = pltpu.make_async_copy(own_hbm, own_ref, weight_sems.at[0])
-    arrival.start()
-
-    def send(source, target, rows, sem):
-        copy = pltpu.make_async_copy(source.at[rows], target.at[rows], sem)
-        copy.start()
-        departures.append(copy)
-
+    slope_ref, weights_ref = (state_ref.at[rows] for rows in state_rows(local))
+    arrivals = [
+        pltpu.make_async_copy(own_hbm, own_ref, weight_sems.at[0]),
+        pltpu.make_async_copy(other_hbm, other_ref, weight_sems.at[1]),
+    ]
     for j in range(0, local, GROUP):
         rows = pl.ds(j * BT, GROUP * BT)
-        copy = pltpu.make_async_copy(feats_ref.at[rows], raw_ref.at[rows], sems.at[j // GROUP])
-        copy.start()
-        copies.append(copy)
+        arrivals.append(
+            pltpu.make_async_copy(feats_ref.at[rows], raw_ref.at[rows], sems.at[j // GROUP])
+        )
+    for copy in arrivals:
+        copy.start()
 
     def unpack(parity, source):
         for chip in range(source.shape[0]):
@@ -134,10 +142,11 @@
             device = 2 * chip + parity
             at = SHARD * device
             for k in range(4):
-                wide_ref[k, at : at + SHARD, :] = tile[SHARD * k : SHARD * (k + 1)]
+                wide_ref[k * D + at : k * D + at + SHARD, :] = tile[SHARD * k : SHARD * (k + 1)]
             extras_ref[device : device + 1, :] = tile[EXTRA : EXTRA + 1, :128]
 
-    arrival.wait()
+    for copy in arrivals[:2]:
+        copy.wait()
 
     @pl.when(core_ref[0] == 0)
     def _():
@@ -150,9 +159,6 @@
         unpack(0, other_ref)
 
     weights_ref[...] = wide_ref[...].astype(BF16)
-    copy = pltpu.make_async_copy(weights_ref, weights_out, weight_sems.at[1])
-    copy.start()
-    departures.append(copy)
     devices = extras_ref.shape[0]
     column = lax.broadcasted_iota(jnp.int32, (128, D), 1).astype(F32)
     place = lax.broadcasted_iota(jnp.int32, (128, D), 0).astype(F32)
@@ -165,33 +171,40 @@
 
     lane = lax.broadcasted_iota(jnp.int32, (1, 128), 1)
     totals = jnp.zeros((1, 128), F32)
+    place = block_place(GROUP * BT)
+    departures = []
     for j in range(0, local, GROUP):
         rows = pl.ds(j * BT, GROUP * BT)
-        copies[j // GROUP].wait()
+        arrivals[2 + j // GROUP].wait()
         keep = row_mask(valid_ref, j, GROUP)
         masked = jnp.where(keep, raw_ref[rows, :].astype(F32), 0.0)
-        before, after = neighbours(masked)
-        masked = masked.astype(BF16)
-        masked_ref[rows, :] = masked
-        first = jnp.dot(before, weights_ref[0], preferred_element_type=F32)
-        first += jnp.dot(masked, weights_ref[1], preferred_element_type=F32)
-        first += jnp.dot(after, weights_ref[2], preferred_element_type=F32)
+        before, after = neighbours(masked, place, BT - 1)
+        first = jnp.dot(before, weight(weights_ref, 0), preferred_element_type=F32)
+        first += jnp.dot(
+            masked.astype(BF16), weight(weights_ref, 1), preferred_element_type=F32
+        )
+        first += jnp.dot(after, weight(weights_ref, 2), preferred_element_type=F32)
         first_act, slope = gate(first)
         low = first_act.astype(BF16)
         low_ref[rows, :] = low
+        copy = pltpu.make_async_copy(low_ref.at[rows], low_out.at[rows], out_sems.at[0, j // GROUP])
+        copy.start()
+        departures.append(copy)
         slope_ref[rows, :] = slope.astype(BF16)
-        second = jnp.dot(low, weights_ref[3], preferred_element_type=F32)
+        second = jnp.dot(low, weight(weights_ref, 3), preferred_element_type=F32)
         second_act, second_slope = gate(second)
         mid_grad_ref[rows, :] = jnp.where(keep, out_w * second_slope, 0.0).astype(BF16)
+        copy = pltpu.make_async_copy(
+            mid_grad_ref.at[rows], mid_grad_out.at[rows], out_sems.at[1, j // GROUP]
+        )
+        copy.start()
+        departures.append(copy)
         total = jnp.where(keep, second_act + first_act, 0.0)
         for i in range(GROUP):
             block = jnp.sum(total[i * BT : (i + 1) * BT], 0, keepdims=True)
             sums_ref[j + i : j + i + 1, :] = block
             block_sum = jnp.sum(block * out_w, 1, keepdims=True)
             totals += jnp.where(lane == owner_ref[j + i], block_sum, 0.0)
-        send(masked_ref, masked_out, rows, out_sems.at[0, j // GROUP])
-        send(low_ref, low_out, rows, out_sems.at[1, j // GROUP])
-        send(mid_grad_ref, mid_grad_out, rows, out_sems.at[2, j // GROUP])
     for device in range(devices):
         totals_ref[device] = totals
     for copy in departures:
@@ -199,43 +212,49 @@
 
 
 def backward_kernel(
-    valid_ref, owner_ref, state_ref, weights_hbm, out_w_ref,
-    first_grad_out, slots_ref, weights_ref, first_grad_ref, ready_ref, sems, out_sems, weight_sems,
+    valid_ref, owner_ref, mid_grad_hbm, state_ref, out_w_ref,
+    first_grad_out, slots_ref, mid_grad_ref, first_grad_ref, ready_ref, sems, out_sems, in_sems,
 ):
     local = valid_ref.shape[0]
-    arrivals = {}
-    for k in (3, 1, 0, 2):
-        arrivals[k] = pltpu.make_async_copy(
-            weights_hbm.at[k], weights_ref.at[k], weight_sems.at[k]
-        )
-        arrivals[k].start()
-    mid_grad_ref, slope_ref = state_ref.at[0], state_ref.at[1]
-    copies = []
-    for j in range(local):
-        rows = pl.ds(j * BT, BT)
-        keep = row_mask(valid_ref, j, 1)
-        if j == 0:
-            arrivals[3].wait()
+    slope_ref, weights_ref = (state_ref.at[rows] for rows in state_rows(local))
+    place = block_place(GROUP * BT)
+    arrivals, copies = [], []
+    for j in range(0, local, GROUP):
+        rows = pl.ds(j * BT, GROUP * BT)
+        copy = pltpu.make_async_copy(
+            mid_grad_hbm.at[rows], mid_grad_ref.at[rows], in_sems.at[j // GROUP]
+        )
+        copy.start()
+        arrivals.append(copy)
+    for j in range(0, local, GROUP):
+        rows = pl.ds(j * BT, GROUP * BT)
+        arrivals[j // GROUP].wait()
+        keep = row_mask(valid_ref, j, GROUP)
         grad = lax.dot_general(
-            mid_grad_ref[rows, :], weights_ref[3], OVER_LAST, preferred_element_type=F32
+            mid_grad_ref[rows, :], weight(weights_ref, 3), OVER_LAST, preferred_element_type=F32
         )
         grad = (grad + jnp.where(keep, out_w_ref[...], 0.0)) * slope_ref[rows, :].astype(F32)
-        before, after = neighbours(grad)
+        before, after = neighbours(grad, place, BT - 1)
         low = grad.astype(BF16)
         first_grad_ref[rows, :] = low
+        total = lax.dot_general(low, weight(weights_ref, 1), OVER_LAST, preferred_element_type=F32)
+        total += lax.dot_general(
+            after, weight(weights_ref, 0), OVER_LAST, preferred_element_type=F32
+        )
+        total += lax.dot_general(
+            before, weight(weights_ref, 2), OVER_LAST, preferred_element_type=F32
+        )
+        total = jnp.where(keep, total, 0.0).astype(BF16)
+        for i in range(GROUP):
+            ready_ref[j + i] = total[i * BT : (i + 1) * BT]
+            copy = pltpu.make_async_copy(
+                ready_ref.at[j + i], slots_ref.at[owner_ref[j + i]], sems.at[j + i]
+            )
+            copy.start()
+            copies.append(copy)
         copy = pltpu.make_async_copy(
-            first_grad_ref.at[rows], first_grad_out.at[rows], out_sems.at[j]
-        )
-        copy.start()
-        copies.append(copy)
-        if j == 0:
-            for k in (1, 0, 2):
-                arrivals[k].wait()
-        total = lax.dot_general(low, weights_ref[1], OVER_LAST, preferred_element_type=F32)
-        total += lax.dot_general(after, weights_ref[0], OVER_LAST, preferred_element_type=F32)
-        total += lax.dot_general(before, weights_ref[2], OVER_LAST, preferred_element_type=F32)
-        ready_ref[j] = jnp.where(keep, total, 0.0).astype(BF16)
-        copy = pltpu.make_async_copy(ready_ref.at[j], slots_ref.at[owner_ref[j]], sems.at[j])
+            first_grad_ref.at[rows], first_grad_out.at[rows], out_sems.at[j // GROUP]
+        )
         copy.start()
         copies.append(copy)
     for copy in copies:
@@ -243,19 +262,40 @@
 
 
 def weight_kernel(
-    factor_ref, masked_ref, low_ref, mid_grad_ref, first_grad_ref, sums_ref,
-    parts_ref, conv_ref, mid_ref, stage_ref,
+    valid_ref, factor_ref, feats_hbm, low_hbm, mid_grad_hbm, first_grad_hbm, sums_ref,
+    parts_ref, feats_ref, low_ref, mid_grad_ref, first_grad_ref, conv_ref, mid_ref, stage_ref, sems,
 ):
-    local = factor_ref.shape[0]
-    out = jnp.zeros((1, D), F32)
+    local = valid_ref.shape[0]
+    pairs = (
+        (feats_hbm, feats_ref),
+        (low_hbm, low_ref),
+        (mid_grad_hbm, mid_grad_ref),
+        (first_grad_hbm, first_grad_ref),
+    )
+    arrivals = []
     for j in range(local):
         rows = pl.ds(j * BT, BT)
+        arrivals.append(
+            [
+                pltpu.make_async_copy(source.at[rows], target.at[rows], sems.at[i, j])
+                for i, (source, target) in enumerate(pairs)
+            ]
+        )
+        for copy in arrivals[j]:
+            copy.start()
+    out = jnp.zeros((1, D), F32)
+    place = block_place(BT)
+    for j in range(local):
+        rows = pl.ds(j * BT, BT)
+        for copy in arrivals[j]:
+            copy.wait()
         factor = factor_ref[j]
         out += sums_ref[j : j + 1, :] * factor
         grad = first_grad_ref[rows, :].astype(F32) * factor
-        before, after = neighbours(grad)
+        before, after = neighbours(grad, place, BT - 1)
         mid_grad = (mid_grad_ref[rows, :].astype(F32) * factor).astype(BF16)
-        masked = masked_ref[rows, :]
+        keep = row_mask(valid_ref, j, 1)
+        masked = jnp.where(keep, feats_ref[rows, :].astype(F32), 0.0).astype(BF16)
         terms = [
             lax.dot_general(masked, x, OVER_ROWS, preferred_element_type=F32)
             for x in (after, grad.astype(BF16), before)
@@ -285,10 +325,10 @@
         parts_ref[d] = stage_ref[...].astype(BF16)
 
 
-def finish_kernel(own_ref, first_ref, second_ref, third_ref, conv_ref, mid_ref, out_ref, total_ref):
-    total = own_ref[...]
-    for piece in (first_ref, second_ref, third_ref):
-        total += piece[...].astype(F32)
+def finish_kernel(pieces_ref, conv_ref, mid_ref, out_ref, total_ref):
+    total = pieces_ref[0].astype(F32)
+    for i in range(1, pieces_ref.shape[0]):
+        total += pieces_ref[i].astype(F32)
     total_ref[...] = total * (1.0 / BT)
     for row in range(3 * SHARD):
         conv_ref[row] = total_ref[row : row + 1, :]
@@ -312,9 +352,8 @@
         arrivals[slot].wait()
         factor = jnp.where(slot < count_ref[0], factor_ref[0], 0.0)
         ready_ref[slot] = (raw_ref[slot].astype(F32) * factor).astype(BF16)
-        copy = pltpu.make_async_copy(
-            ready_ref.at[slot], placed_ref.at[pl.ds(slot * BT, BT)], out_sems.at[slot]
-        )
+        rows = pl.ds(slot * BT, BT)
+        copy = pltpu.make_async_copy(ready_ref.at[slot], placed_ref.at[rows], out_sems.at[slot])
         copy.start()
         departures.append(copy)
     for copy in departures:
@@ -374,17 +413,14 @@
     own = lax.all_to_all(copies, CHIPS, split_axis=0, concat_axis=0, tiled=True)
     other = swapped(own)
 
-    later = (IN_HBM, (tokens_here, D), BF16)
-    masked, low, mid_grad, weights, state, sums, out_w, extras, totals = call(
+    low, mid_grad, state, sums, out_w, extras, totals = call(
         forward_kernel,
         "forward",
-        [IN_SMEM, IN_SMEM, IN_SMEM, IN_HBM, IN_HBM, IN_VMEM],
+        [IN_SMEM, IN_SMEM, IN_SMEM, IN_HBM, IN_HBM, IN_HBM],
         [
-            later,
-            later,
-            later,
-            (IN_HBM, (4, D, D), BF16),
-            (IN_VMEM, (2, tokens_here, D), BF16),
+            (IN_HBM, (tokens_here, D), BF16),
+            (IN_HBM, (tokens_here, D), BF16),
+            (IN_VMEM, (tokens_here + 4 * D, D), BF16),
             (IN_VMEM, (local, D), F32),
             (IN_VMEM, (1, D), F32),
             (IN_VMEM, (devices, 128), F32),
@@ -392,34 +428,37 @@
         ],
         [
             pltpu.VMEM((tokens_here, D), BF16),
-            pltpu.VMEM((4, D, D), BF16),
+            pltpu.VMEM((chips, ROWS, D), BF16),
             pltpu.VMEM((chips, ROWS, D), BF16),
             pltpu.VMEM((tokens_here, D), BF16),
             pltpu.VMEM((tokens_here, D), BF16),
-            pltpu.VMEM((4, D, D), F32),
+            pltpu.VMEM((4 * D, D), F32),
             pltpu.SemaphoreType.DMA((local // GROUP,)),
-            pltpu.SemaphoreType.DMA((3, local // GROUP)),
+            pltpu.SemaphoreType.DMA((2, local // GROUP)),
             pltpu.SemaphoreType.DMA((2,)),
         ],
-    )(valid, owner_map, core, in_hbm(feats[0]), in_hbm(own), in_vmem(other))
+    )(valid, owner_map, core, in_hbm(feats[0]), in_hbm(own), in_hbm(other))
 
     totals = lax.all_to_all(totals, DP, split_axis=0, concat_axis=0, tiled=True)
 
     first_grad, slots = call(
         backward_kernel,
         "backward",
-        [IN_SMEM, IN_SMEM, IN_VMEM, IN_HBM, IN_VMEM],
-        [later, (IN_HBM, (devices, BT, D), BF16)],
+        [IN_SMEM, IN_SMEM, IN_HBM, IN_VMEM, IN_VMEM],
         [
-            pltpu.VMEM((4, D, D), BF16),
+            (IN_HBM, (tokens_here, D), BF16),
+            (IN_HBM, (devices, BT, D), BF16),
+        ],
+        [
+            pltpu.VMEM((tokens_here, D), BF16),
             pltpu.VMEM((tokens_here, D), BF16),
             pltpu.VMEM((local, BT, D), BF16),
             pltpu.SemaphoreType.DMA((local,)),
-            pltpu.SemaphoreType.DMA((local,)),
-            pltpu.SemaphoreType.DMA((4,)),
+            pltpu.SemaphoreType.DMA((local // GROUP,)),
+            pltpu.SemaphoreType.DMA((local // GROUP,)),
         ],
         megabytes=24,
-    )(valid, owner_map, in_vmem(state), in_hbm(weights), in_vmem(out_w))
+    )(valid, owner_map, in_hbm(mid_grad), in_vmem(state), in_vmem(out_w))
 
     slots, totals = lax.optimization_barrier((slots, totals))
     received = lax.all_to_all(slots, DP, split_axis=0, concat_axis=0, tiled=True)
@@ -437,16 +476,27 @@
     (parts,) = call(
         weight_kernel,
         "weight_grads",
-        [IN_SMEM, IN_VMEM, IN_VMEM, IN_VMEM, IN_VMEM, IN_VMEM],
+        [IN_SMEM, IN_SMEM, IN_HBM, IN_HBM, IN_HBM, IN_HBM, IN_VMEM],
         [(IN_VMEM, (devices, ROWS, D), BF16)],
-        [pltpu.VMEM((3, D, D), F32), pltpu.VMEM((D, D), F32), pltpu.VMEM((ROWS, D), F32)],
+        [pltpu.VMEM((tokens_here, D), BF16)] * 4
+        + [
+            pltpu.VMEM((3, D, D), F32),
+            pltpu.VMEM((D, D), F32),
+            pltpu.VMEM((ROWS, D), F32),
+            pltpu.SemaphoreType.DMA((4, local)),
+        ],
         megabytes=16,
-    )(block_factor, masked, low, mid_grad, first_grad, sums)
+    )(
+        valid, block_factor, in_hbm(feats[0]), in_hbm(low), in_hbm(mid_grad),
+        in_hbm(first_grad), in_vmem(sums),
+    )
     parts = parts.reshape(4, 4, 2, ROWS, D)
     parts = scattered_sum(parts, "dp_2", 2)
     parts = scattered_sum(parts, "dp_0", 0)
     parts, received = lax.optimization_barrier((parts, received))
-    pieces = scattered(parts, "dp_1", 0)
+    pieces = lax.all_to_all(
+        parts.astype(BF16), "dp_1", split_axis=0, concat_axis=0, tiled=True
+    )
 
     present = jnp.sum((owners == me).astype(jnp.int32), 1)
     rank = jnp.sum(jnp.where(images[None, :] < images[:, None], present[None, :], 0), 1)
@@ -466,11 +516,11 @@
             pltpu.SemaphoreType.DMA((capacity,)),
         ],
         megabytes=24,
-    )(source, count.reshape(1), own_factor, received)
+    )(source, count.reshape(1), own_factor, in_hbm(received))
 
     conv, mid, out = pl.pallas_call(
         finish_kernel,
-        in_specs=[IN_VMEM] * 4,
+        in_specs=[IN_VMEM],
         out_specs=[IN_VMEM] * 3,
         out_shape=[
             jax.ShapeDtypeStruct((3 * SHARD, 1, D), F32),
@@ -479,7 +529,7 @@
         ],
         scratch_shapes=[pltpu.VMEM((ROWS, D), F32)],
         name="finish",
-    )(*(in_vmem(x) for x in pieces))
+    )(in_vmem(pieces))
     return placed[None], conv.reshape(1, 3, SHARD, D), mid.reshape(1, SHARD, D), out
 
 

time: 149 us -> 149 us (level)
  local copies, waits for them, and re-layouts: 6.36 us -> 1.01 us
  Pallas kernels: 31.2 us -> 34.2 us
  waiting for transfers between devices: 58.4 us -> 60.4 us
    unnamed x18 -> x8, local copies, waits for them, and re-layouts: 6.18 us -> 0.86 us
    ppermute x10 -> x7, starting transfers between devices: 15 us -> 9.81 us  [turned(): lax.ppermute(x, axis, [(i, (i + shift) % count) for i in range(count)])]
    all_to_all x0 -> x1, starting transfers between devices: none -> 4.37 us  [per_device(): lax.all_to_all(parts.astype(BF16), 'dp_1', split_axis=0, concat_axis=0, t...]
    pallas_call x3, Pallas kernels: 12.7 us -> 15.8 us  [the longest x1 7.67 us: per_device(): call(backward_kernel, 'backward', [IN_SMEM, IN_SMEM, IN_HBM, IN_VMEM, IN_...]
    ppermute x10 -> x7, waiting for transfers between devices: 56.6 us -> 58.6 us  [turned(): lax.ppermute(x, axis, [(i, (i + shift) % count) for i in range(count)])]
  transfers between devices with their start and end apart: 13 -> 11, of which waited for: 5 -> 5; matrix products, arithmetic and copies ran while one was open for 2% -> 2% of each run, Pallas kernels for 12% -> 14%
where the time goes in v4:
time: 149 us; the launch traced here: 147 us
  waiting for transfers between devices  60.4 us (41%)
  Pallas kernels  34.2 us (23%)
  starting transfers between devices  27.6 us (19%)
  blocking collectives  19.6 us (13%)
  other arithmetic  3.05 us (2%)
    ppermute x7, waiting for transfers between devices, turned(): lax.ppermute(x, axis, [(i, (i + shift) % count) for i in range(count)])  58.6 us
    all_to_all x1, blocking collectives, per_device(): own = lax.all_to_all(copies, CHIPS, split_axis=0, concat_axis=0, tiled=True)  19.6 us
    pallas_call x1, Pallas kernels, per_device(): call(forward_kernel, 'forward', [IN_SMEM, IN_SMEM, IN_SMEM, IN_HBM, IN_HB...  11.6 us
    ppermute x7, starting transfers between devices, turned(): lax.ppermute(x, axis, [(i, (i + shift) % count) for i in range(count)])  9.81 us
    pallas_call x1, Pallas kernels, per_device(): call(backward_kernel, 'backward', [IN_SMEM, IN_SMEM, IN_HBM, IN_VMEM, IN_...  7.67 us
    all_to_all x1, starting transfers between devices, per_device(): lax.all_to_all(slots, DP, split_axis=0, concat_axis=0, tiled=True)  7.53 us
    pallas_call x1, Pallas kernels, per_device(): call(weight_kernel, 'weight_grads', [IN_SMEM, IN_SMEM, IN_HBM, IN_HBM, IN...  7.46 us
    pallas_call x1, Pallas kernels, per_device(): call(place_kernel, 'place', [IN_SMEM, IN_SMEM, IN_SMEM, IN_HBM], [(IN_HBM...  5.84 us
  transfers between devices with their start and end apart: 11, of which 5 were waited for; matrix products, arithmetic and copies ran while one was open for 2% of the time, Pallas kernels for 14%

profile of v4, /device:TPU:1, one launch (start us, length us, event | category | flops | bytes accessed | tf_op | source)
XLA Modules:
  0.0 147.3 jit_solution(13585758110122176499)
XLA Ops:
  0.6 0.0 copy-start
  0.6 0.0 copy-start.1
  0.7 0.9 pack.1
  1.6 19.6 %all_to_all.20.own_hbm = bf16[16,56,384]{2,1,0:T(8,128)(2,1)S(1)} all-to-all(bf16[16,56,384]{2,1,0:T(8,128)(2,1)S(1)} %pack.1), channel_id=1, replica_groups=mesh['dp_0'=4,'dp_1'=4,'dp_2'=2,'head'=4] {'dp_0','dp_1'}, dimensions={0} | all-to-all | bytes 1376256 | tf_op jit(solution)/shard_map/all_to_all | solution.py:413
  21.2 0.0 copy-start.2
  21.2 2.0 %collective-permute-start = (bf16[16,56,384]{2,1,0:T(8,128)(2,1)S(1)}, bf16[16,56,384]{2,1,0:T(8,128)(2,1)S(1)}, u32[]{:S(2)}, u32[]{:S(2)}) collective-permute-start(bf16[16,56,384]{2,1,0:T(8,128)(2,1)S(1)} %all_to_all.20.own_hbm), channel_id=1, source_target_pairs={{0,4},{4,0},{1,5},{5,1},{2,6},{6,2},{3,7},{7,3},{8,12},{12,8},{9,1... | collective-permute-start | bytes 2064392 | tf_op jit(solution)/shard_map/ppermute | solution.py:30
  23.2 1.8 %collective-permute-done.other_hbm = bf16[16,56,384]{2,1,0:T(8,128)(2,1)S(1)} collective-permute-done((bf16[16,56,384]{2,1,0:T(8,128)(2,1)S(1)}, bf16[16,56,384]{2,1,0:T(8,128)(2,1)S(1)}, u32[]{:S(2)}, u32[]{:S(2)}) %collective-permute-start) | collective-permute-done | bytes 688160 | tf_op jit(solution)/shard_map/ppermute | solution.py:30
  25.0 0.8 copy-done.3
  25.8 0.0 copy-done.2
  25.8 0.0 copy-done
  25.8 0.0 copy-done.1
  25.8 11.6 %forward.1 = (bf16[2048,384]{1,0:T(8,128)(2,1)}, bf16[2048,384]{1,0:T(8,128)(2,1)}, bf16[3584,384]{1,0:T(8,128)(2,1)S(1)}, f32[8,384]{1,0:T(8,128)S(1)}, f32[1,3...) custom-call(s32[8]{0:T(128)S(1)} %copy-done, s32[8]{0:T(128)S(1)} %copy-done.1, s32[1]{0:T(128)} %bitcast.core_ref, ...), custom_call_target="tpu_custom_call" | custom-call | tf_op jit(solution)/shard_map/forward/pallas_call | solution.py:416
  37.5 3.9 %all-to-all-start.1 = ((f32[32,1,128]{2,1,0:T(1,128)}), f32[32,1,128]{2,1,0:T(1,128)S(1)}, u32[]{:S(2)}, u32[]{:S(2)}) async-start(f32[32,1,128]{2,1,0:T(1,128)} %get-tuple-element.25), calls=%async_computation.1 | async-start | bytes 32768 | tf_op jit(solution)/shard_map/all_to_all | solution.py:442
  41.4 7.7 %backward.1 = (bf16[2048,384]{1,0:T(8,128)(2,1)}, bf16[32,256,384]{2,1,0:T(8,128)(2,1)}) custom-call(s32[8]{0:T(128)S(1)} %copy-done, s32[8]{0:T(128)S(1)} %copy-done.1, bf16[2048,384]{1,0:T(8,128)(2,1)} %get-tuple-element.21.mid_grad_hbm, bf16[3584,384]{1,0:T(8,128)(2,1)S(1)} %get-tuple-element.22.state_ref, f32[1,384]{1,0:T(1,128)S(1)} %get-tuple-element.23.out_w_ref), custom_call_target="tpu_custom_call" | custom-call | bytes 25165824 | tf_op jit(solution)/shard_map/backward/pallas_call | solution.py:444
  49.1 0.0 all-to-all-done.1
  49.1 7.5 %all-to-all-start.2 = ((bf16[32,256,384]{2,1,0:T(8,128)(2,1)}), bf16[32,256,384]{2,1,0:T(8,128)(2,1)}, u32[]{:S(2)}, u32[]{:S(2)}) async-start(bf16[32,256,384]{2,1,0:T(8,128)(2,1)} %get-tuple-element.30), calls=%async_computation.2 | async-start | bytes 12582912 | tf_op jit(solution)/shard_map/all_to_all | solution.py:464
  56.6 0.1 slice_convert_fusion
  56.7 0.2 select_reduce_fusion
  56.8 0.1 slice_reduce_fusion
  56.9 3.8 %collective-permute-start.3 = (f32[1,32]{1,0:T(1,128)S(1)}, f32[1,32]{1,0:T(1,128)S(1)}, u32[]{:S(2)}, u32[]{:S(2)}) collective-permute-start(f32[1,32]{1,0:T(1,128)S(1)} %bitcast.52), channel_id=1, source_target_pairs={{0,3},{1,0},{2,1},{3,2},{4,7},{5,4},{6,5},{7,6},{8,11},{9,8},{10,9... | collective-permute-start | bytes 392 | tf_op jit(solution)/shard_map/ppermute | solution.py:35
  60.7 0.0 collective-permute-start.2
  60.7 0.7 collective-permute-start.1
  61.4 0.0 collective-permute-done.3
  61.4 3.6 %collective-permute-done.2 = f32[1,32]{1,0:T(1,128)S(1)} collective-permute-done((f32[1,32]{1,0:T(1,128)S(1)}, f32[1,32]{1,0:T(1,128)S(1)}, u32[]{:S(2)}, u32[]{:S(2)}) %collective-permute-start.2) | collective-permute-done | bytes 160 | tf_op jit(solution)/shard_map/ppermute | solution.py:35
  65.0 0.0 collective-permute-done.1
  65.0 0.2 select_reduce_fusion.3.factor_ref
  65.2 7.5 %weight_grads.1 = bf16[32,56,384]{2,1,0:T(8,128)(2,1)S(1)} custom-call(s32[8]{0:T(128)S(1)} %copy-done, f32[8]{0:T(128)S(1)} %select_reduce_fusion.3.factor_ref, bf16[2048,384]{1,0:T(8,128)(2,1)} %bitcast.48, bf16[2048,384]{1,0:T(8,128)(2,1)} %get-tuple-element.27.low_hbm, bf16[2048,384]{1,0:T(8,128)(2,1)} %get-tuple-element.21.mid_grad_hbm, ...), custom_call_target="tpu_custom_call" | custom-call | bytes 16777216 | tf_op jit(solution)/shard_map/weight_grads/pallas_call | solution.py:476
  72.7 0.1 dynamic-slice_bitcast_fusion
  72.8 1.4 collective-permute-start.4
  74.2 0.7 convert_reduce_fusion
  75.6 0.1 select_reduce_fusion.1
  75.7 0.3 collective-permute-done.4
  76.0 0.2 convert_add_fusion
  76.1 0.1 fusion.2
  76.2 2.8 %collective-permute-start.7 = (bf16[4,56,384]{2,1,0:T(8,128)(2,1)S(1)}, bf16[4,56,384]{2,1,0:T(8,128)(2,1)S(1)}, u32[]{:S(2)}, u32[]{:S(2)}) collective-permute-start(bf16[4,56,384]{2,1,0:T(8,128)(2,1)S(1)} %get-tuple-element.41), channel_id=1, source_target_pairs={{0,96},{32,0},{64,32},{96,64},{1,97},{33,1},{65,33},{97,65},{2,98}... | collective-permute-start | bytes 516104 | tf_op jit(solution)/shard_map/ppermute | solution.py:35
  79.0 0.5 collective-permute-start.6
  79.5 0.6 collective-permute-start.5
  80.1 51.8 %collective-permute-done.7 = bf16[4,56,384]{2,1,0:T(8,128)(2,1)S(1)} collective-permute-done((bf16[4,56,384]{2,1,0:T(8,128)(2,1)S(1)}, bf16[4,56,384]{2,1,0:T(8,128)(2,1)S(1)}, u32[]{:S(2)}, u32[]{:S(2)}) %collective-permute-start.7) | collective-permute-done | bytes 172064 | tf_op jit(solution)/shard_map/ppermute | solution.py:35
  131.9 0.0 collective-permute-done.6
  131.9 2.9 %collective-permute-done.5 = bf16[4,56,384]{2,1,0:T(8,128)(2,1)S(1)} collective-permute-done((bf16[4,56,384]{2,1,0:T(8,128)(2,1)S(1)}, bf16[4,56,384]{2,1,0:T(8,128)(2,1)S(1)}, u32[]{:S(2)}, u32[]{:S(2)}) %collective-permute-start.5) | collective-permute-done | bytes 172064 | tf_op jit(solution)/shard_map/ppermute | solution.py:35
  134.9 0.8 fusion.1
  135.6 0.0 all-to-all-done.2.received_ref
  135.6 4.4 %all-to-all-start.3 = ((bf16[4,56,384]{2,1,0:T(8,128)(2,1)}), bf16[4,56,384]{2,1,0:T(8,128)(2,1)S(1)}, u32[]{:S(2)}, u32[]{:S(2)}) async-start(bf16[4,56,384]{2,1,0:T(8,128)(2,1)} %fusion.1), calls=%async_computation.3 | async-start | bytes 344064 | tf_op jit(solution)/shard_map/all_to_all | solution.py:497
  140.0 0.2 select_reduce_fusion.2.source_ref
  140.2 0.6 fusion.5
  140.8 5.8 %place.1 = bf16[4096,384]{1,0:T(8,128)(2,1)} custom-call(s32[16]{0:T(128)S(1)} %select_reduce_fusion.2.source_ref, s32[1]{0:T(128)} %bitcast.4.count_ref, f32[1]{0:T(128)} %bitcast.7.factor_ref, bf16[32,256,384]{2,1,0:T(8,128)(2,1)} %all-to-all-done.2.received_ref), custom_call_target="tpu_custom_call" | custom-call | bytes 25165824 | tf_op jit(solution)/shard_map/place/pallas_call | solution.py:507
  146.7 0.0 all-to-all-done.3.pieces_ref
  146.7 0.7 finish.1
  (4 shorter events, 0.0 us)
Async XLA Ops:
  0.6 25.2 %copy-start = (s32[8]{0:T(128)S(1)}, s32[8]{0:T(128)}, u32[]{:S(2)}) copy-start(s32[8]{0:T(128)} %valid_ref.5) | copy-start | bytes 100
  0.6 25.2 %copy-start.1 = (s32[8]{0:T(128)S(1)}, s32[8]{0:T(128)}, u32[]{:S(2)}) copy-start(s32[8]{0:T(128)} %owner_ref.3) | copy-start | bytes 100
  21.2 4.7 %copy-start.2 = (bf16[16,56,384]{2,1,0:T(8,128)(2,1)}, bf16[16,56,384]{2,1,0:T(8,128)(2,1)S(1)}, u32[]{:S(2)}) copy-start(bf16[16,56,384]{2,1,0:T(8,128)(2,1)S(1)} %all_to_all.20.own_hbm) | copy-start | bytes 2064388
  21.2 3.8 %collective-permute-start = (bf16[16,56,384]{2,1,0:T(8,128)(2,1)S(1)}, bf16[16,56,384]{2,1,0:T(8,128)(2,1)S(1)}, u32[]{:S(2)}, u32[]{:S(2)}) collective-permute-start(bf16[16,56,384]{2,1,0:T(8,128)(2,1)S(1)} %all_to_all.20.own_hbm), channel_id=1, source_target_pairs={{0,4},{4,0},{1,5},{5,1},{2,6},{6,2},{3,7},{7,3},{8,12},{12,8},{9,1... | collective-permute-start | bytes 2064392 | tf_op jit(solution)/shard_map/ppermute | solution.py:30
  25.0 0.8 copy-start.3
  37.5 11.6 %all-to-all-start.1 = ((f32[32,1,128]{2,1,0:T(1,128)}), f32[32,1,128]{2,1,0:T(1,128)S(1)}, u32[]{:S(2)}, u32[]{:S(2)}) async-start(f32[32,1,128]{2,1,0:T(1,128)} %get-tuple-element.25), calls=%async_computation.1 | async-start | bytes 32768 | tf_op jit(solution)/shard_map/all_to_all | solution.py:442
  49.1 86.5 %all-to-all-start.2 = ((bf16[32,256,384]{2,1,0:T(8,128)(2,1)}), bf16[32,256,384]{2,1,0:T(8,128)(2,1)}, u32[]{:S(2)}, u32[]{:S(2)}) async-start(bf16[32,256,384]{2,1,0:T(8,128)(2,1)} %get-tuple-element.30), calls=%async_computation.2 | async-start | bytes 12582912 | tf_op jit(solution)/shard_map/all_to_all | solution.py:464
  56.9 4.5 %collective-permute-start.3 = (f32[1,32]{1,0:T(1,128)S(1)}, f32[1,32]{1,0:T(1,128)S(1)}, u32[]{:S(2)}, u32[]{:S(2)}) collective-permute-start(f32[1,32]{1,0:T(1,128)S(1)} %bitcast.52), channel_id=1, source_target_pairs={{0,3},{1,0},{2,1},{3,2},{4,7},{5,4},{6,5},{7,6},{8,11},{9,8},{10,9... | collective-permute-start | bytes 392 | tf_op jit(solution)/shard_map/ppermute | solution.py:35
  60.7 4.3 %collective-permute-start.2 = (f32[1,32]{1,0:T(1,128)S(1)}, f32[1,32]{1,0:T(1,128)S(1)}, u32[]{:S(2)}, u32[]{:S(2)}) collective-permute-start(f32[1,32]{1,0:T(1,128)S(1)} %bitcast.53), channel_id=1, source_target_pairs={{0,2},{1,3},{2,0},{3,1},{4,6},{5,7},{6,4},{7,5},{8,10},{9,11},{10,... | collective-permute-start | bytes 392 | tf_op jit(solution)/shard_map/ppermute | solution.py:35
  60.7 4.3 %collective-permute-start.1 = (f32[1,32]{1,0:T(1,128)S(1)}, f32[1,32]{1,0:T(1,128)S(1)}, u32[]{:S(2)}, u32[]{:S(2)}) collective-permute-start(f32[1,32]{1,0:T(1,128)S(1)} %bitcast.54), channel_id=1, source_target_pairs={{0,1},{1,2},{2,3},{3,0},{4,5},{5,6},{6,7},{7,4},{8,9},{9,10},{10,1... | collective-permute-start | bytes 392 | tf_op jit(solution)/shard_map/ppermute | solution.py:35
  72.8 3.2 %collective-permute-start.4 = (bf16[4,4,56,384]{3,2,1,0:T(8,128)(2,1)S(1)}, bf16[4,4,56,384]{3,2,1,0:T(8,128)(2,1)S(1)}, u32[]{:S(2)}, u32[]{:S(2)}) collective-permute-start(bf16[4,4,56,384]{3,2,1,0:T(8,128)(2,1)S(1)} %dynamic-slice_bitcast_fusion), channel_id=1, source_target_pairs={{0,4},{4,0},{1,5},{5,1},{2,6},{6,2},{3,7},{7,3},{8,12},{12,8},{9,1... | collective-permute-start | bytes 2064392 | tf_op jit(solution)/shard_map/ppermute | solution.py:35
  76.2 55.7 %collective-permute-start.7 = (bf16[4,56,384]{2,1,0:T(8,128)(2,1)S(1)}, bf16[4,56,384]{2,1,0:T(8,128)(2,1)S(1)}, u32[]{:S(2)}, u32[]{:S(2)}) collective-permute-start(bf16[4,56,384]{2,1,0:T(8,128)(2,1)S(1)} %get-tuple-element.41), channel_id=1, source_target_pairs={{0,96},{32,0},{64,32},{96,64},{1,97},{33,1},{65,33},{97,65},{2,98}... | collective-permute-start | bytes 516104 | tf_op jit(solution)/shard_map/ppermute | solution.py:35
  79.0 53.0 %collective-permute-start.6 = (bf16[4,56,384]{2,1,0:T(8,128)(2,1)S(1)}, bf16[4,56,384]{2,1,0:T(8,128)(2,1)S(1)}, u32[]{:S(2)}, u32[]{:S(2)}) collective-permute-start(bf16[4,56,384]{2,1,0:T(8,128)(2,1)S(1)} %get-tuple-element.42), channel_id=1, source_target_pairs={{0,64},{32,96},{64,0},{96,32},{1,65},{33,97},{65,1},{97,33},{2,66}... | collective-permute-start | bytes 516104 | tf_op jit(solution)/shard_map/ppermute | solution.py:35
  79.5 55.3 %collective-permute-start.5 = (bf16[4,56,384]{2,1,0:T(8,128)(2,1)S(1)}, bf16[4,56,384]{2,1,0:T(8,128)(2,1)S(1)}, u32[]{:S(2)}, u32[]{:S(2)}) collective-permute-start(bf16[4,56,384]{2,1,0:T(8,128)(2,1)S(1)} %get-tuple-element.40), channel_id=1, source_target_pairs={{0,32},{32,64},{64,96},{96,0},{1,33},{33,65},{65,97},{97,1},{2,34}... | collective-permute-start | bytes 516104 | tf_op jit(solution)/shard_map/ppermute | solution.py:35
  135.6 11.0 %all-to-all-start.3 = ((bf16[4,56,384]{2,1,0:T(8,128)(2,1)}), bf16[4,56,384]{2,1,0:T(8,128)(2,1)S(1)}, u32[]{:S(2)}, u32[]{:S(2)}) async-start(bf16[4,56,384]{2,1,0:T(8,128)(2,1)} %fusion.1), calls=%async_computation.3 | async-start | bytes 344064 | tf_op jit(solution)/shard_map/all_to_all | solution.py:497

commit v5 on v4

--- a/solution.py
+++ b/solution.py
@@ -16,7 +16,8 @@
 SHARD = 12
 EXTRA = 4 * SHARD
 ROWS = 56
-GROUP = 2
+GROUP = 4
+LOG_2 = 0.6931471805599453
 VMEM_LIMIT = 20 * 1024 * 1024
 
 IN_VMEM = pl.BlockSpec(memory_space=pltpu.VMEM)
@@ -54,8 +55,8 @@
 
 def gate(value):
     half = jnp.tanh(0.5 * value)
-    act = jnp.maximum(value, 0.2 * value) - 0.8 * jnp.log(0.5 + 0.5 * jnp.abs(half))
-    return act, 0.6 + 0.4 * half
+    tail = 0.8 * LOG_2 - (0.8 * LOG_2) * jnp.log2(1.0 + jnp.abs(half))
+    return jnp.maximum(value, 0.2 * value) + tail, 0.6 + 0.4 * half
 
 
 def row_mask(valid_ref, first, blocks):
@@ -108,6 +109,11 @@
         copies_ref[j] = packed
 
 
+def chunks(local):
+    half, quarter = local // 2, local // 4
+    return ((0, half), (half, quarter), (half + quarter, quarter))
+
+
 def state_rows(local):
     tokens = local * BT
     return pl.ds(0, tokens), pl.ds(tokens, 4 * D)
@@ -128,11 +134,9 @@
         pltpu.make_async_copy(own_hbm, own_ref, weight_sems.at[0]),
         pltpu.make_async_copy(other_hbm, other_ref, weight_sems.at[1]),
     ]
-    for j in range(0, local, GROUP):
-        rows = pl.ds(j * BT, GROUP * BT)
-        arrivals.append(
-            pltpu.make_async_copy(feats_ref.at[rows], raw_ref.at[rows], sems.at[j // GROUP])
-        )
+    for n, (j, group) in enumerate(chunks(local)):
+        rows = pl.ds(j * BT, group * BT)
+        arrivals.append(pltpu.make_async_copy(feats_ref.at[rows], raw_ref.at[rows], sems.at[n]))
     for copy in arrivals:
         copy.start()
 
@@ -171,12 +175,12 @@
 
     lane = lax.broadcasted_iota(jnp.int32, (1, 128), 1)
     totals = jnp.zeros((1, 128), F32)
-    place = block_place(GROUP * BT)
     departures = []
-    for j in range(0, local, GROUP):
-        rows = pl.ds(j * BT, GROUP * BT)
-        arrivals[2 + j // GROUP].wait()
-        keep = row_mask(valid_ref, j, GROUP)
+    for n, (j, group) in enumerate(chunks(local)):
+        rows = pl.ds(j * BT, group * BT)
+        arrivals[2 + n].wait()
+        place = block_place(group * BT)
+        keep = row_mask(valid_ref, j, group)
         masked = jnp.where(keep, raw_ref[rows, :].astype(F32), 0.0)
         before, after = neighbours(masked, place, BT - 1)
         first = jnp.dot(before, weight(weights_ref, 0), preferred_element_type=F32)
@@ -187,7 +191,7 @@
         first_act, slope = gate(first)
         low = first_act.astype(BF16)
         low_ref[rows, :] = low
-        copy = pltpu.make_async_copy(low_ref.at[rows], low_out.at[rows], out_sems.at[0, j // GROUP])
+        copy = pltpu.make_async_copy(low_ref.at[rows], low_out.at[rows], out_sems.at[0, n])
         copy.start()
         departures.append(copy)
         slope_ref[rows, :] = slope.astype(BF16)
@@ -195,12 +199,12 @@
         second_act, second_slope = gate(second)
         mid_grad_ref[rows, :] = jnp.where(keep, out_w * second_slope, 0.0).astype(BF16)
         copy = pltpu.make_async_copy(
-            mid_grad_ref.at[rows], mid_grad_out.at[rows], out_sems.at[1, j // GROUP]
+            mid_grad_ref.at[rows], mid_grad_out.at[rows], out_sems.at[1, n]
         )
         copy.start()
         departures.append(copy)
         total = jnp.where(keep, second_act + first_act, 0.0)
-        for i in range(GROUP):
+        for i in range(group):
             block = jnp.sum(total[i * BT : (i + 1) * BT], 0, keepdims=True)
             sums_ref[j + i : j + i + 1, :] = block
             block_sum = jnp.sum(block * out_w, 1, keepdims=True)
@@ -325,10 +329,10 @@
         parts_ref[d] = stage_ref[...].astype(BF16)
 
 
-def finish_kernel(pieces_ref, conv_ref, mid_ref, out_ref, total_ref):
-    total = pieces_ref[0].astype(F32)
-    for i in range(1, pieces_ref.shape[0]):
-        total += pieces_ref[i].astype(F32)
+def finish_kernel(own_ref, first_ref, second_ref, third_ref, conv_ref, mid_ref, out_ref, total_ref):
+    total = own_ref[...]
+    for piece in (first_ref, second_ref, third_ref):
+        total += piece[...].astype(F32)
     total_ref[...] = total * (1.0 / BT)
     for row in range(3 * SHARD):
         conv_ref[row] = total_ref[row : row + 1, :]
@@ -433,8 +437,8 @@
             pltpu.VMEM((tokens_here, D), BF16),
             pltpu.VMEM((tokens_here, D), BF16),
             pltpu.VMEM((4 * D, D), F32),
-            pltpu.SemaphoreType.DMA((local // GROUP,)),
-            pltpu.SemaphoreType.DMA((2, local // GROUP)),
+            pltpu.SemaphoreType.DMA((3,)),
+            pltpu.SemaphoreType.DMA((2, 3)),
             pltpu.SemaphoreType.DMA((2,)),
         ],
     )(valid, owner_map, core, in_hbm(feats[0]), in_hbm(own), in_hbm(other))
@@ -492,11 +496,7 @@
     )
     parts = parts.reshape(4, 4, 2, ROWS, D)
     parts = scattered_sum(parts, "dp_2", 2)
-    parts = scattered_sum(parts, "dp_0", 0)
-    parts, received = lax.optimization_barrier((parts, received))
-    pieces = lax.all_to_all(
-        parts.astype(BF16), "dp_1", split_axis=0, concat_axis=0, tiled=True
-    )
+    pieces = scattered(parts, "dp_0", 0)
 
     present = jnp.sum((owners == me).astype(jnp.int32), 1)
     rank = jnp.sum(jnp.where(images[None, :] < images[:, None], present[None, :], 0), 1)
@@ -518,9 +518,11 @@
         megabytes=24,
     )(source, count.reshape(1), own_factor, in_hbm(received))
 
+    pieces, placed = lax.optimization_barrier((pieces, placed))
+    pieces = scattered(sum(piece.astype(F32) for piece in pieces), "dp_1", 0)
     conv, mid, out = pl.pallas_call(
         finish_kernel,
-        in_specs=[IN_VMEM],
+        in_specs=[IN_VMEM] * 4,
         out_specs=[IN_VMEM] * 3,
         out_shape=[
             jax.ShapeDtypeStruct((3 * SHARD, 1, D), F32),
@@ -529,7 +531,7 @@
         ],
         scratch_shapes=[pltpu.VMEM((ROWS, D), F32)],
         name="finish",
-    )(in_vmem(pieces))
+    )(*(in_vmem(x) for x in pieces))
     return placed[None], conv.reshape(1, 3, SHARD, D), mid.reshape(1, SHARD, D), out
 
 

time: 149 us -> 147 us (0.987)
  waiting for transfers between devices: 60.4 us -> 57.3 us
  starting transfers between devices: 27.6 us -> 30.5 us
    ppermute x7 -> x10, waiting for transfers between devices: 58.6 us -> 7.19 us  [turned(): lax.ppermute(x, axis, [(i, (i + shift) % count) for i in range(count)])]
    all_to_all x1, waiting for transfers between devices: 0.01 us -> 48.3 us  [per_device(): lax.all_to_all(slots, DP, split_axis=0, concat_axis=0, tiled=True)]
    ppermute x7 -> x10, starting transfers between devices: 9.81 us -> 17.1 us  [turned(): lax.ppermute(x, axis, [(i, (i + shift) % count) for i in range(count)])]
    all_to_all x1 -> x0, starting transfers between devices: 4.37 us -> none  [per_device(): lax.all_to_all(parts.astype(BF16), 'dp_1', split_axis=0, concat_axis=0, t...]
  transfers between devices with their start and end apart: 11 -> 13, of which waited for: 5 -> 8; matrix products, arithmetic and copies ran while one was open for 2% -> 2% of each run, Pallas kernels for 14% -> 14%
where the time goes in v5:
time: 147 us; the launch traced here: 146 us
  waiting for transfers between devices  57.3 us (39%)
  Pallas kernels  33.2 us (23%)
  starting transfers between devices  30.5 us (21%)
  blocking collectives  19.6 us (13%)
  other arithmetic  2.37 us (2%)
  between operations  1.47 us (1%)
    all_to_all x1, waiting for transfers between devices, per_device(): lax.all_to_all(slots, DP, split_axis=0, concat_axis=0, tiled=True)  48.3 us
    all_to_all x1, blocking collectives, per_device(): own = lax.all_to_all(copies, CHIPS, split_axis=0, concat_axis=0, tiled=True)  19.6 us
    ppermute x10, starting transfers between devices, turned(): lax.ppermute(x, axis, [(i, (i + shift) % count) for i in range(count)])  17.1 us
    pallas_call x1, Pallas kernels, per_device(): call(forward_kernel, 'forward', [IN_SMEM, IN_SMEM, IN_SMEM, IN_HBM, IN_HB...  11 us
    all_to_all x1, starting transfers between devices, per_device(): lax.all_to_all(slots, DP, split_axis=0, concat_axis=0, tiled=True)  7.55 us
    pallas_call x1, Pallas kernels, per_device(): call(weight_kernel, 'weight_grads', [IN_SMEM, IN_SMEM, IN_HBM, IN_HBM, IN...  7.45 us
    pallas_call x1, Pallas kernels, per_device(): call(backward_kernel, 'backward', [IN_SMEM, IN_SMEM, IN_HBM, IN_VMEM, IN_...  7.36 us
    ppermute x10, waiting for transfers between devices, turned(): lax.ppermute(x, axis, [(i, (i + shift) % count) for i in range(count)])  7.19 us
  transfers between devices with their start and end apart: 13, of which 8 were waited for; matrix products, arithmetic and copies ran while one was open for 2% of the time, Pallas kernels for 14%

profile of v5, /device:TPU:1, one launch (start us, length us, event | category | flops | bytes accessed | tf_op | source)
XLA Modules:
  0.0 145.6 jit_solution(15492955294582835349)
XLA Ops:
  0.6 0.0 copy-start
  0.6 0.0 copy-start.1
  0.7 0.9 pack.1
  1.6 19.6 %all_to_all.15.own_hbm = bf16[16,56,384]{2,1,0:T(8,128)(2,1)S(1)} all-to-all(bf16[16,56,384]{2,1,0:T(8,128)(2,1)S(1)} %pack.1), channel_id=1, replica_groups=mesh['dp_0'=4,'dp_1'=4,'dp_2'=2,'head'=4] {'dp_0','dp_1'}, dimensions={0} | all-to-all | bytes 1376256 | tf_op jit(solution)/shard_map/all_to_all | solution.py:417
  21.2 2.0 %collective-permute-start = (bf16[16,56,384]{2,1,0:T(8,128)(2,1)S(1)}, bf16[16,56,384]{2,1,0:T(8,128)(2,1)S(1)}, u32[]{:S(2)}, u32[]{:S(2)}) collective-permute-start(bf16[16,56,384]{2,1,0:T(8,128)(2,1)S(1)} %all_to_all.15.own_hbm), channel_id=1, source_target_pairs={{0,4},{4,0},{1,5},{5,1},{2,6},{6,2},{3,7},{7,3},{8,12},{12,8},{9,1... | collective-permute-start | bytes 2064392 | tf_op jit(solution)/shard_map/ppermute | solution.py:31
  23.2 1.8 %collective-permute-done.other_hbm = bf16[16,56,384]{2,1,0:T(8,128)(2,1)S(1)} collective-permute-done((bf16[16,56,384]{2,1,0:T(8,128)(2,1)S(1)}, bf16[16,56,384]{2,1,0:T(8,128)(2,1)S(1)}, u32[]{:S(2)}, u32[]{:S(2)}) %collective-permute-start) | collective-permute-done | bytes 688160 | tf_op jit(solution)/shard_map/ppermute | solution.py:31
  25.0 0.8 copy-done.3
  25.8 11.0 %forward.1 = (bf16[2048,384]{1,0:T(8,128)(2,1)}, bf16[2048,384]{1,0:T(8,128)(2,1)}, bf16[3584,384]{1,0:T(8,128)(2,1)S(1)}, f32[8,384]{1,0:T(8,128)S(1)}, f32[1,3...) custom-call(s32[8]{0:T(128)S(1)} %copy-done, s32[8]{0:T(128)S(1)} %copy-done.1, s32[1]{0:T(128)} %bitcast.core_ref, ...), custom_call_target="tpu_custom_call" | custom-call | tf_op jit(solution)/shard_map/forward/pallas_call | solution.py:420
  36.9 3.9 %all-to-all-start.1 = ((f32[32,1,128]{2,1,0:T(1,128)}), f32[32,1,128]{2,1,0:T(1,128)S(1)}, u32[]{:S(2)}, u32[]{:S(2)}) async-start(f32[32,1,128]{2,1,0:T(1,128)} %get-tuple-element.27), calls=%async_computation.1 | async-start | bytes 32768 | tf_op jit(solution)/shard_map/all_to_all | solution.py:446
  40.8 7.4 %backward.1 = (bf16[2048,384]{1,0:T(8,128)(2,1)}, bf16[32,256,384]{2,1,0:T(8,128)(2,1)}) custom-call(s32[8]{0:T(128)S(1)} %copy-done, s32[8]{0:T(128)S(1)} %copy-done.1, bf16[2048,384]{1,0:T(8,128)(2,1)} %get-tuple-element.23.mid_grad_hbm, bf16[3584,384]{1,0:T(8,128)(2,1)S(1)} %get-tuple-element.24.state_ref, f32[1,384]{1,0:T(1,128)S(1)} %get-tuple-element.25.out_w_ref), custom_call_target="tpu_custom_call" | custom-call | bytes 25165824 | tf_op jit(solution)/shard_map/backward/pallas_call | solution.py:448
  48.1 0.0 all-to-all-done.1
  48.1 7.5 %all-to-all-start.2 = ((bf16[32,256,384]{2,1,0:T(8,128)(2,1)}), bf16[32,256,384]{2,1,0:T(8,128)(2,1)}, u32[]{:S(2)}, u32[]{:S(2)}) async-start(bf16[32,256,384]{2,1,0:T(8,128)(2,1)} %get-tuple-element.33), calls=%async_computation.2 | async-start | bytes 12582912 | tf_op jit(solution)/shard_map/all_to_all | solution.py:468
  55.7 0.1 slice_convert_fusion
  55.8 0.2 select_reduce_fusion
  55.9 0.1 slice_reduce_fusion
  56.0 3.8 %collective-permute-start.3 = (f32[1,32]{1,0:T(1,128)S(1)}, f32[1,32]{1,0:T(1,128)S(1)}, u32[]{:S(2)}, u32[]{:S(2)}) collective-permute-start(f32[1,32]{1,0:T(1,128)S(1)} %bitcast.56), channel_id=1, source_target_pairs={{0,3},{1,0},{2,1},{3,2},{4,7},{5,4},{6,5},{7,6},{8,11},{9,8},{10,9... | collective-permute-start | bytes 392 | tf_op jit(solution)/shard_map/ppermute | solution.py:36
  59.8 0.0 collective-permute-start.2
  59.8 0.7 collective-permute-start.1
  60.5 0.0 collective-permute-done.3
  60.5 3.6 %collective-permute-done.2 = f32[1,32]{1,0:T(1,128)S(1)} collective-permute-done((f32[1,32]{1,0:T(1,128)S(1)}, f32[1,32]{1,0:T(1,128)S(1)}, u32[]{:S(2)}, u32[]{:S(2)}) %collective-permute-start.2) | collective-permute-done | bytes 160 | tf_op jit(solution)/shard_map/ppermute | solution.py:36
  64.1 0.0 collective-permute-done.1
  64.1 0.6 fusion.6
  64.8 0.2 select_reduce_fusion.3.factor_ref
  65.0 7.4 %weight_grads.1 = bf16[32,56,384]{2,1,0:T(8,128)(2,1)S(1)} custom-call(s32[8]{0:T(128)S(1)} %copy-done, f32[8]{0:T(128)S(1)} %select_reduce_fusion.3.factor_ref, bf16[2048,384]{1,0:T(8,128)(2,1)} %bitcast.52, bf16[2048,384]{1,0:T(8,128)(2,1)} %get-tuple-element.30.low_hbm, bf16[2048,384]{1,0:T(8,128)(2,1)} %get-tuple-element.23.mid_grad_hbm, ...), custom_call_target="tpu_custom_call" | custom-call | bytes 16777216 | tf_op jit(solution)/shard_map/weight_grads/pallas_call | solution.py:480
  72.4 0.1 dynamic-slice_bitcast_fusion
  72.5 1.4 collective-permute-start.4
  73.9 0.7 convert_reduce_fusion
  75.3 0.1 select_reduce_fusion.1
  75.4 0.3 collective-permute-done.4
  75.7 0.2 convert_add_fusion
  75.8 0.1 fusion.2
  75.9 1.5 %collective-permute-start.5 = (bf16[4,56,384]{2,1,0:T(8,128)(2,1)S(1)}, bf16[4,56,384]{2,1,0:T(8,128)(2,1)S(1)}, u32[]{:S(2)}, u32[]{:S(2)}) collective-permute-start(bf16[4,56,384]{2,1,0:T(8,128)(2,1)S(1)} %get-tuple-element.48), channel_id=1, source_target_pairs={{0,32},{32,64},{64,96},{96,0},{1,33},{33,65},{65,97},{97,1},{2,34}... | collective-permute-start | bytes 516104 | tf_op jit(solution)/shard_map/ppermute | solution.py:36
  77.5 2.4 %collective-permute-start.6 = (bf16[4,56,384]{2,1,0:T(8,128)(2,1)S(1)}, bf16[4,56,384]{2,1,0:T(8,128)(2,1)S(1)}, u32[]{:S(2)}, u32[]{:S(2)}) collective-permute-start(bf16[4,56,384]{2,1,0:T(8,128)(2,1)S(1)} %get-tuple-element.47), channel_id=1, source_target_pairs={{0,64},{32,96},{64,0},{96,32},{1,65},{33,97},{65,1},{97,33},{2,66}... | collective-permute-start | bytes 516104 | tf_op jit(solution)/shard_map/ppermute | solution.py:36
  79.9 1.1 collective-permute-start.7
  81.0 0.2 select_reduce_fusion.2.source_ref
  81.2 48.3 %all-to-all-done.2.received_ref = bf16[32,256,384]{2,1,0:T(8,128)(2,1)} async-done(((bf16[32,256,384]{2,1,0:T(8,128)(2,1)}), bf16[32,256,384]{2,1,0:T(8,128)(2,1)}, u32[]{:S(2)}, u32[]{:S(2)}) %all-to-all-start.2) | async-done | bytes 6291488 | tf_op jit(solution)/shard_map/all_to_all | solution.py:468
  129.6 5.8 %place.1 = bf16[4096,384]{1,0:T(8,128)(2,1)} custom-call(s32[16]{0:T(128)S(1)} %select_reduce_fusion.2.source_ref, s32[1]{0:T(128)} %bitcast.14.count_ref, f32[1]{0:T(128)} %bitcast.16.factor_ref, bf16[32,256,384]{2,1,0:T(8,128)(2,1)} %all-to-all-done.2.received_ref), custom_call_target="tpu_custom_call" | custom-call | bytes 25165824 | tf_op jit(solution)/shard_map/place/pallas_call | solution.py:507
  135.4 0.0 collective-permute-done.5
  135.4 0.2 collective-permute-done.6
  135.6 0.0 collective-permute-done.7
  135.6 0.1 convert_add_fusion.1
  135.7 2.9 %collective-permute-start.8 = (bf16[56,384]{1,0:T(8,128)(2,1)S(1)}, bf16[56,384]{1,0:T(8,128)(2,1)S(1)}, u32[]{:S(2)}, u32[]{:S(2)}) collective-permute-start(bf16[56,384]{1,0:T(8,128)(2,1)S(1)} %get-tuple-element.51), channel_id=1, source_target_pairs={{0,8},{8,16},{16,24},{24,0},{1,9},{9,17},{17,25},{25,1},{2,10},{10... | collective-permute-start | bytes 129032 | tf_op jit(solution)/shard_map/ppermute | solution.py:36
  138.6 3.1 %collective-permute-start.9 = (bf16[56,384]{1,0:T(8,128)(2,1)S(1)}, bf16[56,384]{1,0:T(8,128)(2,1)S(1)}, u32[]{:S(2)}, u32[]{:S(2)}) collective-permute-start(bf16[56,384]{1,0:T(8,128)(2,1)S(1)} %get-tuple-element.50), channel_id=1, source_target_pairs={{0,16},{8,24},{16,0},{24,8},{1,17},{9,25},{17,1},{25,9},{2,18},{10... | collective-permute-start | bytes 129032 | tf_op jit(solution)/shard_map/ppermute | solution.py:36
  141.7 0.0 collective-permute-start.10
  141.7 0.2 collective-permute-done.8.first_ref
  142.0 1.6 %collective-permute-done.9.second_ref = bf16[56,384]{1,0:T(8,128)(2,1)S(1)} collective-permute-done((bf16[56,384]{1,0:T(8,128)(2,1)S(1)}, bf16[56,384]{1,0:T(8,128)(2,1)S(1)}, u32[]{:S(2)}, u32[]{:S(2)}) %collective-permute-start.9) | collective-permute-done | bytes 43040 | tf_op jit(solution)/shard_map/ppermute | solution.py:36
  143.6 1.3 collective-permute-done.10.third_ref
  144.9 0.7 finish.1
  (11 shorter events, 0.1 us)
Async XLA Ops:
  0.6 25.2 %copy-start = (s32[8]{0:T(128)S(1)}, s32[8]{0:T(128)}, u32[]{:S(2)}) copy-start(s32[8]{0:T(128)} %valid_ref.5) | copy-start | bytes 100
  0.6 25.2 %copy-start.1 = (s32[8]{0:T(128)S(1)}, s32[8]{0:T(128)}, u32[]{:S(2)}) copy-start(s32[8]{0:T(128)} %owner_ref.3) | copy-start | bytes 100
  21.2 4.7 %copy-start.2 = (bf16[16,56,384]{2,1,0:T(8,128)(2,1)}, bf16[16,56,384]{2,1,0:T(8,128)(2,1)S(1)}, u32[]{:S(2)}) copy-start(bf16[16,56,384]{2,1,0:T(8,128)(2,1)S(1)} %all_to_all.15.own_hbm) | copy-start | bytes 2064388
  21.2 3.8 %collective-permute-start = (bf16[16,56,384]{2,1,0:T(8,128)(2,1)S(1)}, bf16[16,56,384]{2,1,0:T(8,128)(2,1)S(1)}, u32[]{:S(2)}, u32[]{:S(2)}) collective-permute-start(bf16[16,56,384]{2,1,0:T(8,128)(2,1)S(1)} %all_to_all.15.own_hbm), channel_id=1, source_target_pairs={{0,4},{4,0},{1,5},{5,1},{2,6},{6,2},{3,7},{7,3},{8,12},{12,8},{9,1... | collective-permute-start | bytes 2064392 | tf_op jit(solution)/shard_map/ppermute | solution.py:31
  25.0 0.8 copy-start.3
  36.9 11.3 %all-to-all-start.1 = ((f32[32,1,128]{2,1,0:T(1,128)}), f32[32,1,128]{2,1,0:T(1,128)S(1)}, u32[]{:S(2)}, u32[]{:S(2)}) async-start(f32[32,1,128]{2,1,0:T(1,128)} %get-tuple-element.27), calls=%async_computation.1 | async-start | bytes 32768 | tf_op jit(solution)/shard_map/all_to_all | solution.py:446
  48.1 81.4 %all-to-all-start.2 = ((bf16[32,256,384]{2,1,0:T(8,128)(2,1)}), bf16[32,256,384]{2,1,0:T(8,128)(2,1)}, u32[]{:S(2)}, u32[]{:S(2)}) async-start(bf16[32,256,384]{2,1,0:T(8,128)(2,1)} %get-tuple-element.33), calls=%async_computation.2 | async-start | bytes 12582912 | tf_op jit(solution)/shard_map/all_to_all | solution.py:468
  56.0 4.5 %collective-permute-start.3 = (f32[1,32]{1,0:T(1,128)S(1)}, f32[1,32]{1,0:T(1,128)S(1)}, u32[]{:S(2)}, u32[]{:S(2)}) collective-permute-start(f32[1,32]{1,0:T(1,128)S(1)} %bitcast.56), channel_id=1, source_target_pairs={{0,3},{1,0},{2,1},{3,2},{4,7},{5,4},{6,5},{7,6},{8,11},{9,8},{10,9... | collective-permute-start | bytes 392 | tf_op jit(solution)/shard_map/ppermute | solution.py:36
  59.8 4.3 %collective-permute-start.2 = (f32[1,32]{1,0:T(1,128)S(1)}, f32[1,32]{1,0:T(1,128)S(1)}, u32[]{:S(2)}, u32[]{:S(2)}) collective-permute-start(f32[1,32]{1,0:T(1,128)S(1)} %bitcast.57), channel_id=1, source_target_pairs={{0,2},{1,3},{2,0},{3,1},{4,6},{5,7},{6,4},{7,5},{8,10},{9,11},{10,... | collective-permute-start | bytes 392 | tf_op jit(solution)/shard_map/ppermute | solution.py:36
  59.8 4.3 %collective-permute-start.1 = (f32[1,32]{1,0:T(1,128)S(1)}, f32[1,32]{1,0:T(1,128)S(1)}, u32[]{:S(2)}, u32[]{:S(2)}) collective-permute-start(f32[1,32]{1,0:T(1,128)S(1)} %bitcast.58), channel_id=1, source_target_pairs={{0,1},{1,2},{2,3},{3,0},{4,5},{5,6},{6,7},{7,4},{8,9},{9,10},{10,1... | collective-permute-start | bytes 392 | tf_op jit(solution)/shard_map/ppermute | solution.py:36
  72.5 3.2 %collective-permute-start.4 = (bf16[4,4,56,384]{3,2,1,0:T(8,128)(2,1)S(1)}, bf16[4,4,56,384]{3,2,1,0:T(8,128)(2,1)S(1)}, u32[]{:S(2)}, u32[]{:S(2)}) collective-permute-start(bf16[4,4,56,384]{3,2,1,0:T(8,128)(2,1)S(1)} %dynamic-slice_bitcast_fusion), channel_id=1, source_target_pairs={{0,4},{4,0},{1,5},{5,1},{2,6},{6,2},{3,7},{7,3},{8,12},{12,8},{9,1... | collective-permute-start | bytes 2064392 | tf_op jit(solution)/shard_map/ppermute | solution.py:36
  75.9 59.5 %collective-permute-start.5 = (bf16[4,56,384]{2,1,0:T(8,128)(2,1)S(1)}, bf16[4,56,384]{2,1,0:T(8,128)(2,1)S(1)}, u32[]{:S(2)}, u32[]{:S(2)}) collective-permute-start(bf16[4,56,384]{2,1,0:T(8,128)(2,1)S(1)} %get-tuple-element.48), channel_id=1, source_target_pairs={{0,32},{32,64},{64,96},{96,0},{1,33},{33,65},{65,97},{97,1},{2,34}... | collective-permute-start | bytes 516104 | tf_op jit(solution)/shard_map/ppermute | solution.py:36
  77.5 58.1 %collective-permute-start.6 = (bf16[4,56,384]{2,1,0:T(8,128)(2,1)S(1)}, bf16[4,56,384]{2,1,0:T(8,128)(2,1)S(1)}, u32[]{:S(2)}, u32[]{:S(2)}) collective-permute-start(bf16[4,56,384]{2,1,0:T(8,128)(2,1)S(1)} %get-tuple-element.47), channel_id=1, source_target_pairs={{0,64},{32,96},{64,0},{96,32},{1,65},{33,97},{65,1},{97,33},{2,66}... | collective-permute-start | bytes 516104 | tf_op jit(solution)/shard_map/ppermute | solution.py:36
  79.9 55.7 %collective-permute-start.7 = (bf16[4,56,384]{2,1,0:T(8,128)(2,1)S(1)}, bf16[4,56,384]{2,1,0:T(8,128)(2,1)S(1)}, u32[]{:S(2)}, u32[]{:S(2)}) collective-permute-start(bf16[4,56,384]{2,1,0:T(8,128)(2,1)S(1)} %get-tuple-element.46), channel_id=1, source_target_pairs={{0,96},{32,0},{64,32},{96,64},{1,97},{33,1},{65,33},{97,65},{2,98}... | collective-permute-start | bytes 516104 | tf_op jit(solution)/shard_map/ppermute | solution.py:36
  135.7 6.3 %collective-permute-start.8 = (bf16[56,384]{1,0:T(8,128)(2,1)S(1)}, bf16[56,384]{1,0:T(8,128)(2,1)S(1)}, u32[]{:S(2)}, u32[]{:S(2)}) collective-permute-start(bf16[56,384]{1,0:T(8,128)(2,1)S(1)} %get-tuple-element.51), channel_id=1, source_target_pairs={{0,8},{8,16},{16,24},{24,0},{1,9},{9,17},{17,25},{25,1},{2,10},{10... | collective-permute-start | bytes 129032 | tf_op jit(solution)/shard_map/ppermute | solution.py:36
  138.6 5.0 %collective-permute-start.9 = (bf16[56,384]{1,0:T(8,128)(2,1)S(1)}, bf16[56,384]{1,0:T(8,128)(2,1)S(1)}, u32[]{:S(2)}, u32[]{:S(2)}) collective-permute-start(bf16[56,384]{1,0:T(8,128)(2,1)S(1)} %get-tuple-element.50), channel_id=1, source_target_pairs={{0,16},{8,24},{16,0},{24,8},{1,17},{9,25},{17,1},{25,9},{2,18},{10... | collective-permute-start | bytes 129032 | tf_op jit(solution)/shard_map/ppermute | solution.py:36
  141.7 3.2 %collective-permute-start.10 = (bf16[56,384]{1,0:T(8,128)(2,1)S(1)}, bf16[56,384]{1,0:T(8,128)(2,1)S(1)}, u32[]{:S(2)}, u32[]{:S(2)}) collective-permute-start(bf16[56,384]{1,0:T(8,128)(2,1)S(1)} %get-tuple-element.49), channel_id=1, source_target_pairs={{0,24},{8,0},{16,8},{24,16},{1,25},{9,1},{17,9},{25,17},{2,26},{10... | collective-permute-start | bytes 129032 | tf_op jit(solution)/shard_map/ppermute | solution.py:36

commit v6 on v5

--- a/solution.py
+++ b/solution.py
@@ -40,17 +40,16 @@
     return sum((turned(x, axis, r) for r in range(1, lax.axis_size(axis))), x)
 
 
-def scattered(parts, axis, dim):
+def scattered_sum(parts, axis, dim):
     count, index = lax.axis_size(axis), lax.axis_index(axis)
 
     def piece(shift):
         return lax.dynamic_index_in_dim(parts, (index + shift) % count, dim, keepdims=False)
 
-    return [piece(0)] + [turned(piece(r).astype(BF16), axis, r) for r in range(1, count)]
-
-
-def scattered_sum(parts, axis, dim):
-    return sum(piece.astype(F32) for piece in scattered(parts, axis, dim))
+    total = piece(0).astype(F32)
+    for r in range(1, count):
+        total += turned(piece(r), axis, r).astype(F32)
+    return total
 
 
 def gate(value):
@@ -329,10 +328,10 @@
         parts_ref[d] = stage_ref[...].astype(BF16)
 
 
-def finish_kernel(own_ref, first_ref, second_ref, third_ref, conv_ref, mid_ref, out_ref, total_ref):
-    total = own_ref[...]
-    for piece in (first_ref, second_ref, third_ref):
-        total += piece[...].astype(F32)
+def finish_kernel(pieces_ref, conv_ref, mid_ref, out_ref, total_ref):
+    total = pieces_ref[0].astype(F32)
+    for i in range(1, pieces_ref.shape[0]):
+        total += pieces_ref[i].astype(F32)
     total_ref[...] = total * (1.0 / BT)
     for row in range(3 * SHARD):
         conv_ref[row] = total_ref[row : row + 1, :]
@@ -494,16 +493,16 @@
         valid, block_factor, in_hbm(feats[0]), in_hbm(low), in_hbm(mid_grad),
         in_hbm(first_grad), in_vmem(sums),
     )
-    parts = parts.reshape(4, 4, 2, ROWS, D)
-    parts = scattered_sum(parts, "dp_2", 2)
-    pieces = scattered(parts, "dp_0", 0)
-
+    parts = scattered_sum(parts.reshape(chips, 2, ROWS, D), "dp_2", 1).astype(BF16)
     present = jnp.sum((owners == me).astype(jnp.int32), 1)
     rank = jnp.sum(jnp.where(images[None, :] < images[:, None], present[None, :], 0), 1)
     count = jnp.sum(present)
     wanted = jnp.minimum(jnp.arange(capacity, dtype=jnp.int32), count - 1)
     hit = (rank[None, :] == wanted[:, None]) & (present[None, :] > 0)
     source = jnp.sum(jnp.where(hit, images[None, :], 0), 1).astype(jnp.int32)
+    table = (source, count.reshape(1), own_factor)
+    parts, received, table = lax.optimization_barrier((parts, received, table))
+    pieces = lax.all_to_all(parts, CHIPS, split_axis=0, concat_axis=0, tiled=True)
     (placed,) = call(
         place_kernel,
         "place",
@@ -516,13 +515,11 @@
             pltpu.SemaphoreType.DMA((capacity,)),
         ],
         megabytes=24,
-    )(source, count.reshape(1), own_factor, in_hbm(received))
-
-    pieces, placed = lax.optimization_barrier((pieces, placed))
-    pieces = scattered(sum(piece.astype(F32) for piece in pieces), "dp_1", 0)
+    )(*table, in_hbm(received))
+
     conv, mid, out = pl.pallas_call(
         finish_kernel,
-        in_specs=[IN_VMEM] * 4,
+        in_specs=[IN_VMEM],
         out_specs=[IN_VMEM] * 3,
         out_shape=[
             jax.ShapeDtypeStruct((3 * SHARD, 1, D), F32),
@@ -531,7 +528,7 @@
         ],
         scratch_shapes=[pltpu.VMEM((ROWS, D), F32)],
         name="finish",
-    )(*(in_vmem(x) for x in pieces))
+    )(in_vmem(pieces))
     return placed[None], conv.reshape(1, 3, SHARD, D), mid.reshape(1, SHARD, D), out
 
 

time: 147 us -> 150 us (1.020)
  waiting for transfers between devices: 57.3 us -> 61 us
  starting transfers between devices: 30.5 us -> 28.2 us
    ppermute x10 -> x4, starting transfers between devices: 17.1 us -> 7.42 us  [turned(): lax.ppermute(x, axis, [(i, (i + shift) % count) for i in range(count)])]
    all_to_all x0 -> x1, starting transfers between devices: none -> 7.32 us  [per_device(): lax.all_to_all(parts, CHIPS, split_axis=0, concat_axis=0, tiled=True)]
    all_to_all x0 -> x1, waiting for transfers between devices: none -> 5.19 us  [per_device(): lax.all_to_all(parts, CHIPS, split_axis=0, concat_axis=0, tiled=True)]
    ppermute x10 -> x4, waiting for transfers between devices: 7.19 us -> 2.17 us  [turned(): lax.ppermute(x, axis, [(i, (i + shift) % count) for i in range(count)])]
    all_to_all x1, waiting for transfers between devices: 48.3 us -> 51.9 us  [per_device(): lax.all_to_all(slots, DP, split_axis=0, concat_axis=0, tiled=True)]
  transfers between devices with their start and end apart: 13 -> 8, of which waited for: 8 -> 6; matrix products, arithmetic and copies ran while one was open for 2% -> 2% of each run, Pallas kernels for 14% -> 15%
where the time goes in v6:
time: 150 us; the launch traced here: 149 us
  waiting for transfers between devices  61 us (41%)
  Pallas kernels  34.3 us (23%)
  starting transfers between devices  28.2 us (19%)
  blocking collectives  19.6 us (13%)
  other arithmetic  3.19 us (2%)
    all_to_all x1, waiting for transfers between devices, per_device(): lax.all_to_all(slots, DP, split_axis=0, concat_axis=0, tiled=True)  51.9 us
    all_to_all x1, blocking collectives, per_device(): own = lax.all_to_all(copies, CHIPS, split_axis=0, concat_axis=0, tiled=True)  19.6 us
    pallas_call x1, Pallas kernels, per_device(): call(forward_kernel, 'forward', [IN_SMEM, IN_SMEM, IN_SMEM, IN_HBM, IN_HB...  11.1 us
    all_to_all x1, starting transfers between devices, per_device(): lax.all_to_all(slots, DP, split_axis=0, concat_axis=0, tiled=True)  7.59 us
    pallas_call x1, Pallas kernels, per_device(): call(weight_kernel, 'weight_grads', [IN_SMEM, IN_SMEM, IN_HBM, IN_HBM, IN...  7.46 us
    pallas_call x1, Pallas kernels, per_device(): call(backward_kernel, 'backward', [IN_SMEM, IN_SMEM, IN_HBM, IN_VMEM, IN_...  7.44 us
    ppermute x4, starting transfers between devices, turned(): lax.ppermute(x, axis, [(i, (i + shift) % count) for i in range(count)])  7.42 us
    all_to_all x1, starting transfers between devices, per_device(): lax.all_to_all(parts, CHIPS, split_axis=0, concat_axis=0, tiled=True)  7.32 us
  transfers between devices with their start and end apart: 8, of which 6 were waited for; matrix products, arithmetic and copies ran while one was open for 2% of the time, Pallas kernels for 15%

profile of v6, /device:TPU:1, one launch (start us, length us, event | category | flops | bytes accessed | tf_op | source)
XLA Modules:
  0.0 148.8 jit_solution(7268480380990814180)
XLA Ops:
  0.6 0.0 copy-start
  0.6 0.0 copy-start.1
  0.7 0.9 pack.1
  1.6 19.6 %all_to_all.20.own_hbm = bf16[16,56,384]{2,1,0:T(8,128)(2,1)S(1)} all-to-all(bf16[16,56,384]{2,1,0:T(8,128)(2,1)S(1)} %pack.1), channel_id=1, replica_groups=mesh['dp_0'=4,'dp_1'=4,'dp_2'=2,'head'=4] {'dp_0','dp_1'}, dimensions={0} | all-to-all | bytes 1376256 | tf_op jit(solution)/shard_map/all_to_all | solution.py:416
  21.2 0.0 copy-start.2
  21.2 2.0 %collective-permute-start = (bf16[16,56,384]{2,1,0:T(8,128)(2,1)S(1)}, bf16[16,56,384]{2,1,0:T(8,128)(2,1)S(1)}, u32[]{:S(2)}, u32[]{:S(2)}) collective-permute-start(bf16[16,56,384]{2,1,0:T(8,128)(2,1)S(1)} %all_to_all.20.own_hbm), channel_id=1, source_target_pairs={{0,4},{4,0},{1,5},{5,1},{2,6},{6,2},{3,7},{7,3},{8,12},{12,8},{9,1... | collective-permute-start | bytes 2064392 | tf_op jit(solution)/shard_map/ppermute | solution.py:31
  23.2 1.8 %collective-permute-done.other_hbm = bf16[16,56,384]{2,1,0:T(8,128)(2,1)S(1)} collective-permute-done((bf16[16,56,384]{2,1,0:T(8,128)(2,1)S(1)}, bf16[16,56,384]{2,1,0:T(8,128)(2,1)S(1)}, u32[]{:S(2)}, u32[]{:S(2)}) %collective-permute-start) | collective-permute-done | bytes 688160 | tf_op jit(solution)/shard_map/ppermute | solution.py:31
  25.0 0.0 copy-start.3
  25.0 0.8 copy-done.3
  25.8 0.0 copy-done.2
  25.8 0.0 copy-done
  25.8 0.0 copy-done.1
  25.8 11.1 %forward.1 = (bf16[2048,384]{1,0:T(8,128)(2,1)}, bf16[2048,384]{1,0:T(8,128)(2,1)}, bf16[3584,384]{1,0:T(8,128)(2,1)S(1)}, f32[8,384]{1,0:T(8,128)S(1)}, f32[1,3...) custom-call(s32[8]{0:T(128)S(1)} %copy-done, s32[8]{0:T(128)S(1)} %copy-done.1, s32[1]{0:T(128)} %bitcast.core_ref, ...), custom_call_target="tpu_custom_call" | custom-call | tf_op jit(solution)/shard_map/forward/pallas_call | solution.py:419
  36.9 3.9 %all-to-all-start.1 = ((f32[32,1,128]{2,1,0:T(1,128)}), f32[32,1,128]{2,1,0:T(1,128)S(1)}, u32[]{:S(2)}, u32[]{:S(2)}) async-start(f32[32,1,128]{2,1,0:T(1,128)} %get-tuple-element.27), calls=%async_computation.1 | async-start | bytes 32768 | tf_op jit(solution)/shard_map/all_to_all | solution.py:445
  40.8 7.4 %backward.1 = (bf16[2048,384]{1,0:T(8,128)(2,1)}, bf16[32,256,384]{2,1,0:T(8,128)(2,1)}) custom-call(s32[8]{0:T(128)S(1)} %copy-done, s32[8]{0:T(128)S(1)} %copy-done.1, bf16[2048,384]{1,0:T(8,128)(2,1)} %get-tuple-element.23.mid_grad_hbm, bf16[3584,384]{1,0:T(8,128)(2,1)S(1)} %get-tuple-element.24.state_ref, f32[1,384]{1,0:T(1,128)S(1)} %get-tuple-element.25.out_w_ref), custom_call_target="tpu_custom_call" | custom-call | bytes 25165824 | tf_op jit(solution)/shard_map/backward/pallas_call | solution.py:447
  48.3 0.0 all-to-all-done.1
  48.3 7.6 %all-to-all-start.2 = ((bf16[32,256,384]{2,1,0:T(8,128)(2,1)}), bf16[32,256,384]{2,1,0:T(8,128)(2,1)}, u32[]{:S(2)}, u32[]{:S(2)}) async-start(bf16[32,256,384]{2,1,0:T(8,128)(2,1)} %get-tuple-element.33), calls=%async_computation.2 | async-start | bytes 12582912 | tf_op jit(solution)/shard_map/all_to_all | solution.py:467
  55.9 0.1 slice_convert_fusion
  56.0 0.2 select_reduce_fusion
  56.1 0.1 slice_reduce_fusion
  56.2 1.7 %collective-permute-start.1 = (f32[1,32]{1,0:T(1,128)S(1)}, f32[1,32]{1,0:T(1,128)S(1)}, u32[]{:S(2)}, u32[]{:S(2)}) collective-permute-start(f32[1,32]{1,0:T(1,128)S(1)} %bitcast.40), channel_id=1, source_target_pairs={{0,1},{1,2},{2,3},{3,0},{4,5},{5,6},{6,7},{7,4},{8,9},{9,10},{10,1... | collective-permute-start | bytes 392 | tf_op jit(solution)/shard_map/ppermute | solution.py:36
  57.9 3.3 %collective-permute-start.2 = (f32[1,32]{1,0:T(1,128)S(1)}, f32[1,32]{1,0:T(1,128)S(1)}, u32[]{:S(2)}, u32[]{:S(2)}) collective-permute-start(f32[1,32]{1,0:T(1,128)S(1)} %bitcast.41), channel_id=1, source_target_pairs={{0,2},{1,3},{2,0},{3,1},{4,6},{5,7},{6,4},{7,5},{8,10},{9,11},{10,... | collective-permute-start | bytes 392 | tf_op jit(solution)/shard_map/ppermute | solution.py:36
  61.2 0.7 collective-permute-start.3
  61.9 0.0 collective-permute-done.1
  61.9 0.6 collective-permute-done.2
  62.5 1.5 collective-permute-done.3
  64.0 0.6 fusion.1
  64.6 0.2 select_reduce_fusion.3.factor_ref
  64.8 7.5 %weight_grads.1 = bf16[32,56,384]{2,1,0:T(8,128)(2,1)S(1)} custom-call(s32[8]{0:T(128)S(1)} %copy-done, f32[8]{0:T(128)S(1)} %select_reduce_fusion.3.factor_ref, bf16[2048,384]{1,0:T(8,128)(2,1)} %bitcast.36, bf16[2048,384]{1,0:T(8,128)(2,1)} %get-tuple-element.30.low_hbm, bf16[2048,384]{1,0:T(8,128)(2,1)} %get-tuple-element.23.mid_grad_hbm, ...), custom_call_target="tpu_custom_call" | custom-call | bytes 16777216 | tf_op jit(solution)/shard_map/weight_grads/pallas_call | solution.py:479
  72.3 0.1 dynamic-slice_bitcast_fusion
  72.4 1.7 %collective-permute-start.4 = (bf16[16,56,384]{2,1,0:T(8,128)(2,1)S(1)}, bf16[16,56,384]{2,1,0:T(8,128)(2,1)S(1)}, u32[]{:S(2)}, u32[]{:S(2)}) collective-permute-start(bf16[16,56,384]{2,1,0:T(8,128)(2,1)S(1)} %dynamic-slice_bitcast_fusion), channel_id=1, source_target_pairs={{0,4},{4,0},{1,5},{5,1},{2,6},{6,2},{3,7},{7,3},{8,12},{12,8},{9,1... | collective-permute-start | bytes 2064392 | tf_op jit(solution)/shard_map/ppermute | solution.py:36
  74.1 0.7 convert_reduce_fusion
  75.4 0.1 select_reduce_fusion.1
  75.6 0.2 select_reduce_fusion.2.source_ref
  75.7 0.1 collective-permute-done.4
  75.8 1.1 fusion
  76.9 51.9 %all-to-all-done.2.received_ref = bf16[32,256,384]{2,1,0:T(8,128)(2,1)} async-done(((bf16[32,256,384]{2,1,0:T(8,128)(2,1)}), bf16[32,256,384]{2,1,0:T(8,128)(2,1)}, u32[]{:S(2)}, u32[]{:S(2)}) %all-to-all-start.2) | async-done | bytes 6291488 | tf_op jit(solution)/shard_map/all_to_all | solution.py:467
  128.8 7.3 %all-to-all-start.3 = ((bf16[16,56,384]{2,1,0:T(8,128)(2,1)}), bf16[16,56,384]{2,1,0:T(8,128)(2,1)S(1)}, u32[]{:S(2)}, u32[]{:S(2)}) async-start(bf16[16,56,384]{2,1,0:T(8,128)(2,1)} %fusion), calls=%async_computation.3 | async-start | bytes 1376256 | tf_op jit(solution)/shard_map/all_to_all | solution.py:505
  136.1 6.7 %place.1 = bf16[4096,384]{1,0:T(8,128)(2,1)} custom-call(s32[16]{0:T(128)S(1)} %select_reduce_fusion.2.source_ref, s32[1]{0:T(128)} %bitcast.10.count_ref, f32[1]{0:T(128)} %bitcast.12.factor_ref, bf16[32,256,384]{2,1,0:T(8,128)(2,1)} %all-to-all-done.2.received_ref), custom_call_target="tpu_custom_call" | custom-call | bytes 25165824 | tf_op jit(solution)/shard_map/place/pallas_call | solution.py:506
  142.8 5.2 %all-to-all-done.3.pieces_ref = bf16[16,56,384]{2,1,0:T(8,128)(2,1)S(1)} async-done(((bf16[16,56,384]{2,1,0:T(8,128)(2,1)}), bf16[16,56,384]{2,1,0:T(8,128)(2,1)S(1)}, u32[]{:S(2)}, u32[]{:S(2)}) %all-to-all-start.3) | async-done | bytes 688160 | tf_op jit(solution)/shard_map/all_to_all | solution.py:505
  148.0 0.7 finish.1
  (3 shorter events, 0.0 us)
Async XLA Ops:
  0.6 25.2 %copy-start = (s32[8]{0:T(128)S(1)}, s32[8]{0:T(128)}, u32[]{:S(2)}) copy-start(s32[8]{0:T(128)} %valid_ref.5) | copy-start | bytes 100
  0.6 25.2 %copy-start.1 = (s32[8]{0:T(128)S(1)}, s32[8]{0:T(128)}, u32[]{:S(2)}) copy-start(s32[8]{0:T(128)} %owner_ref.3) | copy-start | bytes 100
  21.2 4.7 %copy-start.2 = (bf16[16,56,384]{2,1,0:T(8,128)(2,1)}, bf16[16,56,384]{2,1,0:T(8,128)(2,1)S(1)}, u32[]{:S(2)}) copy-start(bf16[16,56,384]{2,1,0:T(8,128)(2,1)S(1)} %all_to_all.20.own_hbm) | copy-start | bytes 2064388
  21.2 3.8 %collective-permute-start = (bf16[16,56,384]{2,1,0:T(8,128)(2,1)S(1)}, bf16[16,56,384]{2,1,0:T(8,128)(2,1)S(1)}, u32[]{:S(2)}, u32[]{:S(2)}) collective-permute-start(bf16[16,56,384]{2,1,0:T(8,128)(2,1)S(1)} %all_to_all.20.own_hbm), channel_id=1, source_target_pairs={{0,4},{4,0},{1,5},{5,1},{2,6},{6,2},{3,7},{7,3},{8,12},{12,8},{9,1... | collective-permute-start | bytes 2064392 | tf_op jit(solution)/shard_map/ppermute | solution.py:31
  25.0 0.9 copy-start.3
  36.9 11.3 %all-to-all-start.1 = ((f32[32,1,128]{2,1,0:T(1,128)}), f32[32,1,128]{2,1,0:T(1,128)S(1)}, u32[]{:S(2)}, u32[]{:S(2)}) async-start(f32[32,1,128]{2,1,0:T(1,128)} %get-tuple-element.27), calls=%async_computation.1 | async-start | bytes 32768 | tf_op jit(solution)/shard_map/all_to_all | solution.py:445
  48.3 80.5 %all-to-all-start.2 = ((bf16[32,256,384]{2,1,0:T(8,128)(2,1)}), bf16[32,256,384]{2,1,0:T(8,128)(2,1)}, u32[]{:S(2)}, u32[]{:S(2)}) async-start(bf16[32,256,384]{2,1,0:T(8,128)(2,1)} %get-tuple-element.33), calls=%async_computation.2 | async-start | bytes 12582912 | tf_op jit(solution)/shard_map/all_to_all | solution.py:467
  56.2 5.7 %collective-permute-start.1 = (f32[1,32]{1,0:T(1,128)S(1)}, f32[1,32]{1,0:T(1,128)S(1)}, u32[]{:S(2)}, u32[]{:S(2)}) collective-permute-start(f32[1,32]{1,0:T(1,128)S(1)} %bitcast.40), channel_id=1, source_target_pairs={{0,1},{1,2},{2,3},{3,0},{4,5},{5,6},{6,7},{7,4},{8,9},{9,10},{10,1... | collective-permute-start | bytes 392 | tf_op jit(solution)/shard_map/ppermute | solution.py:36
  57.9 4.6 %collective-permute-start.2 = (f32[1,32]{1,0:T(1,128)S(1)}, f32[1,32]{1,0:T(1,128)S(1)}, u32[]{:S(2)}, u32[]{:S(2)}) collective-permute-start(f32[1,32]{1,0:T(1,128)S(1)} %bitcast.41), channel_id=1, source_target_pairs={{0,2},{1,3},{2,0},{3,1},{4,6},{5,7},{6,4},{7,5},{8,10},{9,11},{10,... | collective-permute-start | bytes 392 | tf_op jit(solution)/shard_map/ppermute | solution.py:36
  61.2 2.8 %collective-permute-start.3 = (f32[1,32]{1,0:T(1,128)S(1)}, f32[1,32]{1,0:T(1,128)S(1)}, u32[]{:S(2)}, u32[]{:S(2)}) collective-permute-start(f32[1,32]{1,0:T(1,128)S(1)} %bitcast.42), channel_id=1, source_target_pairs={{0,3},{1,0},{2,1},{3,2},{4,7},{5,4},{6,5},{7,6},{8,11},{9,8},{10,9... | collective-permute-start | bytes 392 | tf_op jit(solution)/shard_map/ppermute | solution.py:36
  72.4 3.5 %collective-permute-start.4 = (bf16[16,56,384]{2,1,0:T(8,128)(2,1)S(1)}, bf16[16,56,384]{2,1,0:T(8,128)(2,1)S(1)}, u32[]{:S(2)}, u32[]{:S(2)}) collective-permute-start(bf16[16,56,384]{2,1,0:T(8,128)(2,1)S(1)} %dynamic-slice_bitcast_fusion), channel_id=1, source_target_pairs={{0,4},{4,0},{1,5},{5,1},{2,6},{6,2},{3,7},{7,3},{8,12},{12,8},{9,1... | collective-permute-start | bytes 2064392 | tf_op jit(solution)/shard_map/ppermute | solution.py:36
  128.8 19.2 %all-to-all-start.3 = ((bf16[16,56,384]{2,1,0:T(8,128)(2,1)}), bf16[16,56,384]{2,1,0:T(8,128)(2,1)S(1)}, u32[]{:S(2)}, u32[]{:S(2)}) async-start(bf16[16,56,384]{2,1,0:T(8,128)(2,1)} %fusion), calls=%async_computation.3 | async-start | bytes 1376256 | tf_op jit(solution)/shard_map/all_to_all | solution.py:505

commit v7 on v5

--- a/solution.py
+++ b/solution.py
@@ -17,6 +17,7 @@
 EXTRA = 4 * SHARD
 ROWS = 56
 GROUP = 4
+HALF = BT // 2
 LOG_2 = 0.6931471805599453
 VMEM_LIMIT = 20 * 1024 * 1024
 
@@ -40,17 +41,21 @@
     return sum((turned(x, axis, r) for r in range(1, lax.axis_size(axis))), x)
 
 
-def scattered(parts, axis, dim):
+def shares(parts, axis, dim):
     count, index = lax.axis_size(axis), lax.axis_index(axis)
 
-    def piece(shift):
+    def share(shift):
         return lax.dynamic_index_in_dim(parts, (index + shift) % count, dim, keepdims=False)
 
-    return [piece(0)] + [turned(piece(r).astype(BF16), axis, r) for r in range(1, count)]
-
-
-def scattered_sum(parts, axis, dim):
-    return sum(piece.astype(F32) for piece in scattered(parts, axis, dim))
+    return [share(0)] + [share(r).astype(BF16) for r in range(1, count)]
+
+
+def delivered(own, *others, axis):
+    return [own] + [turned(other, axis, r) for r, other in enumerate(others, 1)]
+
+
+def added(pieces):
+    return sum(piece.astype(F32) for piece in pieces)
 
 
 def gate(value):
@@ -125,7 +130,7 @@
 
 def forward_kernel(
     valid_ref, owner_ref, core_ref, feats_ref, own_hbm, other_hbm,
-    low_out, mid_grad_out, state_ref, sums_ref, out_w_ref, extras_ref, totals_ref,
+    low_out, mid_grad_out, weights_out, state_ref, sums_ref, out_w_ref, extras_ref, totals_ref,
     raw_ref, own_ref, other_ref, low_ref, mid_grad_ref, wide_ref, sems, out_sems, weight_sems,
 ):
     local = valid_ref.shape[0]
@@ -163,6 +168,8 @@
         unpack(0, other_ref)
 
     weights_ref[...] = wide_ref[...].astype(BF16)
+    departures = [pltpu.make_async_copy(weights_ref, weights_out, weight_sems.at[0])]
+    departures[0].start()
     devices = extras_ref.shape[0]
     column = lax.broadcasted_iota(jnp.int32, (128, D), 1).astype(F32)
     place = lax.broadcasted_iota(jnp.int32, (128, D), 0).astype(F32)
@@ -175,7 +182,6 @@
 
     lane = lax.broadcasted_iota(jnp.int32, (1, 128), 1)
     totals = jnp.zeros((1, 128), F32)
-    departures = []
     for n, (j, group) in enumerate(chunks(local)):
         rows = pl.ds(j * BT, group * BT)
         arrivals[2 + n].wait()
@@ -209,10 +215,39 @@
             sums_ref[j + i : j + i + 1, :] = block
             block_sum = jnp.sum(block * out_w, 1, keepdims=True)
             totals += jnp.where(lane == owner_ref[j + i], block_sum, 0.0)
-    for device in range(devices):
-        totals_ref[device] = totals
+    for chip in range(devices // 2):
+        totals_ref[chip] = totals
     for copy in departures:
         copy.wait()
+
+
+def input_grad(grad, weights_ref, keep, half):
+    blocks = grad.shape[0] // BT
+    before, after = neighbours(grad, block_place(blocks * BT), BT - 1)
+
+    def part(x):
+        starts = [i * BT + half * HALF for i in range(blocks)]
+        return jnp.concatenate([x[at : at + HALF] for at in starts], axis=0)
+
+    def product(x, k):
+        return lax.dot_general(
+            part(x), weight(weights_ref, k), OVER_LAST, preferred_element_type=F32
+        )
+
+    total = product(grad.astype(BF16), 1) + product(after, 0) + product(before, 2)
+    return jnp.where(part(keep) > 0, total, 0.0).astype(BF16)
+
+
+def send_half(total, first, ready_ref, slots_ref, owner_ref, sems):
+    copies = []
+    for i in range(total.shape[0] // HALF):
+        ready_ref[first + i] = total[i * HALF : (i + 1) * HALF]
+        copy = pltpu.make_async_copy(
+            ready_ref.at[first + i], slots_ref.at[owner_ref[first + i]], sems.at[first + i]
+        )
+        copy.start()
+        copies.append(copy)
+    return copies
 
 
 def backward_kernel(
@@ -221,7 +256,6 @@
 ):
     local = valid_ref.shape[0]
     slope_ref, weights_ref = (state_ref.at[rows] for rows in state_rows(local))
-    place = block_place(GROUP * BT)
     arrivals, copies = [], []
     for j in range(0, local, GROUP):
         rows = pl.ds(j * BT, GROUP * BT)
@@ -238,29 +272,37 @@
             mid_grad_ref[rows, :], weight(weights_ref, 3), OVER_LAST, preferred_element_type=F32
         )
         grad = (grad + jnp.where(keep, out_w_ref[...], 0.0)) * slope_ref[rows, :].astype(F32)
-        before, after = neighbours(grad, place, BT - 1)
-        low = grad.astype(BF16)
-        first_grad_ref[rows, :] = low
-        total = lax.dot_general(low, weight(weights_ref, 1), OVER_LAST, preferred_element_type=F32)
-        total += lax.dot_general(
-            after, weight(weights_ref, 0), OVER_LAST, preferred_element_type=F32
-        )
-        total += lax.dot_general(
-            before, weight(weights_ref, 2), OVER_LAST, preferred_element_type=F32
-        )
-        total = jnp.where(keep, total, 0.0).astype(BF16)
-        for i in range(GROUP):
-            ready_ref[j + i] = total[i * BT : (i + 1) * BT]
-            copy = pltpu.make_async_copy(
-                ready_ref.at[j + i], slots_ref.at[owner_ref[j + i]], sems.at[j + i]
-            )
-            copy.start()
-            copies.append(copy)
+        first_grad_ref[rows, :] = grad.astype(BF16)
         copy = pltpu.make_async_copy(
             first_grad_ref.at[rows], first_grad_out.at[rows], out_sems.at[j // GROUP]
         )
         copy.start()
         copies.append(copy)
+        total = input_grad(grad, weights_ref, keep.astype(F32), 0)
+        copies += send_half(total, j, ready_ref, slots_ref, owner_ref, sems)
+    for copy in copies:
+        copy.wait()
+
+
+def second_half_kernel(
+    valid_ref, owner_ref, first_grad_hbm, weights_hbm,
+    slots_ref, first_grad_ref, weights_ref, ready_ref, sems, in_sems,
+):
+    local = valid_ref.shape[0]
+    arrivals = [
+        pltpu.make_async_copy(first_grad_hbm, first_grad_ref, in_sems.at[0]),
+        pltpu.make_async_copy(weights_hbm, weights_ref, in_sems.at[1]),
+    ]
+    for copy in arrivals:
+        copy.start()
+    for copy in arrivals:
+        copy.wait()
+    copies = []
+    for j in range(0, local, GROUP):
+        rows = pl.ds(j * BT, GROUP * BT)
+        keep = row_mask(valid_ref, j, GROUP).astype(F32)
+        total = input_grad(first_grad_ref[rows, :].astype(F32), weights_ref, keep, 1)
+        copies += send_half(total, j, ready_ref, slots_ref, owner_ref, sems)
     for copy in copies:
         copy.wait()
 
@@ -341,27 +383,44 @@
     out_ref[...] = total_ref[EXTRA : EXTRA + 1, 0:SHARD]
 
 
-def place_kernel(
-    source_ref, count_ref, factor_ref, received_ref, placed_ref, raw_ref, ready_ref, in_sems, out_sems
+def place_half(half, read, count_ref, factor_ref, placed_ref, ready_ref, sems):
+    copies = []
+    for slot in range(ready_ref.shape[0]):
+        factor = jnp.where(slot < count_ref[0], factor_ref[0], 0.0)
+        ready_ref[slot] = (read(slot).astype(F32) * factor).astype(BF16)
+        rows = pl.ds(slot * BT + half * HALF, HALF)
+        copy = pltpu.make_async_copy(ready_ref.at[slot], placed_ref.at[rows], sems.at[slot])
+        copy.start()
+        copies.append(copy)
+    for copy in copies:
+        copy.wait()
+
+
+def place_first_kernel(
+    source_ref, count_ref, factor_ref, received_hbm, placed_ref, ready_ref, sems, raw_ref, in_sems
 ):
-    capacity = source_ref.shape[0]
-    arrivals, departures = [], []
-    for slot in range(capacity):
+    arrivals = []
+    for slot in range(raw_ref.shape[0]):
         copy = pltpu.make_async_copy(
-            received_ref.at[source_ref[slot]], raw_ref.at[slot], in_sems.at[slot]
+            received_hbm.at[source_ref[slot]], raw_ref.at[slot], in_sems.at[slot]
         )
         copy.start()
         arrivals.append(copy)
-    for slot in range(capacity):
+
+    def read(slot):
         arrivals[slot].wait()
-        factor = jnp.where(slot < count_ref[0], factor_ref[0], 0.0)
-        ready_ref[slot] = (raw_ref[slot].astype(F32) * factor).astype(BF16)
-        rows = pl.ds(slot * BT, BT)
-        copy = pltpu.make_async_copy(ready_ref.at[slot], placed_ref.at[rows], out_sems.at[slot])
-        copy.start()
-        departures.append(copy)
-    for copy in departures:
-        copy.wait()
+        return raw_ref[slot]
+
+    place_half(0, read, count_ref, factor_ref, placed_ref, ready_ref, sems)
+
+
+def place_second_kernel(
+    source_ref, count_ref, factor_ref, received_ref, begun_ref, placed_ref, ready_ref, sems
+):
+    def read(slot):
+        return received_ref[source_ref[slot]]
+
+    place_half(1, read, count_ref, factor_ref, placed_ref, ready_ref, sems)
 
 
 def in_hbm(x):
@@ -372,7 +431,7 @@
     return pltpu.with_memory_space_constraint(x, pltpu.VMEM)
 
 
-def call(kernel, name, in_specs, outs, scratch=(), megabytes=0):
+def call(kernel, name, in_specs, outs, scratch=(), megabytes=0, aliases={}):
     return pl.pallas_call(
         kernel,
         in_specs=in_specs,
@@ -381,6 +440,7 @@
             (pltpu.HBM if spec is IN_HBM else pltpu.VMEM)(shape, dtype) for spec, shape, dtype in outs
         ],
         scratch_shapes=list(scratch),
+        input_output_aliases=aliases,
         compiler_params=pltpu.CompilerParams(vmem_limit_bytes=VMEM_LIMIT),
         cost_estimate=pl.CostEstimate(
             flops=0, transcendentals=0, bytes_accessed=megabytes * 1024 * 1024
@@ -417,18 +477,19 @@
     own = lax.all_to_all(copies, CHIPS, split_axis=0, concat_axis=0, tiled=True)
     other = swapped(own)
 
-    low, mid_grad, state, sums, out_w, extras, totals = call(
+    low, mid_grad, weights, state, sums, out_w, extras, totals = call(
         forward_kernel,
         "forward",
         [IN_SMEM, IN_SMEM, IN_SMEM, IN_HBM, IN_HBM, IN_HBM],
         [
             (IN_HBM, (tokens_here, D), BF16),
             (IN_HBM, (tokens_here, D), BF16),
+            (IN_HBM, (4 * D, D), BF16),
             (IN_VMEM, (tokens_here + 4 * D, D), BF16),
             (IN_VMEM, (local, D), F32),
             (IN_VMEM, (1, D), F32),
             (IN_VMEM, (devices, 128), F32),
-            (IN_VMEM, (devices, 1, 128), F32),
+            (IN_VMEM, (chips, 1, 128), F32),
         ],
         [
             pltpu.VMEM((tokens_here, D), BF16),
@@ -443,31 +504,47 @@
         ],
     )(valid, owner_map, core, in_hbm(feats[0]), in_hbm(own), in_hbm(other))
 
-    totals = lax.all_to_all(totals, DP, split_axis=0, concat_axis=0, tiled=True)
-
-    first_grad, slots = call(
+    totals = lax.all_to_all(totals, CHIPS, split_axis=0, concat_axis=0, tiled=True)
+
+    first_grad, first_slots = call(
         backward_kernel,
         "backward",
         [IN_SMEM, IN_SMEM, IN_HBM, IN_VMEM, IN_VMEM],
         [
             (IN_HBM, (tokens_here, D), BF16),
-            (IN_HBM, (devices, BT, D), BF16),
+            (IN_HBM, (devices, HALF, D), BF16),
         ],
         [
             pltpu.VMEM((tokens_here, D), BF16),
             pltpu.VMEM((tokens_here, D), BF16),
-            pltpu.VMEM((local, BT, D), BF16),
+            pltpu.VMEM((local, HALF, D), BF16),
             pltpu.SemaphoreType.DMA((local,)),
             pltpu.SemaphoreType.DMA((local // GROUP,)),
             pltpu.SemaphoreType.DMA((local // GROUP,)),
         ],
-        megabytes=24,
+        megabytes=16,
     )(valid, owner_map, in_hbm(mid_grad), in_vmem(state), in_vmem(out_w))
 
-    slots, totals = lax.optimization_barrier((slots, totals))
-    received = lax.all_to_all(slots, DP, split_axis=0, concat_axis=0, tiled=True)
-
-    totals = total_over(jnp.sum(totals[:, 0, :devices], 0)[None], "head")[0]
+    first_slots, totals = lax.optimization_barrier((first_slots, totals))
+    first_received = lax.all_to_all(first_slots, DP, split_axis=0, concat_axis=0, tiled=True)
+
+    (second_slots,) = call(
+        second_half_kernel,
+        "second_half",
+        [IN_SMEM, IN_SMEM, IN_HBM, IN_HBM],
+        [(IN_HBM, (devices, HALF, D), BF16)],
+        [
+            pltpu.VMEM((tokens_here, D), BF16),
+            pltpu.VMEM((4 * D, D), BF16),
+            pltpu.VMEM((local, HALF, D), BF16),
+            pltpu.SemaphoreType.DMA((local,)),
+            pltpu.SemaphoreType.DMA((2,)),
+        ],
+        megabytes=16,
+    )(valid, owner_map, in_hbm(first_grad), in_hbm(weights))
+
+    totals = total_over(jnp.sum(totals[:, 0, :devices], 0)[None], "dp_2")
+    totals = total_over(totals, "head")[0]
     members = (owner_map[:, None] == images[None, :]).astype(F32)
     owners = extras[:, SHARD : SHARD + local].astype(jnp.int32)
     valids = extras[:, SHARD + local : SHARD + 2 * local]
@@ -495,8 +572,9 @@
         in_hbm(first_grad), in_vmem(sums),
     )
     parts = parts.reshape(4, 4, 2, ROWS, D)
-    parts = scattered_sum(parts, "dp_2", 2)
-    pieces = scattered(parts, "dp_0", 0)
+    parts = added(delivered(*shares(parts, "dp_2", 2), axis="dp_2"))
+    ready = shares(parts, "dp_0", 0)
+    pieces = delivered(*ready, axis="dp_0")
 
     present = jnp.sum((owners == me).astype(jnp.int32), 1)
     rank = jnp.sum(jnp.where(images[None, :] < images[:, None], present[None, :], 0), 1)
@@ -504,22 +582,33 @@
     wanted = jnp.minimum(jnp.arange(capacity, dtype=jnp.int32), count - 1)
     hit = (rank[None, :] == wanted[:, None]) & (present[None, :] > 0)
     source = jnp.sum(jnp.where(hit, images[None, :], 0), 1).astype(jnp.int32)
+    half_slots = pltpu.VMEM((capacity, HALF, D), BF16)
+    slot_sems = pltpu.SemaphoreType.DMA((capacity,))
+    result = [(IN_HBM, (capacity * BT, D), BF16)]
+    second_slots, first_received, source, own_factor, _ = lax.optimization_barrier(
+        (second_slots, first_received, source, own_factor, ready)
+    )
+    second_received = lax.all_to_all(second_slots, DP, split_axis=0, concat_axis=0, tiled=True)
+    table = (source, count.reshape(1), own_factor)
     (placed,) = call(
-        place_kernel,
-        "place",
+        place_first_kernel,
+        "place_first",
         [IN_SMEM, IN_SMEM, IN_SMEM, IN_HBM],
-        [(IN_HBM, (capacity * BT, D), BF16)],
-        [
-            pltpu.VMEM((capacity, BT, D), BF16),
-            pltpu.VMEM((capacity, BT, D), BF16),
-            pltpu.SemaphoreType.DMA((capacity,)),
-            pltpu.SemaphoreType.DMA((capacity,)),
-        ],
-        megabytes=24,
-    )(source, count.reshape(1), own_factor, in_hbm(received))
-
+        result,
+        [half_slots, slot_sems, half_slots, slot_sems],
+        megabytes=12,
+    )(*table, in_hbm(first_received))
+    pieces = delivered(*shares(added(pieces), "dp_1", 0), axis="dp_1")
     pieces, placed = lax.optimization_barrier((pieces, placed))
-    pieces = scattered(sum(piece.astype(F32) for piece in pieces), "dp_1", 0)
+    (placed,) = call(
+        place_second_kernel,
+        "place_second",
+        [IN_SMEM, IN_SMEM, IN_SMEM, IN_VMEM, IN_HBM],
+        result,
+        [half_slots, slot_sems],
+        megabytes=12,
+        aliases={4: 0},
+    )(*table, in_vmem(second_received), in_hbm(placed))
     conv, mid, out = pl.pallas_call(
         finish_kernel,
         in_specs=[IN_VMEM] * 4,

time: 147 us -> 150 us (1.020)
  waiting for transfers between devices: 57.3 us -> 46.8 us
  starting transfers between devices: 30.5 us -> 36.3 us
  Pallas kernels: 33.2 us -> 38.9 us
  local copies, waits for them, and re-layouts: 1.07 us -> 2.91 us
    all_to_all x2 -> x3, waiting for transfers between devices: 48.3 us -> 0.53 us  [the longest x1 0.52 us: per_device(): lax.all_to_all(totals, CHIPS, split_axis=0, concat_axis=0, tiled=True)]
    ppermute x10 -> x11, waiting for transfers between devices: 7.19 us -> 44.5 us  [turned(): lax.ppermute(x, axis, [(i, (i + shift) % count) for i in range(count)])]
    pallas_call x1 -> x3, Pallas kernels: 5.81 us -> 13.1 us  [the longest x1 5.31 us: per_device(): call(place_first_kernel, 'place_first', [IN_SMEM, IN_SMEM, IN_SMEM, IN_HB...]
    all_to_all x2 -> x3, starting transfers between devices: 11.4 us -> 16.8 us  [the longest x1 7.13 us: per_device(): lax.all_to_all(first_slots, DP, split_axis=0, concat_axis=0, tiled=True)]
    pallas_call x1, Pallas kernels: 7.36 us -> 5.74 us  [per_device(): call(backward_kernel, 'backward', [IN_SMEM, IN_SMEM, IN_HBM, IN_VMEM, IN_...]
    ppermute x10 -> x11, starting transfers between devices: 17.1 us -> 17.5 us  [turned(): lax.ppermute(x, axis, [(i, (i + shift) % count) for i in range(count)])]
  transfers between devices with their start and end apart: 13 -> 15, of which waited for: 8 -> 8; matrix products, arithmetic and copies ran while one was open for 2% -> 3% of each run, Pallas kernels for 14% -> 16%
where the time goes in v7:
time: 150 us; the launch traced here: 149 us
  waiting for transfers between devices  46.8 us (31%)
  Pallas kernels  38.9 us (26%)
  starting transfers between devices  36.3 us (24%)
  blocking collectives  19.6 us (13%)
  other arithmetic  3.16 us (2%)
  local copies, waits for them, and re-layouts  2.91 us (2%)
  between operations  1.6 us (1%)
    ppermute x11, waiting for transfers between devices, turned(): lax.ppermute(x, axis, [(i, (i + shift) % count) for i in range(count)])  44.5 us
    all_to_all x1, blocking collectives, per_device(): own = lax.all_to_all(copies, CHIPS, split_axis=0, concat_axis=0, tiled=True)  19.6 us
    ppermute x11, starting transfers between devices, turned(): lax.ppermute(x, axis, [(i, (i + shift) % count) for i in range(count)])  17.5 us
    pallas_call x1, Pallas kernels, per_device(): call(forward_kernel, 'forward', [IN_SMEM, IN_SMEM, IN_SMEM, IN_HBM, IN_HB...  11 us
    pallas_call x1, Pallas kernels, per_device(): call(weight_kernel, 'weight_grads', [IN_SMEM, IN_SMEM, IN_HBM, IN_HBM, IN...  7.46 us
    all_to_all x1, starting transfers between devices, per_device(): lax.all_to_all(first_slots, DP, split_axis=0, concat_axis=0, tiled=True)  7.13 us
    all_to_all x1, starting transfers between devices, per_device(): lax.all_to_all(second_slots, DP, split_axis=0, concat_axis=0, tiled=True)  6.17 us
    pallas_call x1, Pallas kernels, per_device(): call(backward_kernel, 'backward', [IN_SMEM, IN_SMEM, IN_HBM, IN_VMEM, IN_...  5.74 us
  transfers between devices with their start and end apart: 15, of which 8 were waited for; matrix products, arithmetic and copies ran while one was open for 3% of the time, Pallas kernels for 16%

profile of v7, /device:TPU:1, one launch (start us, length us, event | category | flops | bytes accessed | tf_op | source)
XLA Modules:
  0.0 149.2 jit_solution(6661894022490384559)
XLA Ops:
  0.7 0.9 pack.1
  1.6 19.6 %all_to_all.20.own_hbm = bf16[16,56,384]{2,1,0:T(8,128)(2,1)S(1)} all-to-all(bf16[16,56,384]{2,1,0:T(8,128)(2,1)S(1)} %pack.1), channel_id=1, replica_groups=mesh['dp_0'=4,'dp_1'=4,'dp_2'=2,'head'=4] {'dp_0','dp_1'}, dimensions={0} | all-to-all | bytes 1376256 | tf_op jit(solution)/shard_map/all_to_all | solution.py:477
  21.2 2.0 %collective-permute-start = (bf16[16,56,384]{2,1,0:T(8,128)(2,1)S(1)}, bf16[16,56,384]{2,1,0:T(8,128)(2,1)S(1)}, u32[]{:S(2)}, u32[]{:S(2)}) collective-permute-start(bf16[16,56,384]{2,1,0:T(8,128)(2,1)S(1)} %all_to_all.20.own_hbm), channel_id=1, source_target_pairs={{0,4},{4,0},{1,5},{5,1},{2,6},{6,2},{3,7},{7,3},{8,12},{12,8},{9,1... | collective-permute-start | bytes 2064392 | tf_op jit(solution)/shard_map/ppermute | solution.py:32
  23.2 1.8 %collective-permute-done.other_hbm = bf16[16,56,384]{2,1,0:T(8,128)(2,1)S(1)} collective-permute-done((bf16[16,56,384]{2,1,0:T(8,128)(2,1)S(1)}, bf16[16,56,384]{2,1,0:T(8,128)(2,1)S(1)}, u32[]{:S(2)}, u32[]{:S(2)}) %collective-permute-start) | collective-permute-done | bytes 688160 | tf_op jit(solution)/shard_map/ppermute | solution.py:32
  25.0 0.9 copy-done.3
  25.9 11.0 %forward.1 = (bf16[2048,384]{1,0:T(8,128)(2,1)}, bf16[2048,384]{1,0:T(8,128)(2,1)}, bf16[1536,384]{1,0:T(8,128)(2,1)}, bf16[3584,384]{1,0:T(8,128)(2,1)S(1)}, f3...) custom-call(s32[8]{0:T(128)S(1)} %copy-done, s32[8]{0:T(128)S(1)} %copy-done.1, ...), custom_call_target="tpu_custom_call" | custom-call | tf_op jit(solution)/shard_map/forward/pallas_call | solution.py:480
  36.8 3.5 %all-to-all-start.1 = ((f32[16,1,128]{2,1,0:T(1,128)}), f32[16,1,128]{2,1,0:T(1,128)S(1)}, u32[]{:S(2)}, u32[]{:S(2)}) async-start(f32[16,1,128]{2,1,0:T(1,128)} %get-tuple-element.34), calls=%async_computation.1 | async-start | bytes 16384 | tf_op jit(solution)/shard_map/all_to_all | solution.py:507
  40.3 5.7 %backward.1 = (bf16[2048,384]{1,0:T(8,128)(2,1)}, bf16[32,128,384]{2,1,0:T(8,128)(2,1)}) custom-call(s32[8]{0:T(128)S(1)} %copy-done, s32[8]{0:T(128)S(1)} %copy-done.1, bf16[2048,384]{1,0:T(8,128)(2,1)} %get-tuple-element.28.mid_grad_hbm, bf16[3584,384]{1,0:T(8,128)(2,1)S(1)} %get-tuple-element.29.state_ref, f32[1,384]{1,0:T(1,128)S(1)} %get-tuple-element.30.out_w_ref), custom_call_target="tpu_custom_call" | custom-call | bytes 16777216 | tf_op jit(solution)/shard_map/backward/pallas_call | solution.py:509
  46.1 0.5 all-to-all-done.1
  46.6 7.1 %all-to-all-start.2 = ((bf16[32,128,384]{2,1,0:T(8,128)(2,1)}), bf16[32,128,384]{2,1,0:T(8,128)(2,1)}, u32[]{:S(2)}, u32[]{:S(2)}) async-start(bf16[32,128,384]{2,1,0:T(8,128)(2,1)} %get-tuple-element.35), calls=%async_computation.2 | async-start | bytes 6291456 | tf_op jit(solution)/shard_map/all_to_all | solution.py:529
  53.7 0.1 slice_convert_fusion
  53.8 0.6 collective-permute-start.1
  54.4 0.1 select_reduce_fusion
  54.5 0.7 collective-permute-done.1
  55.2 1.6 %collective-permute-start.2 = (f32[1,32]{1,0:T(1,128)S(1)}, f32[1,32]{1,0:T(1,128)S(1)}, u32[]{:S(2)}, u32[]{:S(2)}) collective-permute-start(f32[1,32]{1,0:T(1,128)S(1)} %bitcast_add_fusion), channel_id=1, source_target_pairs={{0,1},{1,2},{2,3},{3,0},{4,5},{5,6},{6,7},{7,4},{8,9},{9,10},{10,1... | collective-permute-start | bytes 392 | tf_op jit(solution)/shard_map/ppermute | solution.py:37
  56.9 3.3 %collective-permute-start.3 = (f32[1,32]{1,0:T(1,128)S(1)}, f32[1,32]{1,0:T(1,128)S(1)}, u32[]{:S(2)}, u32[]{:S(2)}) collective-permute-start(f32[1,32]{1,0:T(1,128)S(1)} %bitcast_add_fusion), channel_id=1, source_target_pairs={{0,2},{1,3},{2,0},{3,1},{4,6},{5,7},{6,4},{7,5},{8,10},{9,11},{10,... | collective-permute-start | bytes 392 | tf_op jit(solution)/shard_map/ppermute | solution.py:37
  60.2 0.7 collective-permute-start.4
  60.9 0.6 collective-permute-done.3
  61.5 1.5 collective-permute-done.4
  63.0 0.2 select_reduce_fusion.3.factor_ref
  63.2 7.5 %weight_grads.1 = bf16[32,56,384]{2,1,0:T(8,128)(2,1)S(1)} custom-call(s32[8]{0:T(128)S(1)} %copy-done, f32[8]{0:T(128)S(1)} %select_reduce_fusion.3.factor_ref, bf16[2048,384]{1,0:T(8,128)(2,1)} %bitcast.53, bf16[2048,384]{1,0:T(8,128)(2,1)} %get-tuple-element.38.low_hbm, bf16[2048,384]{1,0:T(8,128)(2,1)} %get-tuple-element.28.mid_grad_hbm, ...), custom_call_target="tpu_custom_call" | custom-call | bytes 16777216 | tf_op jit(solution)/shard_map/weight_grads/pallas_call | solution.py:557
  70.6 0.1 dynamic-slice_bitcast_fusion
  70.7 1.7 %collective-permute-start.5 = (bf16[4,4,56,384]{3,2,1,0:T(8,128)(2,1)S(1)}, bf16[4,4,56,384]{3,2,1,0:T(8,128)(2,1)S(1)}, u32[]{:S(2)}, u32[]{:S(2)}) collective-permute-start(bf16[4,4,56,384]{3,2,1,0:T(8,128)(2,1)S(1)} %dynamic-slice_bitcast_fusion), channel_id=1, source_target_pairs={{0,4},{4,0},{1,5},{5,1},{2,6},{6,2},{3,7},{7,3},{8,12},{12,8},{9,1... | collective-permute-start | bytes 2064392 | tf_op jit(solution)/shard_map/ppermute | solution.py:37
  72.4 4.7 %second_half.1 = bf16[32,128,384]{2,1,0:T(8,128)(2,1)} custom-call(s32[8]{0:T(128)S(1)} %copy-done, s32[8]{0:T(128)S(1)} %copy-done.1, bf16[2048,384]{1,0:T(8,128)(2,1)} %get-tuple-element.31.first_grad_hbm, bf16[1536,384]{1,0:T(8,128)(2,1)} %get-tuple-element.32.weights_hbm), custom_call_target="tpu_custom_call" | custom-call | bytes 16777216 | tf_op jit(solution)/shard_map/second_half/pallas_call | solution.py:531
  77.1 0.7 convert_reduce_fusion
  78.5 0.1 select_reduce_fusion.1
  78.6 0.2 convert_add_fusion
  78.8 0.1 fusion
  78.8 1.6 %collective-permute-start.6 = (bf16[4,56,384]{2,1,0:T(8,128)(2,1)S(1)}, bf16[4,56,384]{2,1,0:T(8,128)(2,1)S(1)}, u32[]{:S(2)}, u32[]{:S(2)}) collective-permute-start(bf16[4,56,384]{2,1,0:T(8,128)(2,1)S(1)} %get-tuple-element.58), channel_id=1, source_target_pairs={{0,32},{32,64},{64,96},{96,0},{1,33},{33,65},{65,97},{97,1},{2,34}... | collective-permute-start | bytes 516104 | tf_op jit(solution)/shard_map/ppermute | solution.py:37
  80.4 2.4 %collective-permute-start.7 = (bf16[4,56,384]{2,1,0:T(8,128)(2,1)S(1)}, bf16[4,56,384]{2,1,0:T(8,128)(2,1)S(1)}, u32[]{:S(2)}, u32[]{:S(2)}) collective-permute-start(bf16[4,56,384]{2,1,0:T(8,128)(2,1)S(1)} %get-tuple-element.60), channel_id=1, source_target_pairs={{0,64},{32,96},{64,0},{96,32},{1,65},{33,97},{65,1},{97,33},{2,66}... | collective-permute-start | bytes 516104 | tf_op jit(solution)/shard_map/ppermute | solution.py:37
  82.8 1.2 collective-permute-start.8
  84.0 0.2 select_reduce_fusion.2.source_ref
  84.2 0.7 fusion.6
  84.9 9.7 %collective-permute-done.6 = bf16[4,56,384]{2,1,0:T(8,128)(2,1)S(1)} collective-permute-done((bf16[4,56,384]{2,1,0:T(8,128)(2,1)S(1)}, bf16[4,56,384]{2,1,0:T(8,128)(2,1)S(1)}, u32[]{:S(2)}, u32[]{:S(2)}) %collective-permute-start.6) | collective-permute-done | bytes 172064 | tf_op jit(solution)/shard_map/ppermute | solution.py:37
  94.5 4.1 %collective-permute-done.7 = bf16[4,56,384]{2,1,0:T(8,128)(2,1)S(1)} collective-permute-done((bf16[4,56,384]{2,1,0:T(8,128)(2,1)S(1)}, bf16[4,56,384]{2,1,0:T(8,128)(2,1)S(1)}, u32[]{:S(2)}, u32[]{:S(2)}) %collective-permute-start.7) | collective-permute-done | bytes 172064 | tf_op jit(solution)/shard_map/ppermute | solution.py:37
  98.6 0.0 collective-permute-done.8
  98.6 0.8 convert_add_fusion.1
  99.5 0.0 all-to-all-done.2.received_hbm
  99.5 6.2 %all-to-all-start.3 = ((bf16[32,128,384]{2,1,0:T(8,128)(2,1)}), bf16[32,128,384]{2,1,0:T(8,128)(2,1)S(1)}, u32[]{:S(2)}, u32[]{:S(2)}) async-start(bf16[32,128,384]{2,1,0:T(8,128)(2,1)} %second_half.1), calls=%async_computation.3 | async-start | bytes 6291456 | tf_op jit(solution)/shard_map/all_to_all | solution.py:591
  105.7 1.0 fusion.5
  106.7 3.0 %collective-permute-start.10 = (bf16[56,384]{1,0:T(8,128)(2,1)S(1)}, bf16[56,384]{1,0:T(8,128)(2,1)S(1)}, u32[]{:S(2)}, u32[]{:S(2)}) collective-permute-start(bf16[56,384]{1,0:T(8,128)(2,1)S(1)} %get-tuple-element.62), channel_id=1, source_target_pairs={{0,16},{8,24},{16,0},{24,8},{1,17},{9,25},{17,1},{25,9},{2,18},{10... | collective-permute-start | bytes 129032 | tf_op jit(solution)/shard_map/ppermute | solution.py:37
  109.7 0.9 collective-permute-start.11
  110.5 0.6 collective-permute-start.9
  111.1 0.9 dynamic-slice_bitcast_fusion.2.own_ref
  112.0 5.3 %place_first.1.begun_ref = bf16[4096,384]{1,0:T(8,128)(2,1)} custom-call(s32[16]{0:T(128)S(1)} %select_reduce_fusion.2.source_ref, s32[1]{0:T(128)} %bitcast.16.count_ref, f32[1]{0:T(128)} %bitcast.6.factor_ref, bf16[32,128,384]{2,1,0:T(8,128)(2,1)} %all-to-all-done.2.received_hbm), custom_call_target="tpu_custom_call" | custom-call | bytes 12582912 | tf_op jit(solution)/shard_map/place_first/pallas_call | solution.py:593
  117.3 28.0 %collective-permute-done.10.second_ref = bf16[56,384]{1,0:T(8,128)(2,1)S(1)} collective-permute-done((bf16[56,384]{1,0:T(8,128)(2,1)S(1)}, bf16[56,384]{1,0:T(8,128)(2,1)S(1)}, u32[]{:S(2)}, u32[]{:S(2)}) %collective-permute-start.10) | collective-permute-done | bytes 43040 | tf_op jit(solution)/shard_map/ppermute | solution.py:37
  145.3 0.7 finish.1
  146.0 3.1 %place_second.1 = bf16[4096,384]{1,0:T(8,128)(2,1)} custom-call(s32[16]{0:T(128)S(1)} %select_reduce_fusion.2.source_ref, s32[1]{0:T(128)} %bitcast.16.count_ref, f32[1]{0:T(128)} %bitcast.6.factor_ref, bf16[32,128,384]{2,1,0:T(8,128)(2,1)S(1)} %all-to-all-done.3.received_ref, bf16[4096,384]{1,0:T(8,128)(2,1)} %place_first.1.begun_ref), custom_call_target="tpu_custom_call", output_to_operand_aliasing={{}: (4, {})} | custom-call | bytes 12582912 | tf_op jit(solution)/shard_map/place_second/pallas_call | solution.py:603
  (17 shorter events, 0.1 us)
Async XLA Ops:
  0.6 25.2 %copy-start = (s32[8]{0:T(128)S(1)}, s32[8]{0:T(128)}, u32[]{:S(2)}) copy-start(s32[8]{0:T(128)} %valid_ref.7) | copy-start | bytes 100
  0.6 25.2 %copy-start.1 = (s32[8]{0:T(128)S(1)}, s32[8]{0:T(128)}, u32[]{:S(2)}) copy-start(s32[8]{0:T(128)} %owner_ref.5) | copy-start | bytes 100
  21.2 4.7 %copy-start.2 = (bf16[16,56,384]{2,1,0:T(8,128)(2,1)}, bf16[16,56,384]{2,1,0:T(8,128)(2,1)S(1)}, u32[]{:S(2)}) copy-start(bf16[16,56,384]{2,1,0:T(8,128)(2,1)S(1)} %all_to_all.20.own_hbm) | copy-start | bytes 2064388
  21.2 3.8 %collective-permute-start = (bf16[16,56,384]{2,1,0:T(8,128)(2,1)S(1)}, bf16[16,56,384]{2,1,0:T(8,128)(2,1)S(1)}, u32[]{:S(2)}, u32[]{:S(2)}) collective-permute-start(bf16[16,56,384]{2,1,0:T(8,128)(2,1)S(1)} %all_to_all.20.own_hbm), channel_id=1, source_target_pairs={{0,4},{4,0},{1,5},{5,1},{2,6},{6,2},{3,7},{7,3},{8,12},{12,8},{9,1... | collective-permute-start | bytes 2064392 | tf_op jit(solution)/shard_map/ppermute | solution.py:32
  25.0 0.9 copy-start.3
  36.8 9.8 %all-to-all-start.1 = ((f32[16,1,128]{2,1,0:T(1,128)}), f32[16,1,128]{2,1,0:T(1,128)S(1)}, u32[]{:S(2)}, u32[]{:S(2)}) async-start(f32[16,1,128]{2,1,0:T(1,128)} %get-tuple-element.34), calls=%async_computation.1 | async-start | bytes 16384 | tf_op jit(solution)/shard_map/all_to_all | solution.py:507
  46.6 52.9 %all-to-all-start.2 = ((bf16[32,128,384]{2,1,0:T(8,128)(2,1)}), bf16[32,128,384]{2,1,0:T(8,128)(2,1)}, u32[]{:S(2)}, u32[]{:S(2)}) async-start(bf16[32,128,384]{2,1,0:T(8,128)(2,1)} %get-tuple-element.35), calls=%async_computation.2 | async-start | bytes 6291456 | tf_op jit(solution)/shard_map/all_to_all | solution.py:529
  53.8 1.4 collective-permute-start.1
  55.2 5.7 %collective-permute-start.2 = (f32[1,32]{1,0:T(1,128)S(1)}, f32[1,32]{1,0:T(1,128)S(1)}, u32[]{:S(2)}, u32[]{:S(2)}) collective-permute-start(f32[1,32]{1,0:T(1,128)S(1)} %bitcast_add_fusion), channel_id=1, source_target_pairs={{0,1},{1,2},{2,3},{3,0},{4,5},{5,6},{6,7},{7,4},{8,9},{9,10},{10,1... | collective-permute-start | bytes 392 | tf_op jit(solution)/shard_map/ppermute | solution.py:37
  56.9 4.6 %collective-permute-start.3 = (f32[1,32]{1,0:T(1,128)S(1)}, f32[1,32]{1,0:T(1,128)S(1)}, u32[]{:S(2)}, u32[]{:S(2)}) collective-permute-start(f32[1,32]{1,0:T(1,128)S(1)} %bitcast_add_fusion), channel_id=1, source_target_pairs={{0,2},{1,3},{2,0},{3,1},{4,6},{5,7},{6,4},{7,5},{8,10},{9,11},{10,... | collective-permute-start | bytes 392 | tf_op jit(solution)/shard_map/ppermute | solution.py:37
  60.2 2.8 %collective-permute-start.4 = (f32[1,32]{1,0:T(1,128)S(1)}, f32[1,32]{1,0:T(1,128)S(1)}, u32[]{:S(2)}, u32[]{:S(2)}) collective-permute-start(f32[1,32]{1,0:T(1,128)S(1)} %bitcast_add_fusion), channel_id=1, source_target_pairs={{0,3},{1,0},{2,1},{3,2},{4,7},{5,4},{6,5},{7,6},{8,11},{9,8},{10,9... | collective-permute-start | bytes 392 | tf_op jit(solution)/shard_map/ppermute | solution.py:37
  70.7 7.9 %collective-permute-start.5 = (bf16[4,4,56,384]{3,2,1,0:T(8,128)(2,1)S(1)}, bf16[4,4,56,384]{3,2,1,0:T(8,128)(2,1)S(1)}, u32[]{:S(2)}, u32[]{:S(2)}) collective-permute-start(bf16[4,4,56,384]{3,2,1,0:T(8,128)(2,1)S(1)} %dynamic-slice_bitcast_fusion), channel_id=1, source_target_pairs={{0,4},{4,0},{1,5},{5,1},{2,6},{6,2},{3,7},{7,3},{8,12},{12,8},{9,1... | collective-permute-start | bytes 2064392 | tf_op jit(solution)/shard_map/ppermute | solution.py:37
  78.8 15.7 %collective-permute-start.6 = (bf16[4,56,384]{2,1,0:T(8,128)(2,1)S(1)}, bf16[4,56,384]{2,1,0:T(8,128)(2,1)S(1)}, u32[]{:S(2)}, u32[]{:S(2)}) collective-permute-start(bf16[4,56,384]{2,1,0:T(8,128)(2,1)S(1)} %get-tuple-element.58), channel_id=1, source_target_pairs={{0,32},{32,64},{64,96},{96,0},{1,33},{33,65},{65,97},{97,1},{2,34}... | collective-permute-start | bytes 516104 | tf_op jit(solution)/shard_map/ppermute | solution.py:37
  80.4 18.2 %collective-permute-start.7 = (bf16[4,56,384]{2,1,0:T(8,128)(2,1)S(1)}, bf16[4,56,384]{2,1,0:T(8,128)(2,1)S(1)}, u32[]{:S(2)}, u32[]{:S(2)}) collective-permute-start(bf16[4,56,384]{2,1,0:T(8,128)(2,1)S(1)} %get-tuple-element.60), channel_id=1, source_target_pairs={{0,64},{32,96},{64,0},{96,32},{1,65},{33,97},{65,1},{97,33},{2,66}... | collective-permute-start | bytes 516104 | tf_op jit(solution)/shard_map/ppermute | solution.py:37
  82.8 15.8 %collective-permute-start.8 = (bf16[4,56,384]{2,1,0:T(8,128)(2,1)S(1)}, bf16[4,56,384]{2,1,0:T(8,128)(2,1)S(1)}, u32[]{:S(2)}, u32[]{:S(2)}) collective-permute-start(bf16[4,56,384]{2,1,0:T(8,128)(2,1)S(1)} %get-tuple-element.59), channel_id=1, source_target_pairs={{0,96},{32,0},{64,32},{96,64},{1,97},{33,1},{65,33},{97,65},{2,98}... | collective-permute-start | bytes 516104 | tf_op jit(solution)/shard_map/ppermute | solution.py:37
  99.5 46.5 %all-to-all-start.3 = ((bf16[32,128,384]{2,1,0:T(8,128)(2,1)}), bf16[32,128,384]{2,1,0:T(8,128)(2,1)S(1)}, u32[]{:S(2)}, u32[]{:S(2)}) async-start(bf16[32,128,384]{2,1,0:T(8,128)(2,1)} %second_half.1), calls=%async_computation.3 | async-start | bytes 6291456 | tf_op jit(solution)/shard_map/all_to_all | solution.py:591
  106.7 38.6 %collective-permute-start.10 = (bf16[56,384]{1,0:T(8,128)(2,1)S(1)}, bf16[56,384]{1,0:T(8,128)(2,1)S(1)}, u32[]{:S(2)}, u32[]{:S(2)}) collective-permute-start(bf16[56,384]{1,0:T(8,128)(2,1)S(1)} %get-tuple-element.62), channel_id=1, source_target_pairs={{0,16},{8,24},{16,0},{24,8},{1,17},{9,25},{17,1},{25,9},{2,18},{10... | collective-permute-start | bytes 129032 | tf_op jit(solution)/shard_map/ppermute | solution.py:37
  109.7 35.6 %collective-permute-start.11 = (bf16[56,384]{1,0:T(8,128)(2,1)S(1)}, bf16[56,384]{1,0:T(8,128)(2,1)S(1)}, u32[]{:S(2)}, u32[]{:S(2)}) collective-permute-start(bf16[56,384]{1,0:T(8,128)(2,1)S(1)} %get-tuple-element.61), channel_id=1, source_target_pairs={{0,24},{8,0},{16,8},{24,16},{1,25},{9,1},{17,9},{25,17},{2,26},{10... | collective-permute-start | bytes 129032 | tf_op jit(solution)/shard_map/ppermute | solution.py:37
  110.5 34.8 %collective-permute-start.9 = (bf16[56,384]{1,0:T(8,128)(2,1)S(1)}, bf16[56,384]{1,0:T(8,128)(2,1)S(1)}, u32[]{:S(2)}, u32[]{:S(2)}) collective-permute-start(bf16[56,384]{1,0:T(8,128)(2,1)S(1)} %get-tuple-element.63), channel_id=1, source_target_pairs={{0,8},{8,16},{16,24},{24,0},{1,9},{9,17},{17,25},{25,1},{2,10},{10... | collective-permute-start | bytes 129032 | tf_op jit(solution)/shard_map/ppermute | solution.py:37

commit v8 on v6

--- a/solution.py
+++ b/solution.py
@@ -48,7 +48,7 @@
 
     total = piece(0).astype(F32)
     for r in range(1, count):
-        total += turned(piece(r), axis, r).astype(F32)
+        total += turned(piece(r).astype(BF16), axis, r).astype(F32)
     return total
 
 
@@ -108,11 +108,6 @@
         copies_ref[j] = packed
 
 
-def chunks(local):
-    half, quarter = local // 2, local // 4
-    return ((0, half), (half, quarter), (half + quarter, quarter))
-
-
 def state_rows(local):
     tokens = local * BT
     return pl.ds(0, tokens), pl.ds(tokens, 4 * D)
@@ -133,8 +128,8 @@
         pltpu.make_async_copy(own_hbm, own_ref, weight_sems.at[0]),
         pltpu.make_async_copy(other_hbm, other_ref, weight_sems.at[1]),
     ]
-    for n, (j, group) in enumerate(chunks(local)):
-        rows = pl.ds(j * BT, group * BT)
+    for n, j in enumerate(range(0, local, GROUP)):
+        rows = pl.ds(j * BT, GROUP * BT)
         arrivals.append(pltpu.make_async_copy(feats_ref.at[rows], raw_ref.at[rows], sems.at[n]))
     for copy in arrivals:
         copy.start()
@@ -175,11 +170,11 @@
     lane = lax.broadcasted_iota(jnp.int32, (1, 128), 1)
     totals = jnp.zeros((1, 128), F32)
     departures = []
-    for n, (j, group) in enumerate(chunks(local)):
-        rows = pl.ds(j * BT, group * BT)
+    for n, j in enumerate(range(0, local, GROUP)):
+        rows = pl.ds(j * BT, GROUP * BT)
         arrivals[2 + n].wait()
-        place = block_place(group * BT)
-        keep = row_mask(valid_ref, j, group)
+        place = block_place(GROUP * BT)
+        keep = row_mask(valid_ref, j, GROUP)
         masked = jnp.where(keep, raw_ref[rows, :].astype(F32), 0.0)
         before, after = neighbours(masked, place, BT - 1)
         first = jnp.dot(before, weight(weights_ref, 0), preferred_element_type=F32)
@@ -203,13 +198,13 @@
         copy.start()
         departures.append(copy)
         total = jnp.where(keep, second_act + first_act, 0.0)
-        for i in range(group):
+        for i in range(GROUP):
             block = jnp.sum(total[i * BT : (i + 1) * BT], 0, keepdims=True)
             sums_ref[j + i : j + i + 1, :] = block
             block_sum = jnp.sum(block * out_w, 1, keepdims=True)
             totals += jnp.where(lane == owner_ref[j + i], block_sum, 0.0)
-    for device in range(devices):
-        totals_ref[device] = totals
+    for chip in range(devices // 2):
+        totals_ref[chip] = totals
     for copy in departures:
         copy.wait()
 
@@ -427,7 +422,7 @@
             (IN_VMEM, (local, D), F32),
             (IN_VMEM, (1, D), F32),
             (IN_VMEM, (devices, 128), F32),
-            (IN_VMEM, (devices, 1, 128), F32),
+            (IN_VMEM, (chips, 1, 128), F32),
         ],
         [
             pltpu.VMEM((tokens_here, D), BF16),
@@ -436,13 +431,13 @@
             pltpu.VMEM((tokens_here, D), BF16),
             pltpu.VMEM((tokens_here, D), BF16),
             pltpu.VMEM((4 * D, D), F32),
-            pltpu.SemaphoreType.DMA((3,)),
-            pltpu.SemaphoreType.DMA((2, 3)),
+            pltpu.SemaphoreType.DMA((local // GROUP,)),
+            pltpu.SemaphoreType.DMA((2, local // GROUP)),
             pltpu.SemaphoreType.DMA((2,)),
         ],
     )(valid, owner_map, core, in_hbm(feats[0]), in_hbm(own), in_hbm(other))
 
-    totals = lax.all_to_all(totals, DP, split_axis=0, concat_axis=0, tiled=True)
+    totals = lax.all_to_all(totals, CHIPS, split_axis=0, concat_axis=0, tiled=True)
 
     first_grad, slots = call(
         backward_kernel,
@@ -466,7 +461,8 @@
     slots, totals = lax.optimization_barrier((slots, totals))
     received = lax.all_to_all(slots, DP, split_axis=0, concat_axis=0, tiled=True)
 
-    totals = total_over(jnp.sum(totals[:, 0, :devices], 0)[None], "head")[0]
+    totals = total_over(jnp.sum(totals[:, 0, :devices], 0)[None], "dp_2")
+    totals = total_over(totals, "head")[0]
     members = (owner_map[:, None] == images[None, :]).astype(F32)
     owners = extras[:, SHARD : SHARD + local].astype(jnp.int32)
     valids = extras[:, SHARD + local : SHARD + 2 * local]
@@ -493,7 +489,10 @@
         valid, block_factor, in_hbm(feats[0]), in_hbm(low), in_hbm(mid_grad),
         in_hbm(first_grad), in_vmem(sums),
     )
-    parts = scattered_sum(parts.reshape(chips, 2, ROWS, D), "dp_2", 1).astype(BF16)
+    parts = parts.reshape(4, 4, 2, ROWS, D)
+    parts = scattered_sum(parts, "dp_2", 2)
+    parts = scattered_sum(parts, "dp_0", 0).astype(BF16)
+
     present = jnp.sum((owners == me).astype(jnp.int32), 1)
     rank = jnp.sum(jnp.where(images[None, :] < images[:, None], present[None, :], 0), 1)
     count = jnp.sum(present)
@@ -502,7 +501,7 @@
     source = jnp.sum(jnp.where(hit, images[None, :], 0), 1).astype(jnp.int32)
     table = (source, count.reshape(1), own_factor)
     parts, received, table = lax.optimization_barrier((parts, received, table))
-    pieces = lax.all_to_all(parts, CHIPS, split_axis=0, concat_axis=0, tiled=True)
+    pieces = lax.all_to_all(parts, "dp_1", split_axis=0, concat_axis=0, tiled=True)
     (placed,) = call(
         place_kernel,
         "place",

time: 150 us -> 148 us (0.987)
  waiting for transfers between devices: 61 us -> 58.2 us
  starting transfers between devices: 28.2 us -> 29.8 us
    ppermute x4 -> x8, waiting for transfers between devices: 2.17 us -> 56.4 us  [turned(): lax.ppermute(x, axis, [(i, (i + shift) % count) for i in range(count)])]
    all_to_all x1, waiting for transfers between devices: 51.9 us -> 0.01 us  [per_device(): lax.all_to_all(slots, DP, split_axis=0, concat_axis=0, tiled=True)]
    ppermute x4 -> x8, starting transfers between devices: 7.42 us -> 12.8 us  [turned(): lax.ppermute(x, axis, [(i, (i + shift) % count) for i in range(count)])]
    all_to_all x2, waiting for transfers between devices: 5.19 us -> 0.01 us  [the longest x1 0.01 us: per_device(): lax.all_to_all(parts, 'dp_1', split_axis=0, concat_axis=0, tiled=True)]
    all_to_all x2, starting transfers between devices: 11.2 us -> 7.51 us  [the longest x1 3.84 us: per_device(): lax.all_to_all(parts, 'dp_1', split_axis=0, concat_axis=0, tiled=True)]
  transfers between devices with their start and end apart: 8 -> 12, of which waited for: 6 -> 7; matrix products, arithmetic and copies ran while one was open for 2% -> 2% of each run, Pallas kernels for 15% -> 14%
where the time goes in v8:
time: 148 us; the launch traced here: 146 us
  waiting for transfers between devices  58.2 us (39%)
  Pallas kernels  33 us (22%)
  starting transfers between devices  29.8 us (20%)
  blocking collectives  19.6 us (13%)
  other arithmetic  3.03 us (2%)
    ppermute x8, waiting for transfers between devices, turned(): lax.ppermute(x, axis, [(i, (i + shift) % count) for i in range(count)])  56.4 us
    all_to_all x1, blocking collectives, per_device(): own = lax.all_to_all(copies, CHIPS, split_axis=0, concat_axis=0, tiled=True)  19.6 us
    ppermute x8, starting transfers between devices, turned(): lax.ppermute(x, axis, [(i, (i + shift) % count) for i in range(count)])  12.8 us
    pallas_call x1, Pallas kernels, per_device(): call(forward_kernel, 'forward', [IN_SMEM, IN_SMEM, IN_SMEM, IN_HBM, IN_HB...  10.7 us
    pallas_call x1, Pallas kernels, per_device(): call(weight_kernel, 'weight_grads', [IN_SMEM, IN_SMEM, IN_HBM, IN_HBM, IN...  7.46 us
    all_to_all x1, starting transfers between devices, per_device(): lax.all_to_all(slots, DP, split_axis=0, concat_axis=0, tiled=True)  7.44 us
    pallas_call x1, Pallas kernels, per_device(): call(backward_kernel, 'backward', [IN_SMEM, IN_SMEM, IN_HBM, IN_VMEM, IN_...  7.38 us
    pallas_call x1, Pallas kernels, per_device(): call(place_kernel, 'place', [IN_SMEM, IN_SMEM, IN_SMEM, IN_HBM], [(IN_HBM...  5.86 us
  transfers between devices with their start and end apart: 12, of which 7 were waited for; matrix products, arithmetic and copies ran while one was open for 2% of the time, Pallas kernels for 14%

profile of v8, /device:TPU:1, one launch (start us, length us, event | category | flops | bytes accessed | tf_op | source)
XLA Modules:
  0.0 146.1 jit_solution(1480201800987738032)
XLA Ops:
  0.6 0.0 copy-start
  0.6 0.0 copy-start.1
  0.7 0.9 pack.1
  1.6 19.6 %all_to_all.20.own_hbm = bf16[16,56,384]{2,1,0:T(8,128)(2,1)S(1)} all-to-all(bf16[16,56,384]{2,1,0:T(8,128)(2,1)S(1)} %pack.1), channel_id=1, replica_groups=mesh['dp_0'=4,'dp_1'=4,'dp_2'=2,'head'=4] {'dp_0','dp_1'}, dimensions={0} | all-to-all | bytes 1376256 | tf_op jit(solution)/shard_map/all_to_all | solution.py:411
  21.2 2.0 %collective-permute-start = (bf16[16,56,384]{2,1,0:T(8,128)(2,1)S(1)}, bf16[16,56,384]{2,1,0:T(8,128)(2,1)S(1)}, u32[]{:S(2)}, u32[]{:S(2)}) collective-permute-start(bf16[16,56,384]{2,1,0:T(8,128)(2,1)S(1)} %all_to_all.20.own_hbm), channel_id=1, source_target_pairs={{0,4},{4,0},{1,5},{5,1},{2,6},{6,2},{3,7},{7,3},{8,12},{12,8},{9,1... | collective-permute-start | bytes 2064392 | tf_op jit(solution)/shard_map/ppermute | solution.py:31
  23.2 1.8 %collective-permute-done.other_hbm = bf16[16,56,384]{2,1,0:T(8,128)(2,1)S(1)} collective-permute-done((bf16[16,56,384]{2,1,0:T(8,128)(2,1)S(1)}, bf16[16,56,384]{2,1,0:T(8,128)(2,1)S(1)}, u32[]{:S(2)}, u32[]{:S(2)}) %collective-permute-start) | collective-permute-done | bytes 688160 | tf_op jit(solution)/shard_map/ppermute | solution.py:31
  25.0 0.9 copy-done.3
  25.8 0.0 copy-done.2
  25.8 0.0 copy-done
  25.8 0.0 copy-done.1
  25.9 10.7 %forward.1 = (bf16[2048,384]{1,0:T(8,128)(2,1)}, bf16[2048,384]{1,0:T(8,128)(2,1)}, bf16[3584,384]{1,0:T(8,128)(2,1)S(1)}, f32[8,384]{1,0:T(8,128)S(1)}, f32[1,3...) custom-call(s32[8]{0:T(128)S(1)} %copy-done, s32[8]{0:T(128)S(1)} %copy-done.1, s32[1]{0:T(128)} %bitcast.core_ref, ...), custom_call_target="tpu_custom_call" | custom-call | tf_op jit(solution)/shard_map/forward/pallas_call | solution.py:414
  36.5 3.7 %all-to-all-start.1 = ((f32[16,1,128]{2,1,0:T(1,128)}), f32[16,1,128]{2,1,0:T(1,128)S(1)}, u32[]{:S(2)}, u32[]{:S(2)}) async-start(f32[16,1,128]{2,1,0:T(1,128)} %get-tuple-element.27), calls=%async_computation.1 | async-start | bytes 16384 | tf_op jit(solution)/shard_map/all_to_all | solution.py:440
  40.2 7.4 %backward.1 = (bf16[2048,384]{1,0:T(8,128)(2,1)}, bf16[32,256,384]{2,1,0:T(8,128)(2,1)}) custom-call(s32[8]{0:T(128)S(1)} %copy-done, s32[8]{0:T(128)S(1)} %copy-done.1, bf16[2048,384]{1,0:T(8,128)(2,1)} %get-tuple-element.23.mid_grad_hbm, bf16[3584,384]{1,0:T(8,128)(2,1)S(1)} %get-tuple-element.24.state_ref, f32[1,384]{1,0:T(1,128)S(1)} %get-tuple-element.25.out_w_ref), custom_call_target="tpu_custom_call" | custom-call | bytes 25165824 | tf_op jit(solution)/shard_map/backward/pallas_call | solution.py:442
  47.6 0.0 all-to-all-done.1
  47.6 7.4 %all-to-all-start.2 = ((bf16[32,256,384]{2,1,0:T(8,128)(2,1)}), bf16[32,256,384]{2,1,0:T(8,128)(2,1)}, u32[]{:S(2)}, u32[]{:S(2)}) async-start(bf16[32,256,384]{2,1,0:T(8,128)(2,1)} %get-tuple-element.33), calls=%async_computation.2 | async-start | bytes 12582912 | tf_op jit(solution)/shard_map/all_to_all | solution.py:462
  55.1 0.1 slice_convert_fusion
  55.2 0.4 collective-permute-start.1
  55.5 0.1 select_reduce_fusion
  55.7 0.7 collective-permute-done.1
  56.4 1.7 %collective-permute-start.2 = (f32[1,32]{1,0:T(1,128)S(1)}, f32[1,32]{1,0:T(1,128)S(1)}, u32[]{:S(2)}, u32[]{:S(2)}) collective-permute-start(f32[1,32]{1,0:T(1,128)S(1)} %bitcast_add_fusion.1), channel_id=1, source_target_pairs={{0,1},{1,2},{2,3},{3,0},{4,5},{5,6},{6,7},{7,4},{8,9},{9,10},{10,1... | collective-permute-start | bytes 392 | tf_op jit(solution)/shard_map/ppermute | solution.py:36
  58.0 3.3 %collective-permute-start.3 = (f32[1,32]{1,0:T(1,128)S(1)}, f32[1,32]{1,0:T(1,128)S(1)}, u32[]{:S(2)}, u32[]{:S(2)}) collective-permute-start(f32[1,32]{1,0:T(1,128)S(1)} %bitcast_add_fusion.1), channel_id=1, source_target_pairs={{0,2},{1,3},{2,0},{3,1},{4,6},{5,7},{6,4},{7,5},{8,10},{9,11},{10,... | collective-permute-start | bytes 392 | tf_op jit(solution)/shard_map/ppermute | solution.py:36
  61.3 0.7 collective-permute-start.4
  62.0 0.0 collective-permute-done.2
  62.0 0.6 collective-permute-done.3
  62.7 1.5 %collective-permute-done.4 = f32[1,32]{1,0:T(1,128)S(1)} collective-permute-done((f32[1,32]{1,0:T(1,128)S(1)}, f32[1,32]{1,0:T(1,128)S(1)}, u32[]{:S(2)}, u32[]{:S(2)}) %collective-permute-start.4) | collective-permute-done | bytes 160 | tf_op jit(solution)/shard_map/ppermute | solution.py:36
  64.1 0.6 fusion.6
  64.8 0.2 select_reduce_fusion.3.factor_ref
  65.0 7.5 %weight_grads.1 = bf16[32,56,384]{2,1,0:T(8,128)(2,1)S(1)} custom-call(s32[8]{0:T(128)S(1)} %copy-done, f32[8]{0:T(128)S(1)} %select_reduce_fusion.3.factor_ref, bf16[2048,384]{1,0:T(8,128)(2,1)} %bitcast.49, bf16[2048,384]{1,0:T(8,128)(2,1)} %get-tuple-element.30.low_hbm, bf16[2048,384]{1,0:T(8,128)(2,1)} %get-tuple-element.23.mid_grad_hbm, ...), custom_call_target="tpu_custom_call" | custom-call | bytes 16777216 | tf_op jit(solution)/shard_map/weight_grads/pallas_call | solution.py:475
  72.4 0.1 dynamic-slice_bitcast_fusion
  72.5 1.7 %collective-permute-start.5 = (bf16[4,4,56,384]{3,2,1,0:T(8,128)(2,1)S(1)}, bf16[4,4,56,384]{3,2,1,0:T(8,128)(2,1)S(1)}, u32[]{:S(2)}, u32[]{:S(2)}) collective-permute-start(bf16[4,4,56,384]{3,2,1,0:T(8,128)(2,1)S(1)} %dynamic-slice_bitcast_fusion), channel_id=1, source_target_pairs={{0,4},{4,0},{1,5},{5,1},{2,6},{6,2},{3,7},{7,3},{8,12},{12,8},{9,1... | collective-permute-start | bytes 2064392 | tf_op jit(solution)/shard_map/ppermute | solution.py:36
  74.2 0.7 convert_reduce_fusion
  75.6 0.1 select_reduce_fusion.1
  75.7 0.3 collective-permute-done.5
  76.0 0.2 convert_add_fusion
  76.1 0.1 fusion.3
  76.2 1.5 %collective-permute-start.6 = (bf16[4,56,384]{2,1,0:T(8,128)(2,1)S(1)}, bf16[4,56,384]{2,1,0:T(8,128)(2,1)S(1)}, u32[]{:S(2)}, u32[]{:S(2)}) collective-permute-start(bf16[4,56,384]{2,1,0:T(8,128)(2,1)S(1)} %get-tuple-element.46), channel_id=1, source_target_pairs={{0,32},{32,64},{64,96},{96,0},{1,33},{33,65},{65,97},{97,1},{2,34}... | collective-permute-start | bytes 516104 | tf_op jit(solution)/shard_map/ppermute | solution.py:36
  77.7 2.4 %collective-permute-start.7 = (bf16[4,56,384]{2,1,0:T(8,128)(2,1)S(1)}, bf16[4,56,384]{2,1,0:T(8,128)(2,1)S(1)}, u32[]{:S(2)}, u32[]{:S(2)}) collective-permute-start(bf16[4,56,384]{2,1,0:T(8,128)(2,1)S(1)} %get-tuple-element.48), channel_id=1, source_target_pairs={{0,64},{32,96},{64,0},{96,32},{1,65},{33,97},{65,1},{97,33},{2,66}... | collective-permute-start | bytes 516104 | tf_op jit(solution)/shard_map/ppermute | solution.py:36
  80.2 1.1 collective-permute-start.8
  81.3 0.2 select_reduce_fusion.2.source_ref
  81.5 46.0 %collective-permute-done.6 = bf16[4,56,384]{2,1,0:T(8,128)(2,1)S(1)} collective-permute-done((bf16[4,56,384]{2,1,0:T(8,128)(2,1)S(1)}, bf16[4,56,384]{2,1,0:T(8,128)(2,1)S(1)}, u32[]{:S(2)}, u32[]{:S(2)}) %collective-permute-start.6) | collective-permute-done | bytes 172064 | tf_op jit(solution)/shard_map/ppermute | solution.py:36
  127.5 7.4 %collective-permute-done.7 = bf16[4,56,384]{2,1,0:T(8,128)(2,1)S(1)} collective-permute-done((bf16[4,56,384]{2,1,0:T(8,128)(2,1)S(1)}, bf16[4,56,384]{2,1,0:T(8,128)(2,1)S(1)}, u32[]{:S(2)}, u32[]{:S(2)}) %collective-permute-start.7) | collective-permute-done | bytes 172064 | tf_op jit(solution)/shard_map/ppermute | solution.py:36
  134.9 0.0 collective-permute-done.8
  134.9 0.8 fusion.2
  135.7 0.0 all-to-all-done.2.received_ref
  135.7 3.8 %all-to-all-start.3 = ((bf16[4,56,384]{2,1,0:T(8,128)(2,1)}), bf16[4,56,384]{2,1,0:T(8,128)(2,1)S(1)}, u32[]{:S(2)}, u32[]{:S(2)}) async-start(bf16[4,56,384]{2,1,0:T(8,128)(2,1)} %fusion.2), calls=%async_computation.3 | async-start | bytes 344064 | tf_op jit(solution)/shard_map/all_to_all | solution.py:504
  139.5 5.9 %place.1 = bf16[4096,384]{1,0:T(8,128)(2,1)} custom-call(s32[16]{0:T(128)S(1)} %select_reduce_fusion.2.source_ref, s32[1]{0:T(128)} %bitcast.14.count_ref, f32[1]{0:T(128)} %bitcast.16.factor_ref, bf16[32,256,384]{2,1,0:T(8,128)(2,1)} %all-to-all-done.2.received_ref), custom_call_target="tpu_custom_call" | custom-call | bytes 25165824 | tf_op jit(solution)/shard_map/place/pallas_call | solution.py:505
  145.4 0.0 all-to-all-done.3.pieces_ref
  145.4 0.7 finish.1
  (7 shorter events, 0.1 us)
Async XLA Ops:
  0.6 25.2 %copy-start = (s32[8]{0:T(128)S(1)}, s32[8]{0:T(128)}, u32[]{:S(2)}) copy-start(s32[8]{0:T(128)} %valid_ref.5) | copy-start | bytes 100
  0.6 25.2 %copy-start.1 = (s32[8]{0:T(128)S(1)}, s32[8]{0:T(128)}, u32[]{:S(2)}) copy-start(s32[8]{0:T(128)} %owner_ref.3) | copy-start | bytes 100
  21.2 4.7 %copy-start.2 = (bf16[16,56,384]{2,1,0:T(8,128)(2,1)}, bf16[16,56,384]{2,1,0:T(8,128)(2,1)S(1)}, u32[]{:S(2)}) copy-start(bf16[16,56,384]{2,1,0:T(8,128)(2,1)S(1)} %all_to_all.20.own_hbm) | copy-start | bytes 2064388
  21.2 3.8 %collective-permute-start = (bf16[16,56,384]{2,1,0:T(8,128)(2,1)S(1)}, bf16[16,56,384]{2,1,0:T(8,128)(2,1)S(1)}, u32[]{:S(2)}, u32[]{:S(2)}) collective-permute-start(bf16[16,56,384]{2,1,0:T(8,128)(2,1)S(1)} %all_to_all.20.own_hbm), channel_id=1, source_target_pairs={{0,4},{4,0},{1,5},{5,1},{2,6},{6,2},{3,7},{7,3},{8,12},{12,8},{9,1... | collective-permute-start | bytes 2064392 | tf_op jit(solution)/shard_map/ppermute | solution.py:31
  25.0 0.9 copy-start.3
  36.5 11.1 %all-to-all-start.1 = ((f32[16,1,128]{2,1,0:T(1,128)}), f32[16,1,128]{2,1,0:T(1,128)S(1)}, u32[]{:S(2)}, u32[]{:S(2)}) async-start(f32[16,1,128]{2,1,0:T(1,128)} %get-tuple-element.27), calls=%async_computation.1 | async-start | bytes 16384 | tf_op jit(solution)/shard_map/all_to_all | solution.py:440
  47.6 88.1 %all-to-all-start.2 = ((bf16[32,256,384]{2,1,0:T(8,128)(2,1)}), bf16[32,256,384]{2,1,0:T(8,128)(2,1)}, u32[]{:S(2)}, u32[]{:S(2)}) async-start(bf16[32,256,384]{2,1,0:T(8,128)(2,1)} %get-tuple-element.33), calls=%async_computation.2 | async-start | bytes 12582912 | tf_op jit(solution)/shard_map/all_to_all | solution.py:462
  55.2 1.2 collective-permute-start.1
  56.4 5.7 %collective-permute-start.2 = (f32[1,32]{1,0:T(1,128)S(1)}, f32[1,32]{1,0:T(1,128)S(1)}, u32[]{:S(2)}, u32[]{:S(2)}) collective-permute-start(f32[1,32]{1,0:T(1,128)S(1)} %bitcast_add_fusion.1), channel_id=1, source_target_pairs={{0,1},{1,2},{2,3},{3,0},{4,5},{5,6},{6,7},{7,4},{8,9},{9,10},{10,1... | collective-permute-start | bytes 392 | tf_op jit(solution)/shard_map/ppermute | solution.py:36
  58.0 4.6 %collective-permute-start.3 = (f32[1,32]{1,0:T(1,128)S(1)}, f32[1,32]{1,0:T(1,128)S(1)}, u32[]{:S(2)}, u32[]{:S(2)}) collective-permute-start(f32[1,32]{1,0:T(1,128)S(1)} %bitcast_add_fusion.1), channel_id=1, source_target_pairs={{0,2},{1,3},{2,0},{3,1},{4,6},{5,7},{6,4},{7,5},{8,10},{9,11},{10,... | collective-permute-start | bytes 392 | tf_op jit(solution)/shard_map/ppermute | solution.py:36
  61.3 2.8 %collective-permute-start.4 = (f32[1,32]{1,0:T(1,128)S(1)}, f32[1,32]{1,0:T(1,128)S(1)}, u32[]{:S(2)}, u32[]{:S(2)}) collective-permute-start(f32[1,32]{1,0:T(1,128)S(1)} %bitcast_add_fusion.1), channel_id=1, source_target_pairs={{0,3},{1,0},{2,1},{3,2},{4,7},{5,4},{6,5},{7,6},{8,11},{9,8},{10,9... | collective-permute-start | bytes 392 | tf_op jit(solution)/shard_map/ppermute | solution.py:36
  72.5 3.5 %collective-permute-start.5 = (bf16[4,4,56,384]{3,2,1,0:T(8,128)(2,1)S(1)}, bf16[4,4,56,384]{3,2,1,0:T(8,128)(2,1)S(1)}, u32[]{:S(2)}, u32[]{:S(2)}) collective-permute-start(bf16[4,4,56,384]{3,2,1,0:T(8,128)(2,1)S(1)} %dynamic-slice_bitcast_fusion), channel_id=1, source_target_pairs={{0,4},{4,0},{1,5},{5,1},{2,6},{6,2},{3,7},{7,3},{8,12},{12,8},{9,1... | collective-permute-start | bytes 2064392 | tf_op jit(solution)/shard_map/ppermute | solution.py:36
  76.2 51.3 %collective-permute-start.6 = (bf16[4,56,384]{2,1,0:T(8,128)(2,1)S(1)}, bf16[4,56,384]{2,1,0:T(8,128)(2,1)S(1)}, u32[]{:S(2)}, u32[]{:S(2)}) collective-permute-start(bf16[4,56,384]{2,1,0:T(8,128)(2,1)S(1)} %get-tuple-element.46), channel_id=1, source_target_pairs={{0,32},{32,64},{64,96},{96,0},{1,33},{33,65},{65,97},{97,1},{2,34}... | collective-permute-start | bytes 516104 | tf_op jit(solution)/shard_map/ppermute | solution.py:36
  77.7 57.2 %collective-permute-start.7 = (bf16[4,56,384]{2,1,0:T(8,128)(2,1)S(1)}, bf16[4,56,384]{2,1,0:T(8,128)(2,1)S(1)}, u32[]{:S(2)}, u32[]{:S(2)}) collective-permute-start(bf16[4,56,384]{2,1,0:T(8,128)(2,1)S(1)} %get-tuple-element.48), channel_id=1, source_target_pairs={{0,64},{32,96},{64,0},{96,32},{1,65},{33,97},{65,1},{97,33},{2,66}... | collective-permute-start | bytes 516104 | tf_op jit(solution)/shard_map/ppermute | solution.py:36
  80.2 54.7 %collective-permute-start.8 = (bf16[4,56,384]{2,1,0:T(8,128)(2,1)S(1)}, bf16[4,56,384]{2,1,0:T(8,128)(2,1)S(1)}, u32[]{:S(2)}, u32[]{:S(2)}) collective-permute-start(bf16[4,56,384]{2,1,0:T(8,128)(2,1)S(1)} %get-tuple-element.47), channel_id=1, source_target_pairs={{0,96},{32,0},{64,32},{96,64},{1,97},{33,1},{65,33},{97,65},{2,98}... | collective-permute-start | bytes 516104 | tf_op jit(solution)/shard_map/ppermute | solution.py:36
  135.7 9.7 %all-to-all-start.3 = ((bf16[4,56,384]{2,1,0:T(8,128)(2,1)}), bf16[4,56,384]{2,1,0:T(8,128)(2,1)S(1)}, u32[]{:S(2)}, u32[]{:S(2)}) async-start(bf16[4,56,384]{2,1,0:T(8,128)(2,1)} %fusion.2), calls=%async_computation.3 | async-start | bytes 344064 | tf_op jit(solution)/shard_map/all_to_all | solution.py:504

commit v9 on v8

--- a/solution.py
+++ b/solution.py
@@ -40,16 +40,34 @@
     return sum((turned(x, axis, r) for r in range(1, lax.axis_size(axis))), x)
 
 
-def scattered_sum(parts, axis, dim):
-    count, index = lax.axis_size(axis), lax.axis_index(axis)
-
-    def piece(shift):
-        return lax.dynamic_index_in_dim(parts, (index + shift) % count, dim, keepdims=False)
-
-    total = piece(0).astype(F32)
-    for r in range(1, count):
-        total += turned(piece(r).astype(BF16), axis, r).astype(F32)
-    return total
+def shares(parts, index):
+    count = parts.shape[0]
+
+    def share(shift):
+        return lax.dynamic_index_in_dim(parts, (index + shift) % count, 0, keepdims=False)
+
+    return [share(0)] + [share(r).astype(BF16) for r in range(1, count)]
+
+
+def crossed(x, shift, stage):
+    tall, wide = lax.axis_size("dp_0"), lax.axis_size("dp_1")
+    pairs = []
+    for y in range(tall):
+        for x_at in range(wide):
+            for core in range(2):
+                along_first = core == stage
+                to_y = (y + shift) % tall if along_first else y
+                to_x = x_at if along_first else (x_at + shift) % wide
+                pairs.append(((y * wide + x_at) * 2 + core, (to_y * wide + to_x) * 2 + core))
+    return lax.ppermute(x, DP, pairs)
+
+
+def delivered(own, *others, stage):
+    return [own] + [crossed(other, r, stage) for r, other in enumerate(others, 1)]
+
+
+def added(pieces):
+    return sum(piece.astype(F32) for piece in pieces)
 
 
 def gate(value):
@@ -323,10 +341,10 @@
         parts_ref[d] = stage_ref[...].astype(BF16)
 
 
-def finish_kernel(pieces_ref, conv_ref, mid_ref, out_ref, total_ref):
-    total = pieces_ref[0].astype(F32)
-    for i in range(1, pieces_ref.shape[0]):
-        total += pieces_ref[i].astype(F32)
+def finish_kernel(own_ref, first_ref, second_ref, third_ref, conv_ref, mid_ref, out_ref, total_ref):
+    total = own_ref[...]
+    for piece in (first_ref, second_ref, third_ref):
+        total += piece[...].astype(F32)
     total_ref[...] = total * (1.0 / BT)
     for row in range(3 * SHARD):
         conv_ref[row] = total_ref[row : row + 1, :]
@@ -489,9 +507,12 @@
         valid, block_factor, in_hbm(feats[0]), in_hbm(low), in_hbm(mid_grad),
         in_hbm(first_grad), in_vmem(sums),
     )
-    parts = parts.reshape(4, 4, 2, ROWS, D)
-    parts = scattered_sum(parts, "dp_2", 2)
-    parts = scattered_sum(parts, "dp_0", 0).astype(BF16)
+    own_parts, other_parts = shares(jnp.moveaxis(parts.reshape(chips, 2, ROWS, D), 1, 0), core[0])
+    parts = added([own_parts, swapped(other_parts)]).reshape(4, 4, ROWS, D)
+    parts = jnp.where(core[0] == 0, parts, jnp.swapaxes(parts, 0, 1))
+    row, column = lax.axis_index("dp_0"), lax.axis_index("dp_1")
+    ready = shares(parts, jnp.where(core[0] == 0, row, column))
+    parts = added(delivered(*ready, stage=0))
 
     present = jnp.sum((owners == me).astype(jnp.int32), 1)
     rank = jnp.sum(jnp.where(images[None, :] < images[:, None], present[None, :], 0), 1)
@@ -501,7 +522,8 @@
     source = jnp.sum(jnp.where(hit, images[None, :], 0), 1).astype(jnp.int32)
     table = (source, count.reshape(1), own_factor)
     parts, received, table = lax.optimization_barrier((parts, received, table))
-    pieces = lax.all_to_all(parts, "dp_1", split_axis=0, concat_axis=0, tiled=True)
+    ready = shares(parts, jnp.where(core[0] == 0, column, row))
+    pieces = delivered(*ready, stage=1)
     (placed,) = call(
         place_kernel,
         "place",
@@ -518,7 +540,7 @@
 
     conv, mid, out = pl.pallas_call(
         finish_kernel,
-        in_specs=[IN_VMEM],
+        in_specs=[IN_VMEM] * 4,
         out_specs=[IN_VMEM] * 3,
         out_shape=[
             jax.ShapeDtypeStruct((3 * SHARD, 1, D), F32),
@@ -527,7 +549,7 @@
         ],
         scratch_shapes=[pltpu.VMEM((ROWS, D), F32)],
         name="finish",
-    )(in_vmem(pieces))
+    )(*(in_vmem(x) for x in pieces))
     return placed[None], conv.reshape(1, 3, SHARD, D), mid.reshape(1, SHARD, D), out
 
 

time: 148 us -> 146 us (0.986)
    ppermute x8 -> x4, waiting for transfers between devices: 56.4 us -> 2.76 us  [turned(): lax.ppermute(x, axis, [(i, (i + shift) % count) for i in range(count)])]
    ppermute x0 -> x6, waiting for transfers between devices: none -> 53.1 us  [crossed(): return lax.ppermute(x, DP, pairs)]
    ppermute x0 -> x6, starting transfers between devices: none -> 9.24 us  [crossed(): return lax.ppermute(x, DP, pairs)]
    ppermute x8 -> x4, starting transfers between devices: 12.8 us -> 6.03 us  [turned(): lax.ppermute(x, axis, [(i, (i + shift) % count) for i in range(count)])]
    all_to_all x1 -> x0, starting transfers between devices: 3.84 us -> none  [per_device(): lax.all_to_all(parts, 'dp_1', split_axis=0, concat_axis=0, tiled=True)]
    ppermute x1 -> x2, starting transfers between devices: 2.03 us -> 3.73 us  [swapped(): return lax.ppermute(x, 'dp_2', [(0, 1), (1, 0)])]
  transfers between devices with their start and end apart: 12 -> 14, of which waited for: 7 -> 7; matrix products, arithmetic and copies ran while one was open for 2% -> 2% of each run, Pallas kernels for 14% -> 14%
where the time goes in v9:
time: 146 us; the launch traced here: 145 us
  waiting for transfers between devices  58 us (40%)
  Pallas kernels  32 us (22%)
  starting transfers between devices  30.1 us (21%)
  blocking collectives  19.6 us (13%)
  other arithmetic  2.42 us (2%)
  between operations  1.49 us (1%)
    ppermute x6, waiting for transfers between devices, crossed(): return lax.ppermute(x, DP, pairs)  53.1 us
    all_to_all x1, blocking collectives, per_device(): own = lax.all_to_all(copies, CHIPS, split_axis=0, concat_axis=0, tiled=True)  19.6 us
    pallas_call x1, Pallas kernels, per_device(): call(forward_kernel, 'forward', [IN_SMEM, IN_SMEM, IN_SMEM, IN_HBM, IN_HB...  10.7 us
    ppermute x6, starting transfers between devices, crossed(): return lax.ppermute(x, DP, pairs)  9.24 us
    all_to_all x1, starting transfers between devices, per_device(): lax.all_to_all(slots, DP, split_axis=0, concat_axis=0, tiled=True)  7.47 us
    pallas_call x1, Pallas kernels, per_device(): call(weight_kernel, 'weight_grads', [IN_SMEM, IN_SMEM, IN_HBM, IN_HBM, IN...  7.45 us
    pallas_call x1, Pallas kernels, per_device(): call(backward_kernel, 'backward', [IN_SMEM, IN_SMEM, IN_HBM, IN_VMEM, IN_...  7.37 us
    ppermute x4, starting transfers between devices, turned(): lax.ppermute(x, axis, [(i, (i + shift) % count) for i in range(count)])  6.03 us
  transfers between devices with their start and end apart: 14, of which 7 were waited for; matrix products, arithmetic and copies ran while one was open for 2% of the time, Pallas kernels for 14%

profile of v9, /device:TPU:1, one launch (start us, length us, event | category | flops | bytes accessed | tf_op | source)
XLA Modules:
  0.0 144.7 jit_solution(4298066748176026217)
XLA Ops:
  0.7 0.9 pack.1
  1.6 19.6 %all_to_all.15.own_hbm = bf16[16,56,384]{2,1,0:T(8,128)(2,1)S(1)} all-to-all(bf16[16,56,384]{2,1,0:T(8,128)(2,1)S(1)} %pack.1), channel_id=1, replica_groups=mesh['dp_0'=4,'dp_1'=4,'dp_2'=2,'head'=4] {'dp_0','dp_1'}, dimensions={0} | all-to-all | bytes 1376256 | tf_op jit(solution)/shard_map/all_to_all | solution.py:429
  21.2 2.0 %collective-permute-start = (bf16[16,56,384]{2,1,0:T(8,128)(2,1)S(1)}, bf16[16,56,384]{2,1,0:T(8,128)(2,1)S(1)}, u32[]{:S(2)}, u32[]{:S(2)}) collective-permute-start(bf16[16,56,384]{2,1,0:T(8,128)(2,1)S(1)} %all_to_all.15.own_hbm), channel_id=1, source_target_pairs={{0,4},{4,0},{1,5},{5,1},{2,6},{6,2},{3,7},{7,3},{8,12},{12,8},{9,1... | collective-permute-start | bytes 2064392 | tf_op jit(solution)/shard_map/ppermute | solution.py:31
  23.2 1.8 %collective-permute-done.other_hbm = bf16[16,56,384]{2,1,0:T(8,128)(2,1)S(1)} collective-permute-done((bf16[16,56,384]{2,1,0:T(8,128)(2,1)S(1)}, bf16[16,56,384]{2,1,0:T(8,128)(2,1)S(1)}, u32[]{:S(2)}, u32[]{:S(2)}) %collective-permute-start) | collective-permute-done | bytes 688160 | tf_op jit(solution)/shard_map/ppermute | solution.py:31
  25.0 0.9 copy-done.3
  25.9 10.7 %forward.1 = (bf16[2048,384]{1,0:T(8,128)(2,1)}, bf16[2048,384]{1,0:T(8,128)(2,1)}, bf16[3584,384]{1,0:T(8,128)(2,1)S(1)}, f32[8,384]{1,0:T(8,128)S(1)}, f32[1,3...) custom-call(s32[8]{0:T(128)S(1)} %copy-done, s32[8]{0:T(128)S(1)} %copy-done.1, s32[1]{0:T(128)} %bitcast.core_ref, ...), custom_call_target="tpu_custom_call" | custom-call | tf_op jit(solution)/shard_map/forward/pallas_call | solution.py:432
  36.5 3.7 %all-to-all-start.1 = ((f32[16,1,128]{2,1,0:T(1,128)}), f32[16,1,128]{2,1,0:T(1,128)S(1)}, u32[]{:S(2)}, u32[]{:S(2)}) async-start(f32[16,1,128]{2,1,0:T(1,128)} %get-tuple-element.27), calls=%async_computation.1 | async-start | bytes 16384 | tf_op jit(solution)/shard_map/all_to_all | solution.py:458
  40.2 7.4 %backward.1 = (bf16[2048,384]{1,0:T(8,128)(2,1)}, bf16[32,256,384]{2,1,0:T(8,128)(2,1)}) custom-call(s32[8]{0:T(128)S(1)} %copy-done, s32[8]{0:T(128)S(1)} %copy-done.1, bf16[2048,384]{1,0:T(8,128)(2,1)} %get-tuple-element.23.mid_grad_hbm, bf16[3584,384]{1,0:T(8,128)(2,1)S(1)} %get-tuple-element.24.state_ref, f32[1,384]{1,0:T(1,128)S(1)} %get-tuple-element.25.out_w_ref), custom_call_target="tpu_custom_call" | custom-call | bytes 25165824 | tf_op jit(solution)/shard_map/backward/pallas_call | solution.py:460
  47.6 0.0 all-to-all-done.1
  47.6 7.5 %all-to-all-start.2 = ((bf16[32,256,384]{2,1,0:T(8,128)(2,1)}), bf16[32,256,384]{2,1,0:T(8,128)(2,1)}, u32[]{:S(2)}, u32[]{:S(2)}) async-start(bf16[32,256,384]{2,1,0:T(8,128)(2,1)} %get-tuple-element.33), calls=%async_computation.2 | async-start | bytes 12582912 | tf_op jit(solution)/shard_map/all_to_all | solution.py:480
  55.1 0.1 slice_convert_fusion
  55.2 0.4 collective-permute-start.1
  55.6 0.1 select_reduce_fusion
  55.7 0.7 collective-permute-done.1
  56.4 1.6 %collective-permute-start.2 = (f32[1,32]{1,0:T(1,128)S(1)}, f32[1,32]{1,0:T(1,128)S(1)}, u32[]{:S(2)}, u32[]{:S(2)}) collective-permute-start(f32[1,32]{1,0:T(1,128)S(1)} %bitcast_add_fusion.1), channel_id=1, source_target_pairs={{0,1},{1,2},{2,3},{3,0},{4,5},{5,6},{6,7},{7,4},{8,9},{9,10},{10,1... | collective-permute-start | bytes 392 | tf_op jit(solution)/shard_map/ppermute | solution.py:36
  58.0 3.3 %collective-permute-start.3 = (f32[1,32]{1,0:T(1,128)S(1)}, f32[1,32]{1,0:T(1,128)S(1)}, u32[]{:S(2)}, u32[]{:S(2)}) collective-permute-start(f32[1,32]{1,0:T(1,128)S(1)} %bitcast_add_fusion.1), channel_id=1, source_target_pairs={{0,2},{1,3},{2,0},{3,1},{4,6},{5,7},{6,4},{7,5},{8,10},{9,11},{10,... | collective-permute-start | bytes 392 | tf_op jit(solution)/shard_map/ppermute | solution.py:36
  61.3 0.7 collective-permute-start.4
  62.0 0.0 collective-permute-done.2
  62.1 0.6 collective-permute-done.3
  62.7 1.5 %collective-permute-done.4 = f32[1,32]{1,0:T(1,128)S(1)} collective-permute-done((f32[1,32]{1,0:T(1,128)S(1)}, f32[1,32]{1,0:T(1,128)S(1)}, u32[]{:S(2)}, u32[]{:S(2)}) %collective-permute-start.4) | collective-permute-done | bytes 160 | tf_op jit(solution)/shard_map/ppermute | solution.py:36
  64.1 0.6 fusion.8
  64.8 0.2 select_reduce_fusion.3.factor_ref
  65.0 7.5 %weight_grads.1 = bf16[32,56,384]{2,1,0:T(8,128)(2,1)S(1)} custom-call(s32[8]{0:T(128)S(1)} %copy-done, f32[8]{0:T(128)S(1)} %select_reduce_fusion.3.factor_ref, bf16[2048,384]{1,0:T(8,128)(2,1)} %bitcast.58, bf16[2048,384]{1,0:T(8,128)(2,1)} %get-tuple-element.30.low_hbm, bf16[2048,384]{1,0:T(8,128)(2,1)} %get-tuple-element.23.mid_grad_hbm, ...), custom_call_target="tpu_custom_call" | custom-call | bytes 16777216 | tf_op jit(solution)/shard_map/weight_grads/pallas_call | solution.py:493
  72.4 0.1 dynamic-slice_bitcast_fusion
  72.5 1.7 %collective-permute-start.5 = (bf16[16,56,384]{2,1,0:T(8,128)(2,1)S(1)}, bf16[16,56,384]{2,1,0:T(8,128)(2,1)S(1)}, u32[]{:S(2)}, u32[]{:S(2)}) collective-permute-start(bf16[16,56,384]{2,1,0:T(8,128)(2,1)S(1)} %dynamic-slice_bitcast_fusion), channel_id=1, source_target_pairs={{0,4},{4,0},{1,5},{5,1},{2,6},{6,2},{3,7},{7,3},{8,12},{12,8},{9,1... | collective-permute-start | bytes 2064392 | tf_op jit(solution)/shard_map/ppermute | solution.py:31
  74.2 0.7 convert_reduce_fusion
  75.6 0.1 select_reduce_fusion.1
  75.7 0.3 collective-permute-done.5
  76.0 0.1 convert_add_fusion
  76.1 0.1 bitcast_select_fusion
  76.2 0.1 fusion.2
  76.3 1.5 %collective-permute-start.6 = (bf16[4,56,384]{2,1,0:T(8,128)(2,1)S(1)}, bf16[4,56,384]{2,1,0:T(8,128)(2,1)S(1)}, u32[]{:S(2)}, u32[]{:S(2)}) collective-permute-start(bf16[4,56,384]{2,1,0:T(8,128)(2,1)S(1)} %get-tuple-element.46), channel_id=1, source_target_pairs={{0,32},{4,12},{8,40},{12,20},{16,48},{20,28},{24,56},{28,4},{32,64... | collective-permute-start | bytes 516104 | tf_op jit(solution)/shard_map/ppermute | solution.py:62
  77.8 2.4 %collective-permute-start.7 = (bf16[4,56,384]{2,1,0:T(8,128)(2,1)S(1)}, bf16[4,56,384]{2,1,0:T(8,128)(2,1)S(1)}, u32[]{:S(2)}, u32[]{:S(2)}) collective-permute-start(bf16[4,56,384]{2,1,0:T(8,128)(2,1)S(1)} %get-tuple-element.48), channel_id=1, source_target_pairs={{0,64},{4,20},{8,72},{12,28},{16,80},{20,4},{24,88},{28,12},{32,96... | collective-permute-start | bytes 516104 | tf_op jit(solution)/shard_map/ppermute | solution.py:62
  80.2 1.2 collective-permute-start.8
  81.4 0.2 select_reduce_fusion.2.source_ref
  81.6 47.0 %collective-permute-done.6 = bf16[4,56,384]{2,1,0:T(8,128)(2,1)S(1)} collective-permute-done((bf16[4,56,384]{2,1,0:T(8,128)(2,1)S(1)}, bf16[4,56,384]{2,1,0:T(8,128)(2,1)S(1)}, u32[]{:S(2)}, u32[]{:S(2)}) %collective-permute-start.6) | collective-permute-done | bytes 172064 | tf_op jit(solution)/shard_map/ppermute | solution.py:62
  128.6 6.1 %collective-permute-done.7 = bf16[4,56,384]{2,1,0:T(8,128)(2,1)S(1)} collective-permute-done((bf16[4,56,384]{2,1,0:T(8,128)(2,1)S(1)}, bf16[4,56,384]{2,1,0:T(8,128)(2,1)S(1)}, u32[]{:S(2)}, u32[]{:S(2)}) %collective-permute-start.7) | collective-permute-done | bytes 172064 | tf_op jit(solution)/shard_map/ppermute | solution.py:62
  134.7 0.0 collective-permute-done.8
  134.7 0.1 fusion.1
  134.8 0.0 all-to-all-done.2.received_ref
  134.9 2.4 %collective-permute-start.10 = (bf16[56,384]{1,0:T(8,128)(2,1)S(1)}, bf16[56,384]{1,0:T(8,128)(2,1)S(1)}, u32[]{:S(2)}, u32[]{:S(2)}) collective-permute-start(bf16[56,384]{1,0:T(8,128)(2,1)S(1)} %get-tuple-element.50), channel_id=1, source_target_pairs={{0,16},{4,68},{8,24},{12,76},{16,0},{20,84},{24,8},{28,92},{32,48}... | collective-permute-start | bytes 129032 | tf_op jit(solution)/shard_map/ppermute | solution.py:62
  137.3 1.8 %collective-permute-start.11 = (bf16[56,384]{1,0:T(8,128)(2,1)S(1)}, bf16[56,384]{1,0:T(8,128)(2,1)S(1)}, u32[]{:S(2)}, u32[]{:S(2)}) collective-permute-start(bf16[56,384]{1,0:T(8,128)(2,1)S(1)} %get-tuple-element.49), channel_id=1, source_target_pairs={{0,24},{4,100},{8,0},{12,108},{16,8},{20,116},{24,16},{28,124},{32... | collective-permute-start | bytes 129032 | tf_op jit(solution)/shard_map/ppermute | solution.py:62
  139.0 0.0 collective-permute-start.9
  139.0 5.0 %place.1 = bf16[4096,384]{1,0:T(8,128)(2,1)} custom-call(s32[16]{0:T(128)S(1)} %select_reduce_fusion.2.source_ref, s32[1]{0:T(128)} %bitcast.16.count_ref, f32[1]{0:T(128)} %bitcast.18.factor_ref, bf16[32,256,384]{2,1,0:T(8,128)(2,1)} %all-to-all-done.2.received_ref), custom_call_target="tpu_custom_call" | custom-call | bytes 25165824 | tf_op jit(solution)/shard_map/place/pallas_call | solution.py:527
  144.0 0.0 collective-permute-done.10.second_ref
  144.0 0.0 collective-permute-done.11.third_ref
  144.0 0.0 collective-permute-done.9.first_ref
  144.0 0.7 finish.1
  (14 shorter events, 0.1 us)
Async XLA Ops:
  0.6 25.2 %copy-start = (s32[8]{0:T(128)S(1)}, s32[8]{0:T(128)}, u32[]{:S(2)}) copy-start(s32[8]{0:T(128)} %valid_ref.5) | copy-start | bytes 100
  0.6 25.2 %copy-start.1 = (s32[8]{0:T(128)S(1)}, s32[8]{0:T(128)}, u32[]{:S(2)}) copy-start(s32[8]{0:T(128)} %owner_ref.3) | copy-start | bytes 100
  21.2 4.7 %copy-start.2 = (bf16[16,56,384]{2,1,0:T(8,128)(2,1)}, bf16[16,56,384]{2,1,0:T(8,128)(2,1)S(1)}, u32[]{:S(2)}) copy-start(bf16[16,56,384]{2,1,0:T(8,128)(2,1)S(1)} %all_to_all.15.own_hbm) | copy-start | bytes 2064388
  21.2 3.8 %collective-permute-start = (bf16[16,56,384]{2,1,0:T(8,128)(2,1)S(1)}, bf16[16,56,384]{2,1,0:T(8,128)(2,1)S(1)}, u32[]{:S(2)}, u32[]{:S(2)}) collective-permute-start(bf16[16,56,384]{2,1,0:T(8,128)(2,1)S(1)} %all_to_all.15.own_hbm), channel_id=1, source_target_pairs={{0,4},{4,0},{1,5},{5,1},{2,6},{6,2},{3,7},{7,3},{8,12},{12,8},{9,1... | collective-permute-start | bytes 2064392 | tf_op jit(solution)/shard_map/ppermute | solution.py:31
  25.0 0.9 copy-start.3
  36.5 11.1 %all-to-all-start.1 = ((f32[16,1,128]{2,1,0:T(1,128)}), f32[16,1,128]{2,1,0:T(1,128)S(1)}, u32[]{:S(2)}, u32[]{:S(2)}) async-start(f32[16,1,128]{2,1,0:T(1,128)} %get-tuple-element.27), calls=%async_computation.1 | async-start | bytes 16384 | tf_op jit(solution)/shard_map/all_to_all | solution.py:458
  47.6 87.2 %all-to-all-start.2 = ((bf16[32,256,384]{2,1,0:T(8,128)(2,1)}), bf16[32,256,384]{2,1,0:T(8,128)(2,1)}, u32[]{:S(2)}, u32[]{:S(2)}) async-start(bf16[32,256,384]{2,1,0:T(8,128)(2,1)} %get-tuple-element.33), calls=%async_computation.2 | async-start | bytes 12582912 | tf_op jit(solution)/shard_map/all_to_all | solution.py:480
  55.2 1.2 collective-permute-start.1
  56.4 5.7 %collective-permute-start.2 = (f32[1,32]{1,0:T(1,128)S(1)}, f32[1,32]{1,0:T(1,128)S(1)}, u32[]{:S(2)}, u32[]{:S(2)}) collective-permute-start(f32[1,32]{1,0:T(1,128)S(1)} %bitcast_add_fusion.1), channel_id=1, source_target_pairs={{0,1},{1,2},{2,3},{3,0},{4,5},{5,6},{6,7},{7,4},{8,9},{9,10},{10,1... | collective-permute-start | bytes 392 | tf_op jit(solution)/shard_map/ppermute | solution.py:36
  58.0 4.7 %collective-permute-start.3 = (f32[1,32]{1,0:T(1,128)S(1)}, f32[1,32]{1,0:T(1,128)S(1)}, u32[]{:S(2)}, u32[]{:S(2)}) collective-permute-start(f32[1,32]{1,0:T(1,128)S(1)} %bitcast_add_fusion.1), channel_id=1, source_target_pairs={{0,2},{1,3},{2,0},{3,1},{4,6},{5,7},{6,4},{7,5},{8,10},{9,11},{10,... | collective-permute-start | bytes 392 | tf_op jit(solution)/shard_map/ppermute | solution.py:36
  61.3 2.8 %collective-permute-start.4 = (f32[1,32]{1,0:T(1,128)S(1)}, f32[1,32]{1,0:T(1,128)S(1)}, u32[]{:S(2)}, u32[]{:S(2)}) collective-permute-start(f32[1,32]{1,0:T(1,128)S(1)} %bitcast_add_fusion.1), channel_id=1, source_target_pairs={{0,3},{1,0},{2,1},{3,2},{4,7},{5,4},{6,5},{7,6},{8,11},{9,8},{10,9... | collective-permute-start | bytes 392 | tf_op jit(solution)/shard_map/ppermute | solution.py:36
  72.5 3.5 %collective-permute-start.5 = (bf16[16,56,384]{2,1,0:T(8,128)(2,1)S(1)}, bf16[16,56,384]{2,1,0:T(8,128)(2,1)S(1)}, u32[]{:S(2)}, u32[]{:S(2)}) collective-permute-start(bf16[16,56,384]{2,1,0:T(8,128)(2,1)S(1)} %dynamic-slice_bitcast_fusion), channel_id=1, source_target_pairs={{0,4},{4,0},{1,5},{5,1},{2,6},{6,2},{3,7},{7,3},{8,12},{12,8},{9,1... | collective-permute-start | bytes 2064392 | tf_op jit(solution)/shard_map/ppermute | solution.py:31
  76.3 52.3 %collective-permute-start.6 = (bf16[4,56,384]{2,1,0:T(8,128)(2,1)S(1)}, bf16[4,56,384]{2,1,0:T(8,128)(2,1)S(1)}, u32[]{:S(2)}, u32[]{:S(2)}) collective-permute-start(bf16[4,56,384]{2,1,0:T(8,128)(2,1)S(1)} %get-tuple-element.46), channel_id=1, source_target_pairs={{0,32},{4,12},{8,40},{12,20},{16,48},{20,28},{24,56},{28,4},{32,64... | collective-permute-start | bytes 516104 | tf_op jit(solution)/shard_map/ppermute | solution.py:62
  77.8 56.9 %collective-permute-start.7 = (bf16[4,56,384]{2,1,0:T(8,128)(2,1)S(1)}, bf16[4,56,384]{2,1,0:T(8,128)(2,1)S(1)}, u32[]{:S(2)}, u32[]{:S(2)}) collective-permute-start(bf16[4,56,384]{2,1,0:T(8,128)(2,1)S(1)} %get-tuple-element.48), channel_id=1, source_target_pairs={{0,64},{4,20},{8,72},{12,28},{16,80},{20,4},{24,88},{28,12},{32,96... | collective-permute-start | bytes 516104 | tf_op jit(solution)/shard_map/ppermute | solution.py:62
  80.2 54.5 %collective-permute-start.8 = (bf16[4,56,384]{2,1,0:T(8,128)(2,1)S(1)}, bf16[4,56,384]{2,1,0:T(8,128)(2,1)S(1)}, u32[]{:S(2)}, u32[]{:S(2)}) collective-permute-start(bf16[4,56,384]{2,1,0:T(8,128)(2,1)S(1)} %get-tuple-element.47), channel_id=1, source_target_pairs={{0,96},{4,28},{8,104},{12,4},{16,112},{20,12},{24,120},{28,20},{32... | collective-permute-start | bytes 516104 | tf_op jit(solution)/shard_map/ppermute | solution.py:62
  134.9 9.1 %collective-permute-start.10 = (bf16[56,384]{1,0:T(8,128)(2,1)S(1)}, bf16[56,384]{1,0:T(8,128)(2,1)S(1)}, u32[]{:S(2)}, u32[]{:S(2)}) collective-permute-start(bf16[56,384]{1,0:T(8,128)(2,1)S(1)} %get-tuple-element.50), channel_id=1, source_target_pairs={{0,16},{4,68},{8,24},{12,76},{16,0},{20,84},{24,8},{28,92},{32,48}... | collective-permute-start | bytes 129032 | tf_op jit(solution)/shard_map/ppermute | solution.py:62
  137.3 6.7 %collective-permute-start.11 = (bf16[56,384]{1,0:T(8,128)(2,1)S(1)}, bf16[56,384]{1,0:T(8,128)(2,1)S(1)}, u32[]{:S(2)}, u32[]{:S(2)}) collective-permute-start(bf16[56,384]{1,0:T(8,128)(2,1)S(1)} %get-tuple-element.49), channel_id=1, source_target_pairs={{0,24},{4,100},{8,0},{12,108},{16,8},{20,116},{24,16},{28,124},{32... | collective-permute-start | bytes 129032 | tf_op jit(solution)/shard_map/ppermute | solution.py:62
  139.0 5.0 %collective-permute-start.9 = (bf16[56,384]{1,0:T(8,128)(2,1)S(1)}, bf16[56,384]{1,0:T(8,128)(2,1)S(1)}, u32[]{:S(2)}, u32[]{:S(2)}) collective-permute-start(bf16[56,384]{1,0:T(8,128)(2,1)S(1)} %get-tuple-element.51), channel_id=1, source_target_pairs={{0,8},{4,36},{8,16},{12,44},{16,24},{20,52},{24,0},{28,60},{32,40}... | collective-permute-start | bytes 129032 | tf_op jit(solution)/shard_map/ppermute | solution.py:62

commit v10 on v9

--- a/solution.py
+++ b/solution.py
@@ -521,9 +521,9 @@
     hit = (rank[None, :] == wanted[:, None]) & (present[None, :] > 0)
     source = jnp.sum(jnp.where(hit, images[None, :], 0), 1).astype(jnp.int32)
     table = (source, count.reshape(1), own_factor)
-    parts, received, table = lax.optimization_barrier((parts, received, table))
     ready = shares(parts, jnp.where(core[0] == 0, column, row))
     pieces = delivered(*ready, stage=1)
+    received, table, _ = lax.optimization_barrier((received, table, ready))
     (placed,) = call(
         place_kernel,
         "place",
@@ -538,6 +538,7 @@
         megabytes=24,
     )(*table, in_hbm(received))
 
+    pieces, placed = lax.optimization_barrier((pieces, placed))
     conv, mid, out = pl.pallas_call(
         finish_kernel,
         in_specs=[IN_VMEM] * 4,

time: 146 us -> 146 us (level)
  no operation moved by 1% of the time
where the time goes in v10:
time: 146 us
  waiting for transfers between devices  58 us (40%)
  Pallas kernels  33.3 us (23%)
  starting transfers between devices  30.1 us (21%)
  blocking collectives  19.6 us (13%)
  other arithmetic  2.42 us (2%)
  between operations  1.49 us (1%)
    ppermute x6, waiting for transfers between devices, crossed(): return lax.ppermute(x, DP, pairs)  53.1 us
    all_to_all x1, blocking collectives, per_device(): own = lax.all_to_all(copies, CHIPS, split_axis=0, concat_axis=0, tiled=True)  19.6 us
    pallas_call x1, Pallas kernels, per_device(): call(forward_kernel, 'forward', [IN_SMEM, IN_SMEM, IN_SMEM, IN_HBM, IN_HB...  10.7 us
    ppermute x6, starting transfers between devices, crossed(): return lax.ppermute(x, DP, pairs)  9.24 us
    all_to_all x1, starting transfers between devices, per_device(): lax.all_to_all(slots, DP, split_axis=0, concat_axis=0, tiled=True)  7.47 us
    pallas_call x1, Pallas kernels, per_device(): call(weight_kernel, 'weight_grads', [IN_SMEM, IN_SMEM, IN_HBM, IN_HBM, IN...  7.45 us
    pallas_call x1, Pallas kernels, per_device(): call(backward_kernel, 'backward', [IN_SMEM, IN_SMEM, IN_HBM, IN_VMEM, IN_...  7.36 us
    pallas_call x1, Pallas kernels, per_device(): call(place_kernel, 'place', [IN_SMEM, IN_SMEM, IN_SMEM, IN_HBM], [(IN_HBM...  6.27 us
  transfers between devices with their start and end apart: 14, of which 7 were waited for; matrix products, arithmetic and copies ran while one was open for 2% of the time, Pallas kernels for 14%

profile of v10, /device:TPU:1, one launch (start us, length us, event | category | flops | bytes accessed | tf_op | source)
XLA Modules:
  0.0 146.0 jit_solution(13747481636550866997)
XLA Ops:
  0.7 0.9 pack.1
  1.6 19.6 %all_to_all.15.own_hbm = bf16[16,56,384]{2,1,0:T(8,128)(2,1)S(1)} all-to-all(bf16[16,56,384]{2,1,0:T(8,128)(2,1)S(1)} %pack.1), channel_id=1, replica_groups=mesh['dp_0'=4,'dp_1'=4,'dp_2'=2,'head'=4] {'dp_0','dp_1'}, dimensions={0} | all-to-all | bytes 1376256 | tf_op jit(solution)/shard_map/all_to_all | solution.py:429
  21.2 2.0 %collective-permute-start = (bf16[16,56,384]{2,1,0:T(8,128)(2,1)S(1)}, bf16[16,56,384]{2,1,0:T(8,128)(2,1)S(1)}, u32[]{:S(2)}, u32[]{:S(2)}) collective-permute-start(bf16[16,56,384]{2,1,0:T(8,128)(2,1)S(1)} %all_to_all.15.own_hbm), channel_id=1, source_target_pairs={{0,4},{4,0},{1,5},{5,1},{2,6},{6,2},{3,7},{7,3},{8,12},{12,8},{9,1... | collective-permute-start | bytes 2064392 | tf_op jit(solution)/shard_map/ppermute | solution.py:31
  23.2 1.8 %collective-permute-done.other_hbm = bf16[16,56,384]{2,1,0:T(8,128)(2,1)S(1)} collective-permute-done((bf16[16,56,384]{2,1,0:T(8,128)(2,1)S(1)}, bf16[16,56,384]{2,1,0:T(8,128)(2,1)S(1)}, u32[]{:S(2)}, u32[]{:S(2)}) %collective-permute-start) | collective-permute-done | bytes 688160 | tf_op jit(solution)/shard_map/ppermute | solution.py:31
  25.0 0.9 copy-done.3
  25.9 10.7 %forward.1 = (bf16[2048,384]{1,0:T(8,128)(2,1)}, bf16[2048,384]{1,0:T(8,128)(2,1)}, bf16[3584,384]{1,0:T(8,128)(2,1)S(1)}, f32[8,384]{1,0:T(8,128)S(1)}, f32[1,3...) custom-call(s32[8]{0:T(128)S(1)} %copy-done, s32[8]{0:T(128)S(1)} %copy-done.1, s32[1]{0:T(128)} %bitcast.core_ref, ...), custom_call_target="tpu_custom_call" | custom-call | tf_op jit(solution)/shard_map/forward/pallas_call | solution.py:432
  36.5 3.7 %all-to-all-start.1 = ((f32[16,1,128]{2,1,0:T(1,128)}), f32[16,1,128]{2,1,0:T(1,128)S(1)}, u32[]{:S(2)}, u32[]{:S(2)}) async-start(f32[16,1,128]{2,1,0:T(1,128)} %get-tuple-element.31), calls=%async_computation.1 | async-start | bytes 16384 | tf_op jit(solution)/shard_map/all_to_all | solution.py:458
  40.2 7.4 %backward.1 = (bf16[2048,384]{1,0:T(8,128)(2,1)}, bf16[32,256,384]{2,1,0:T(8,128)(2,1)}) custom-call(s32[8]{0:T(128)S(1)} %copy-done, s32[8]{0:T(128)S(1)} %copy-done.1, bf16[2048,384]{1,0:T(8,128)(2,1)} %get-tuple-element.27.mid_grad_hbm, bf16[3584,384]{1,0:T(8,128)(2,1)S(1)} %get-tuple-element.28.state_ref, f32[1,384]{1,0:T(1,128)S(1)} %get-tuple-element.29.out_w_ref), custom_call_target="tpu_custom_call" | custom-call | bytes 25165824 | tf_op jit(solution)/shard_map/backward/pallas_call | solution.py:460
  47.6 0.0 all-to-all-done.1
  47.6 7.5 %all-to-all-start.2 = ((bf16[32,256,384]{2,1,0:T(8,128)(2,1)}), bf16[32,256,384]{2,1,0:T(8,128)(2,1)}, u32[]{:S(2)}, u32[]{:S(2)}) async-start(bf16[32,256,384]{2,1,0:T(8,128)(2,1)} %get-tuple-element.37), calls=%async_computation.2 | async-start | bytes 12582912 | tf_op jit(solution)/shard_map/all_to_all | solution.py:480
  55.1 0.1 slice_convert_fusion
  55.2 0.4 collective-permute-start.1
  55.6 0.1 select_reduce_fusion
  55.7 0.7 collective-permute-done.1
  56.4 1.6 %collective-permute-start.2 = (f32[1,32]{1,0:T(1,128)S(1)}, f32[1,32]{1,0:T(1,128)S(1)}, u32[]{:S(2)}, u32[]{:S(2)}) collective-permute-start(f32[1,32]{1,0:T(1,128)S(1)} %bitcast_add_fusion.1), channel_id=1, source_target_pairs={{0,1},{1,2},{2,3},{3,0},{4,5},{5,6},{6,7},{7,4},{8,9},{9,10},{10,1... | collective-permute-start | bytes 392 | tf_op jit(solution)/shard_map/ppermute | solution.py:36
  58.0 3.3 %collective-permute-start.3 = (f32[1,32]{1,0:T(1,128)S(1)}, f32[1,32]{1,0:T(1,128)S(1)}, u32[]{:S(2)}, u32[]{:S(2)}) collective-permute-start(f32[1,32]{1,0:T(1,128)S(1)} %bitcast_add_fusion.1), channel_id=1, source_target_pairs={{0,2},{1,3},{2,0},{3,1},{4,6},{5,7},{6,4},{7,5},{8,10},{9,11},{10,... | collective-permute-start | bytes 392 | tf_op jit(solution)/shard_map/ppermute | solution.py:36
  61.3 0.7 collective-permute-start.4
  62.0 0.0 collective-permute-done.2
  62.0 0.6 collective-permute-done.3
  62.7 1.5 %collective-permute-done.4 = f32[1,32]{1,0:T(1,128)S(1)} collective-permute-done((f32[1,32]{1,0:T(1,128)S(1)}, f32[1,32]{1,0:T(1,128)S(1)}, u32[]{:S(2)}, u32[]{:S(2)}) %collective-permute-start.4) | collective-permute-done | bytes 160 | tf_op jit(solution)/shard_map/ppermute | solution.py:36
  64.1 0.6 fusion.8
  64.8 0.2 select_reduce_fusion.3.factor_ref
  65.0 7.5 %weight_grads.1 = bf16[32,56,384]{2,1,0:T(8,128)(2,1)S(1)} custom-call(s32[8]{0:T(128)S(1)} %copy-done, f32[8]{0:T(128)S(1)} %select_reduce_fusion.3.factor_ref, bf16[2048,384]{1,0:T(8,128)(2,1)} %bitcast.58, bf16[2048,384]{1,0:T(8,128)(2,1)} %get-tuple-element.34.low_hbm, bf16[2048,384]{1,0:T(8,128)(2,1)} %get-tuple-element.27.mid_grad_hbm, ...), custom_call_target="tpu_custom_call" | custom-call | bytes 16777216 | tf_op jit(solution)/shard_map/weight_grads/pallas_call | solution.py:493
  72.4 0.1 dynamic-slice_bitcast_fusion
  72.5 1.7 %collective-permute-start.5 = (bf16[16,56,384]{2,1,0:T(8,128)(2,1)S(1)}, bf16[16,56,384]{2,1,0:T(8,128)(2,1)S(1)}, u32[]{:S(2)}, u32[]{:S(2)}) collective-permute-start(bf16[16,56,384]{2,1,0:T(8,128)(2,1)S(1)} %dynamic-slice_bitcast_fusion), channel_id=1, source_target_pairs={{0,4},{4,0},{1,5},{5,1},{2,6},{6,2},{3,7},{7,3},{8,12},{12,8},{9,1... | collective-permute-start | bytes 2064392 | tf_op jit(solution)/shard_map/ppermute | solution.py:31
  74.2 0.7 convert_reduce_fusion
  75.6 0.1 select_reduce_fusion.1
  75.7 0.3 collective-permute-done.5
  76.0 0.1 convert_add_fusion
  76.1 0.1 bitcast_select_fusion
  76.2 0.1 fusion.2
  76.3 1.5 %collective-permute-start.6 = (bf16[4,56,384]{2,1,0:T(8,128)(2,1)S(1)}, bf16[4,56,384]{2,1,0:T(8,128)(2,1)S(1)}, u32[]{:S(2)}, u32[]{:S(2)}) collective-permute-start(bf16[4,56,384]{2,1,0:T(8,128)(2,1)S(1)} %get-tuple-element.54), channel_id=1, source_target_pairs={{0,32},{4,12},{8,40},{12,20},{16,48},{20,28},{24,56},{28,4},{32,64... | collective-permute-start | bytes 516104 | tf_op jit(solution)/shard_map/ppermute | solution.py:62
  77.8 2.4 %collective-permute-start.7 = (bf16[4,56,384]{2,1,0:T(8,128)(2,1)S(1)}, bf16[4,56,384]{2,1,0:T(8,128)(2,1)S(1)}, u32[]{:S(2)}, u32[]{:S(2)}) collective-permute-start(bf16[4,56,384]{2,1,0:T(8,128)(2,1)S(1)} %get-tuple-element.56), channel_id=1, source_target_pairs={{0,64},{4,20},{8,72},{12,28},{16,80},{20,4},{24,88},{28,12},{32,96... | collective-permute-start | bytes 516104 | tf_op jit(solution)/shard_map/ppermute | solution.py:62
  80.2 1.2 collective-permute-start.8
  81.4 0.2 select_reduce_fusion.2.source_ref
  81.6 47.0 %collective-permute-done.6 = bf16[4,56,384]{2,1,0:T(8,128)(2,1)S(1)} collective-permute-done((bf16[4,56,384]{2,1,0:T(8,128)(2,1)S(1)}, bf16[4,56,384]{2,1,0:T(8,128)(2,1)S(1)}, u32[]{:S(2)}, u32[]{:S(2)}) %collective-permute-start.6) | collective-permute-done | bytes 172064 | tf_op jit(solution)/shard_map/ppermute | solution.py:62
  128.6 6.1 %collective-permute-done.7 = bf16[4,56,384]{2,1,0:T(8,128)(2,1)S(1)} collective-permute-done((bf16[4,56,384]{2,1,0:T(8,128)(2,1)S(1)}, bf16[4,56,384]{2,1,0:T(8,128)(2,1)S(1)}, u32[]{:S(2)}, u32[]{:S(2)}) %collective-permute-start.7) | collective-permute-done | bytes 172064 | tf_op jit(solution)/shard_map/ppermute | solution.py:62
  134.7 0.0 collective-permute-done.8
  134.7 0.1 fusion.1
  134.9 2.4 %collective-permute-start.10 = (bf16[56,384]{1,0:T(8,128)(2,1)S(1)}, bf16[56,384]{1,0:T(8,128)(2,1)S(1)}, u32[]{:S(2)}, u32[]{:S(2)}) collective-permute-start(bf16[56,384]{1,0:T(8,128)(2,1)S(1)} %get-tuple-element.58), channel_id=1, source_target_pairs={{0,16},{4,68},{8,24},{12,76},{16,0},{20,84},{24,8},{28,92},{32,48}... | collective-permute-start | bytes 129032 | tf_op jit(solution)/shard_map/ppermute | solution.py:62
  137.3 1.8 %collective-permute-start.11 = (bf16[56,384]{1,0:T(8,128)(2,1)S(1)}, bf16[56,384]{1,0:T(8,128)(2,1)S(1)}, u32[]{:S(2)}, u32[]{:S(2)}) collective-permute-start(bf16[56,384]{1,0:T(8,128)(2,1)S(1)} %get-tuple-element.57), channel_id=1, source_target_pairs={{0,24},{4,100},{8,0},{12,108},{16,8},{20,116},{24,16},{28,124},{32... | collective-permute-start | bytes 129032 | tf_op jit(solution)/shard_map/ppermute | solution.py:62
  139.0 0.0 collective-permute-start.9
  139.0 0.0 all-to-all-done.2.received_ref
  139.0 6.3 %place.1 = bf16[4096,384]{1,0:T(8,128)(2,1)} custom-call(s32[16]{0:T(128)S(1)} %select_reduce_fusion.2.source_ref, s32[1]{0:T(128)} %bitcast.20.count_ref, f32[1]{0:T(128)} %bitcast.22.factor_ref, bf16[32,256,384]{2,1,0:T(8,128)(2,1)} %all-to-all-done.2.received_ref), custom_call_target="tpu_custom_call" | custom-call | bytes 25165824 | tf_op jit(solution)/shard_map/place/pallas_call | solution.py:527
  145.3 0.0 collective-permute-done.10.second_ref
  145.3 0.0 collective-permute-done.11.third_ref
  145.3 0.0 collective-permute-done.9.first_ref
  145.3 0.7 finish.1
  (14 shorter events, 0.1 us)
Async XLA Ops:
  0.6 25.2 %copy-start = (s32[8]{0:T(128)S(1)}, s32[8]{0:T(128)}, u32[]{:S(2)}) copy-start(s32[8]{0:T(128)} %valid_ref.5) | copy-start | bytes 100
  0.6 25.2 %copy-start.1 = (s32[8]{0:T(128)S(1)}, s32[8]{0:T(128)}, u32[]{:S(2)}) copy-start(s32[8]{0:T(128)} %owner_ref.3) | copy-start | bytes 100
  21.2 4.7 %copy-start.2 = (bf16[16,56,384]{2,1,0:T(8,128)(2,1)}, bf16[16,56,384]{2,1,0:T(8,128)(2,1)S(1)}, u32[]{:S(2)}) copy-start(bf16[16,56,384]{2,1,0:T(8,128)(2,1)S(1)} %all_to_all.15.own_hbm) | copy-start | bytes 2064388
  21.2 3.8 %collective-permute-start = (bf16[16,56,384]{2,1,0:T(8,128)(2,1)S(1)}, bf16[16,56,384]{2,1,0:T(8,128)(2,1)S(1)}, u32[]{:S(2)}, u32[]{:S(2)}) collective-permute-start(bf16[16,56,384]{2,1,0:T(8,128)(2,1)S(1)} %all_to_all.15.own_hbm), channel_id=1, source_target_pairs={{0,4},{4,0},{1,5},{5,1},{2,6},{6,2},{3,7},{7,3},{8,12},{12,8},{9,1... | collective-permute-start | bytes 2064392 | tf_op jit(solution)/shard_map/ppermute | solution.py:31
  25.0 0.9 copy-start.3
  36.5 11.0 %all-to-all-start.1 = ((f32[16,1,128]{2,1,0:T(1,128)}), f32[16,1,128]{2,1,0:T(1,128)S(1)}, u32[]{:S(2)}, u32[]{:S(2)}) async-start(f32[16,1,128]{2,1,0:T(1,128)} %get-tuple-element.31), calls=%async_computation.1 | async-start | bytes 16384 | tf_op jit(solution)/shard_map/all_to_all | solution.py:458
  47.6 91.4 %all-to-all-start.2 = ((bf16[32,256,384]{2,1,0:T(8,128)(2,1)}), bf16[32,256,384]{2,1,0:T(8,128)(2,1)}, u32[]{:S(2)}, u32[]{:S(2)}) async-start(bf16[32,256,384]{2,1,0:T(8,128)(2,1)} %get-tuple-element.37), calls=%async_computation.2 | async-start | bytes 12582912 | tf_op jit(solution)/shard_map/all_to_all | solution.py:480
  55.2 1.2 collective-permute-start.1
  56.4 5.7 %collective-permute-start.2 = (f32[1,32]{1,0:T(1,128)S(1)}, f32[1,32]{1,0:T(1,128)S(1)}, u32[]{:S(2)}, u32[]{:S(2)}) collective-permute-start(f32[1,32]{1,0:T(1,128)S(1)} %bitcast_add_fusion.1), channel_id=1, source_target_pairs={{0,1},{1,2},{2,3},{3,0},{4,5},{5,6},{6,7},{7,4},{8,9},{9,10},{10,1... | collective-permute-start | bytes 392 | tf_op jit(solution)/shard_map/ppermute | solution.py:36
  58.0 4.7 %collective-permute-start.3 = (f32[1,32]{1,0:T(1,128)S(1)}, f32[1,32]{1,0:T(1,128)S(1)}, u32[]{:S(2)}, u32[]{:S(2)}) collective-permute-start(f32[1,32]{1,0:T(1,128)S(1)} %bitcast_add_fusion.1), channel_id=1, source_target_pairs={{0,2},{1,3},{2,0},{3,1},{4,6},{5,7},{6,4},{7,5},{8,10},{9,11},{10,... | collective-permute-start | bytes 392 | tf_op jit(solution)/shard_map/ppermute | solution.py:36
  61.3 2.8 %collective-permute-start.4 = (f32[1,32]{1,0:T(1,128)S(1)}, f32[1,32]{1,0:T(1,128)S(1)}, u32[]{:S(2)}, u32[]{:S(2)}) collective-permute-start(f32[1,32]{1,0:T(1,128)S(1)} %bitcast_add_fusion.1), channel_id=1, source_target_pairs={{0,3},{1,0},{2,1},{3,2},{4,7},{5,4},{6,5},{7,6},{8,11},{9,8},{10,9... | collective-permute-start | bytes 392 | tf_op jit(solution)/shard_map/ppermute | solution.py:36
  72.5 3.5 %collective-permute-start.5 = (bf16[16,56,384]{2,1,0:T(8,128)(2,1)S(1)}, bf16[16,56,384]{2,1,0:T(8,128)(2,1)S(1)}, u32[]{:S(2)}, u32[]{:S(2)}) collective-permute-start(bf16[16,56,384]{2,1,0:T(8,128)(2,1)S(1)} %dynamic-slice_bitcast_fusion), channel_id=1, source_target_pairs={{0,4},{4,0},{1,5},{5,1},{2,6},{6,2},{3,7},{7,3},{8,12},{12,8},{9,1... | collective-permute-start | bytes 2064392 | tf_op jit(solution)/shard_map/ppermute | solution.py:31
  76.3 52.3 %collective-permute-start.6 = (bf16[4,56,384]{2,1,0:T(8,128)(2,1)S(1)}, bf16[4,56,384]{2,1,0:T(8,128)(2,1)S(1)}, u32[]{:S(2)}, u32[]{:S(2)}) collective-permute-start(bf16[4,56,384]{2,1,0:T(8,128)(2,1)S(1)} %get-tuple-element.54), channel_id=1, source_target_pairs={{0,32},{4,12},{8,40},{12,20},{16,48},{20,28},{24,56},{28,4},{32,64... | collective-permute-start | bytes 516104 | tf_op jit(solution)/shard_map/ppermute | solution.py:62
  77.8 56.9 %collective-permute-start.7 = (bf16[4,56,384]{2,1,0:T(8,128)(2,1)S(1)}, bf16[4,56,384]{2,1,0:T(8,128)(2,1)S(1)}, u32[]{:S(2)}, u32[]{:S(2)}) collective-permute-start(bf16[4,56,384]{2,1,0:T(8,128)(2,1)S(1)} %get-tuple-element.56), channel_id=1, source_target_pairs={{0,64},{4,20},{8,72},{12,28},{16,80},{20,4},{24,88},{28,12},{32,96... | collective-permute-start | bytes 516104 | tf_op jit(solution)/shard_map/ppermute | solution.py:62
  80.2 54.5 %collective-permute-start.8 = (bf16[4,56,384]{2,1,0:T(8,128)(2,1)S(1)}, bf16[4,56,384]{2,1,0:T(8,128)(2,1)S(1)}, u32[]{:S(2)}, u32[]{:S(2)}) collective-permute-start(bf16[4,56,384]{2,1,0:T(8,128)(2,1)S(1)} %get-tuple-element.55), channel_id=1, source_target_pairs={{0,96},{4,28},{8,104},{12,4},{16,112},{20,12},{24,120},{28,20},{32... | collective-permute-start | bytes 516104 | tf_op jit(solution)/shard_map/ppermute | solution.py:62
  134.9 10.5 %collective-permute-start.10 = (bf16[56,384]{1,0:T(8,128)(2,1)S(1)}, bf16[56,384]{1,0:T(8,128)(2,1)S(1)}, u32[]{:S(2)}, u32[]{:S(2)}) collective-permute-start(bf16[56,384]{1,0:T(8,128)(2,1)S(1)} %get-tuple-element.58), channel_id=1, source_target_pairs={{0,16},{4,68},{8,24},{12,76},{16,0},{20,84},{24,8},{28,92},{32,48}... | collective-permute-start | bytes 129032 | tf_op jit(solution)/shard_map/ppermute | solution.py:62
  137.3 8.1 %collective-permute-start.11 = (bf16[56,384]{1,0:T(8,128)(2,1)S(1)}, bf16[56,384]{1,0:T(8,128)(2,1)S(1)}, u32[]{:S(2)}, u32[]{:S(2)}) collective-permute-start(bf16[56,384]{1,0:T(8,128)(2,1)S(1)} %get-tuple-element.57), channel_id=1, source_target_pairs={{0,24},{4,100},{8,0},{12,108},{16,8},{20,116},{24,16},{28,124},{32... | collective-permute-start | bytes 129032 | tf_op jit(solution)/shard_map/ppermute | solution.py:62
  139.0 6.3 %collective-permute-start.9 = (bf16[56,384]{1,0:T(8,128)(2,1)S(1)}, bf16[56,384]{1,0:T(8,128)(2,1)S(1)}, u32[]{:S(2)}, u32[]{:S(2)}) collective-permute-start(bf16[56,384]{1,0:T(8,128)(2,1)S(1)} %get-tuple-element.59), channel_id=1, source_target_pairs={{0,8},{4,36},{8,16},{12,44},{16,24},{20,52},{24,0},{28,60},{32,40}... | collective-permute-start | bytes 129032 | tf_op jit(solution)/shard_map/ppermute | solution.py:62
